TPU v7x, 512 devices: a whole 4x8x8 slice. The times are simulated.
512 devices in a mesh: gx: 64 (over x, z, core), gy: 8 (over y).
Axes of the slice: x: 4, y: 8, z: 8, core: 2. Of those that a mesh axis runs over, the one named last changes fastest.
Arguments:
- right_side: float32 [64, 16, 8, 8, 128], P('gx', 'gy'), may hold values from -6 to 6
- inverse_blocks: float32 [64, 16, 8, 128, 128], P('gx', 'gy'), may hold values from -1.7 to 1.7
- couple_x: float32 [64, 16, 8, 8, 128], P('gx', 'gy'), may hold values from -0.127 to -0.105
- couple_y: float32 [64, 16, 8, 8, 128], P('gx', 'gy'), may hold values from -0.007 to -0.003
- couple_z: float32 [64, 16, 8, 8, 8], P('gx', 'gy'), may hold values from -0.75 to 0.75
Outputs:
- solution: float32 [64, 16, 8, 8, 128], P('gx', 'gy')
All inputs are finite; a program needn't handle non-finite values.
Results may differ from a plain program's by a relative error of at most 0.0001.
Values sent between devices are 32-bit elements; how exact they have to be, the bound alone decides.
No kernel may reach another device: no remote copies, remote signals or barrier semaphores. Data moves between devices by JAX's collectives and lax.ppermute only.
A program may use at most 64 MiB of HBM per device.

v0:
```python
import jax
import jax.numpy as jnp
from jax import lax
from jax.sharding import PartitionSpec as P

exact_mode = lax.Precision.HIGHEST


def from_behind(block, axis, distance):
    devices = range(lax.axis_size(axis))
    route = [(i - distance, i) for i in devices if i - distance in devices]
    return lax.ppermute(block, axis, route)


def couple(matrix, values_in):
    return jnp.einsum("cdz,ndz->ncz", matrix, values_in, precision=exact_mode)


def solve_group(rhs_group, inverse_group, along_x, along_y, corners, x_in, y_in, z_prior):
    width_x, width_y, vectors, components, section_cells = rhs_group.shape
    groups = inverse_group.shape[2]
    seg_len = section_cells // groups
    done_line = []
    for y_cell in range(width_y):
        x_prior = x_in[y_cell]
        y_prior = y_in[0] if y_cell == 0 else done_line[y_cell - 1]
        partial_value = rhs_group[0, y_cell] - couple(along_x[0, y_cell], x_prior)
        partial_value = partial_value - couple(along_y[0, y_cell], y_prior)
        below = z_prior[0, y_cell]
        seg_piece = partial_value[:, :, 0:seg_len]
        head_row = seg_piece[:, :, 0] - jnp.einsum(
            "cd,nd->nc", corners[0, y_cell, 0], below, precision=exact_mode
        )
        seg_piece = jnp.concatenate([head_row[:, :, None], seg_piece[:, :, 1:]], axis=2)
        flattened = seg_piece.reshape(vectors, components * seg_len)
        solved = lax.dot_general(
            flattened,
            inverse_group[0, y_cell, 0],
            (((1,), (1,)), ((), ())),
            precision=exact_mode,
            preferred_element_type=jnp.float32,
        )
        solved = solved.reshape(vectors, components, seg_len)
        below = solved[:, :, -1]
        pieces = [solved]
        done_line.append(jnp.concatenate(pieces, axis=2))
    done_rows = [done_line]
    return jnp.stack([jnp.stack(done_line) for done_line in done_rows])


def local(right_side, inverse_blocks, couple_x, couple_y, couple_z):
    width_x, width_y, vectors, components, z_cells = right_side.shape
    segments = inverse_blocks.shape[2]
    seg_len = z_cells // segments
    per_section = 1
    sections = segments // per_section
    section_cells = per_section * seg_len
    x_size = lax.axis_size("gx")
    y_size = lax.axis_size("gy")
    offset = lax.axis_index("gx") + lax.axis_index("gy")
    total_steps = x_size + y_size - 2 + sections

    def advance(step_index, state_now):
        solution, x_in, y_in = state_now
        section_now = step_index - offset
        active = (section_now >= 0) & (section_now < sections)
        chosen = jnp.clip(section_now, 0, sections - 1)

        def compute(current):
            start_cell = chosen * section_cells
            rhs_group = lax.dynamic_slice_in_dim(right_side, start_cell, section_cells, 4)
            along_x = lax.dynamic_slice_in_dim(couple_x, start_cell, section_cells, 4)
            along_y = lax.dynamic_slice_in_dim(couple_y, start_cell, section_cells, 4)
            inverse_group = lax.dynamic_slice_in_dim(
                inverse_blocks, chosen * per_section, per_section, 2
            )
            corners = lax.dynamic_slice_in_dim(couple_z, chosen * per_section, per_section, 2)
            edge_cell = jnp.maximum(start_cell - 1, 0)
            z_prior = lax.dynamic_index_in_dim(current, edge_cell, 4, keepdims=False) * (
                chosen > 0
            ).astype(jnp.float32)
            new_block = solve_group(
                rhs_group, inverse_group, along_x, along_y, corners, x_in, y_in, z_prior
            )
            return (lax.dynamic_update_slice_in_dim(current, new_block, start_cell, 4), new_block)

        def skip_section(current):
            return (
                current,
                jnp.zeros((width_x, width_y, vectors, components, section_cells), jnp.float32),
            )

        solution, new_block = lax.cond(active, compute, skip_section, solution)
        x_next = from_behind(new_block[width_x - 1], "gx", 1)
        y_next = from_behind(new_block[:, width_y - 1], "gy", 1)
        return (solution, x_next, y_next)

    initial = (
        jnp.zeros(right_side.shape, jnp.float32),
        jnp.zeros((width_y, vectors, components, section_cells), jnp.float32),
        jnp.zeros((width_x, vectors, components, section_cells), jnp.float32),
    )
    solution, _, _ = lax.fori_loop(0, total_steps, advance, initial)
    return solution


def solution(mesh):
    return jax.shard_map(
        local,
        mesh=mesh,
        in_specs=(
            P("gx", "gy", None, None, None),
            P("gx", "gy", None, None, None),
            P("gx", "gy", None, None, None),
            P("gx", "gy", None, None, None),
            P("gx", "gy", None, None, None),
        ),
        out_specs=P("gx", "gy", None, None, None),
        check_vma=False,
    )
```

profile of v0, /device:TPU:510, one launch (start us, length us, event | category | flops | bytes accessed | tf_op | source)
XLA Modules:
  0.0 1141.9 jit_solution(5175211108158630344)
XLA Ops:
  3.5 1137.4 %while.20 = (s32[]{:T(128)}, f32[1,2,8,8,128]{3,2,1,4,0:T(8,128)S(1)}, f32[2,8,8,16]{3,1,2,0:T(8,128)S(1)}, f32[1,8,8,16]{3,1,2,0:T(8,128)S(1)}, s32[]{:T(128)},...) while((s32[]{:T(128)}, ...), condition=%wide.region_3.4_spmd, body=%wide.region_0.3_spmd.sunk | while | flops 3559698 | bytes 1342451 | solution.py:103
  54.2 5.7 collective-permute-done.1
  64.5 5.7 collective-permute-done.1
  74.8 5.7 collective-permute-done.1
  85.2 5.7 collective-permute-done.1
  95.5 5.7 collective-permute-done.1
  105.8 5.7 collective-permute-done.1
  116.1 5.7 collective-permute-done.1
  126.5 5.7 collective-permute-done.1
  136.8 5.7 collective-permute-done.1
  147.1 5.7 collective-permute-done.1
  157.5 5.7 collective-permute-done.1
  167.8 5.7 collective-permute-done.1
  178.1 5.7 collective-permute-done.1
  188.4 5.7 collective-permute-done.1
  198.8 5.7 collective-permute-done.1
  209.1 5.7 collective-permute-done.1
  219.4 5.7 collective-permute-done.1
  229.8 5.7 collective-permute-done.1
  240.1 5.7 collective-permute-done.1
  250.4 5.7 collective-permute-done.1
  260.7 5.7 collective-permute-done.1
  271.1 5.7 collective-permute-done.1
  281.4 5.7 collective-permute-done.1
  291.7 5.7 collective-permute-done.1
  302.0 5.7 collective-permute-done.1
  312.4 5.7 collective-permute-done.1
  322.7 5.7 collective-permute-done.1
  333.0 5.7 collective-permute-done.1
  343.4 5.7 collective-permute-done.1
  353.7 5.7 collective-permute-done.1
  364.0 5.7 collective-permute-done.1
  374.3 5.7 collective-permute-done.1
  384.7 5.7 collective-permute-done.1
  395.0 5.7 collective-permute-done.1
  405.3 5.7 collective-permute-done.1
  415.7 5.7 collective-permute-done.1
  426.0 5.7 collective-permute-done.1
  436.3 5.7 collective-permute-done.1
  446.6 5.7 collective-permute-done.1
  457.0 5.7 collective-permute-done.1
  467.3 5.7 collective-permute-done.1
  477.6 5.7 collective-permute-done.1
  487.9 5.7 collective-permute-done.1
  508.6 5.7 collective-permute-done.1
  549.9 5.7 collective-permute-done.1
  663.5 5.7 collective-permute-done.1
  704.8 269.1 %collective-permute-done.1 = f32[1,8,8,16]{3,1,2,0:T(8,128)S(1)} collective-permute-done((f32[1,8,8,16]{3,1,2,0:T(8,128)S(1)}, f32[1,8,8,16]{3,1,2,0:T(8,128)S(1)}, u32[]{:S(2)}, u32[]{:S(2)}) %collective-permute-start.1) | collective-permute-done | bytes 4128 | tf_op jit(solution)/shard_map/while/body/eval_jaxpr/ppermute | solution.py:12
  973.9 9.7 conditional.2
  987.6 5.7 collective-permute-done.1
  993.3 9.7 conditional.2
  1007.0 5.7 collective-permute-done.1
  1012.7 9.7 conditional.2
  1026.4 5.7 collective-permute-done.1
  1032.1 9.7 conditional.2
  1045.8 5.7 collective-permute-done.1
  1051.5 9.7 conditional.2
  1065.2 5.7 collective-permute-done.1
  1070.9 9.7 conditional.2
  1084.6 5.7 collective-permute-done.1
  1090.3 9.7 conditional.2
  1103.9 5.7 collective-permute-done.1
  1109.7 9.7 conditional.2
  1128.5 5.8 collective-permute-start
  (750 shorter events, 605.8 us)
Async XLA Ops:
  50.2 9.7 collective-permute-start
  60.5 9.7 collective-permute-start
  70.9 9.7 collective-permute-start
  81.2 9.7 collective-permute-start
  91.5 9.7 collective-permute-start
  101.8 9.7 collective-permute-start
  112.2 9.7 collective-permute-start
  122.5 9.7 collective-permute-start
  132.8 9.7 collective-permute-start
  143.2 9.7 collective-permute-start
  153.5 9.7 collective-permute-start
  163.8 9.7 collective-permute-start
  174.1 9.7 collective-permute-start
  184.5 9.7 collective-permute-start
  194.8 9.7 collective-permute-start
  205.1 9.7 collective-permute-start
  215.5 9.7 collective-permute-start
  225.8 9.7 collective-permute-start
  236.1 9.7 collective-permute-start
  246.4 9.7 collective-permute-start
  256.8 9.7 collective-permute-start
  267.1 9.7 collective-permute-start
  277.4 9.7 collective-permute-start
  287.7 9.7 collective-permute-start
  298.1 9.7 collective-permute-start
  308.4 9.7 collective-permute-start
  318.7 9.7 collective-permute-start
  329.1 9.7 collective-permute-start
  339.4 9.7 collective-permute-start
  349.7 9.7 collective-permute-start
  360.0 9.7 collective-permute-start
  370.4 9.7 collective-permute-start
  380.7 9.7 collective-permute-start
  391.0 9.7 collective-permute-start
  401.4 9.7 collective-permute-start
  411.7 9.7 collective-permute-start
  422.0 9.7 collective-permute-start
  432.3 9.7 collective-permute-start
  442.7 9.7 collective-permute-start
  453.0 9.7 collective-permute-start
  463.3 9.7 collective-permute-start
  473.6 9.7 collective-permute-start
  484.0 9.7 collective-permute-start
  494.3 9.7 collective-permute-start
  504.6 9.7 collective-permute-start
  515.0 9.7 collective-permute-start
  525.3 9.7 collective-permute-start
  535.6 9.7 collective-permute-start
  545.9 9.7 collective-permute-start
  576.9 9.7 collective-permute-start
  618.2 9.7 collective-permute-start
  649.2 9.7 collective-permute-start
  659.5 9.7 collective-permute-start
  690.5 9.7 collective-permute-start
  700.9 273.1 %collective-permute-start = (f32[2,8,8,16]{3,1,2,0:T(8,128)}, f32[2,8,8,16]{3,1,2,0:T(8,128)S(1)}, u32[]{:S(2)}, u32[]{:S(2)}) collective-permute-start(f32[2,8,8,16]{3,1,2,0:T(8,128)} %bitcast.85), channel_id=1, source_target_pairs={{0,8},{8,16},{16,24},{24,32},{32,40},{40,48},{48,56},{56,64},{64,7... | collective-permute-start | bytes 24584 | tf_op jit(solution)/shard_map/while/body/eval_jaxpr/ppermute | solution.py:12
  703.5 270.4 %collective-permute-start.1 = (f32[1,8,8,16]{3,1,2,0:T(8,128)S(1)}, f32[1,8,8,16]{3,1,2,0:T(8,128)S(1)}, u32[]{:S(2)}, u32[]{:S(2)}) collective-permute-start(f32[1,8,8,16]{3,1,2,0:T(8,128)S(1)} %slice_bitcast_fusion.10), channel_id=1, source_target_pairs={{0,1},{1,2},{2,3},{3,4},{4,5},{5,6},{6,7},{8,9},{9,10},{10,11},{11... | collective-permute-start | bytes 12296 | tf_op jit(solution)/shard_map/while/body/eval_jaxpr/ppermute | solution.py:12
  983.6 9.7 collective-permute-start
  1003.0 9.7 collective-permute-start
  1022.4 9.7 collective-permute-start
  1041.8 9.7 collective-permute-start
  1061.2 9.7 collective-permute-start
  1080.6 9.7 collective-permute-start
  1100.0 9.7 collective-permute-start
  1128.5 12.4 %collective-permute-start = (f32[2,8,8,16]{3,1,2,0:T(8,128)}, f32[2,8,8,16]{3,1,2,0:T(8,128)S(1)}, u32[]{:S(2)}, u32[]{:S(2)}) collective-permute-start(f32[2,8,8,16]{3,1,2,0:T(8,128)} %bitcast.85), channel_id=1, source_target_pairs={{0,8},{8,16},{16,24},{24,32},{32,40},{40,48},{48,56},{56,64},{64,7... | collective-permute-start | bytes 24584 | tf_op jit(solution)/shard_map/while/body/eval_jaxpr/ppermute | solution.py:12
  (94 other events, 672.1 us)
where the time goes:
time: 1150 us; the launch traced here: 1140 us
  waiting for transfers between devices  701 us (61%)
  starting transfers between devices  253 us (22%)
  local copies, waits for them, and re-layouts  132 us (11%)
  matrix products  47.2 us (4%)
    ppermute x156, waiting for transfers between devices, from_behind(): return lax.ppermute(block, axis, route)  701 us
    ppermute x156, starting transfers between devices, from_behind(): return lax.ppermute(block, axis, route)  253 us
    squeeze x78, local copies, waits for them, and re-layouts, advance(): y_next = from_behind(new_block[:, width_y - 1], 'gy', 1)  59.6 us
    another operation x94, local copies, waits for them, and re-layouts  46.8 us
  transfers between devices with their start and end apart: 156, of which 78 were waited for; matrix products, arithmetic and copies ran while one was open for 5% of the time, Pallas kernels for 0%

commit v1 on v0

v1 whole, which is shorter than its diff:
```python
import jax
import jax.numpy as jnp
from jax import lax
from jax.experimental import pallas as pl
from jax.experimental.pallas import tpu as pltpu
from jax.sharding import PartitionSpec as P

AXES = ("gx", "gy")
ROUNDS = 8
REPEAT = 9
VMEM = pl.BlockSpec(memory_space=pltpu.VMEM)
ANY = pl.BlockSpec(memory_space=pl.ANY)


def swap_groups(a):
    row = lax.broadcasted_iota(jnp.int32, a.shape, 0)
    group = lax.broadcasted_iota(jnp.int32, a.shape, 1) // 16
    ahead = (group - row) & 7
    out = a
    for d in range(1, 8):
        moved = pltpu.roll(pltpu.roll(a, 8 - d, 0), 16 * d, 1)
        out = jnp.where(ahead == d, moved, out)
    return out


def pack_kernel(rhs, inverse, cx, cy, cz, *rest):
    outs, small = rest[:4], rest[4]
    chip = lax.rem(lax.axis_index("gx"), ROUNDS) // 2
    row = lax.broadcasted_iota(jnp.int32, (8, 128), 0)
    group = lax.broadcasted_iota(jnp.int32, (8, 128), 1) // 16
    spread_row = lax.broadcasted_iota(jnp.int32, (8, 128), 0)
    spread_lane = lax.broadcasted_iota(jnp.int32, (8, 128), 1)
    spread = jnp.where(spread_lane == 16 * spread_row, 1.0, 0.0)
    heads = jnp.dot(
        cz[...], spread, precision=lax.Precision.HIGHEST, preferred_element_type=jnp.float32
    )
    for y in range(2):
        for n in range(8):
            small[y, :, n, :] = swap_groups(rhs[y, n])
        for ref, base in ((cx, 8), (cy, 16)):
            for m in range(8):
                a = ref[y, m]
                for c in range(8):
                    if c != m:
                        a = jnp.where(row == (c - m) % 8, ref[y, c], a)
                small[y, :, base + m, :] = swap_groups(a)
        for s in range(8):
            t = heads[(y * 8 + s) * 8 : (y * 8 + s + 1) * 8]
            out = t
            for d in range(1, 8):
                out = jnp.where(group == d, pltpu.roll(t, 8 - d, 0), out)
            small[y, s, 24:32, :] = out
    for q in range(4):
        first = 2 * (chip ^ q)
        for y in range(2):
            for k in range(2):
                outs[q][y * 2 + k, 0:128, :] = inverse[y, first + k].T
                outs[q][y * 2 + k, 128:160, :] = small[y, first + k]


def prepare_kernel(*refs):
    parts, weights, rows = refs[:ROUNDS], refs[ROUNDS], refs[ROUNDS + 1]
    place = lax.rem(lax.axis_index("gx"), ROUNDS)
    for r in range(ROUNDS):
        x = place ^ r
        for b in range(4):
            full = parts[r][b, 0:128, :]
            high = full.astype(jnp.bfloat16)
            low = (full - high.astype(jnp.float32)).astype(jnp.bfloat16)
            weights[x, b, :, 0:128] = high
            weights[x, b, :, 128:256] = low
            rows[x, b] = parts[r][b, 128:160, :]


def step_kernel(step, weights, rows, in_x, in_y, in_z, _, tile, out_x, out_y, out_z):
    gx, gy = lax.axis_index("gx"), lax.axis_index("gy")
    level = gx // ROUNDS + gy + lax.rem(gx, ROUNDS) // 2
    last_lane = lax.rem(lax.broadcasted_iota(jnp.int32, (8, 128), 1), 16) == 15

    @pl.when((level == step) & (lax.rem(gx, 2) == 0))
    def _():
        z_packed = in_z[...]

        def advance(i, carry):
            done, z_out = carry[:4], carry[4]
            new = []
            for y in range(2):
                for k in range(2):
                    b = y * 2 + k
                    x = i - y - k
                    inside = (x >= 0) & (x < ROUNDS)
                    xc = jnp.clip(x, 0, ROUNDS - 1)
                    from_x = done[b]
                    from_y = in_y[xc, k] if y == 0 else done[k]
                    if k == 0:
                        from_z = pltpu.roll(z_packed, lax.rem(128 - (xc * 2 + y), 128), 1)
                    else:
                        from_z = pltpu.roll(done[y * 2], 113, 1)
                    terms = []
                    for m in range(8):
                        q = (
                            rows[xc, b, 8 + m : 9 + m, :] * from_x
                            + rows[xc, b, 16 + m : 17 + m, :] * from_y
                            + rows[xc, b, 24 + m : 25 + m, :] * from_z
                        )
                        terms.append(pltpu.roll(q, 16 * m, 1) if m else q)
                    while len(terms) > 1:
                        terms = [u + v for u, v in zip(terms[::2], terms[1::2])]
                    partial = rows[xc, b, 0:8, :] - terms[0]
                    high = partial.astype(jnp.bfloat16).astype(jnp.float32)
                    both = jnp.concatenate([high, partial - high], axis=0).astype(jnp.bfloat16)
                    product = jnp.dot(
                        both, weights[xc, b], preferred_element_type=jnp.float32
                    )
                    solved = (product[0:8, 0:128] + product[8:16, 0:128]) + (
                        product[0:8, 128:256] + product[8:16, 128:256]
                    )
                    solved = jnp.where(inside, solved, done[b])
                    tile[xc, b] = solved
                    if y == 1:
                        out_y[xc, k] = solved
                    if k == 1:
                        kept = jnp.where(last_lane & inside, solved, 0.0)
                        z_out = z_out + pltpu.roll(kept, lax.rem(xc * 2 + y + 113, 128), 1)
                    new.append(solved)
            return (*new, z_out)

        carry = tuple(in_x[b] for b in range(4)) + (jnp.zeros((8, 128), jnp.float32),)
        carry = lax.fori_loop(0, ROUNDS + 2, advance, carry)
        for b in range(4):
            out_x[b] = carry[b]
        out_z[...] = carry[4]


def unpack_kernel(parts, out):
    for y in range(2):
        for n in range(8):
            rows = jnp.concatenate(
                [parts[2 * (s // 2), y * 2 + s % 2, n : n + 1, :] for s in range(8)], axis=0
            )
            out[y, n] = swap_groups(rows)


def f32(*shape):
    return jax.ShapeDtypeStruct(shape, jnp.float32)


def tile_level(gx, gy):
    return gx // ROUNDS + gy + gx % ROUNDS // 2


def local(right_side, inverse_blocks, couple_x, couple_y, couple_z):
    nx, ny = lax.axis_size("gx"), lax.axis_size("gy")
    outs = pl.pallas_call(
        pack_kernel,
        out_shape=[f32(4, 160, 128)] * 4,
        in_specs=[VMEM] * 5,
        out_specs=[VMEM] * 4,
        scratch_shapes=[pltpu.VMEM((2, 8, 32, 128), jnp.float32)],
        compiler_params=pltpu.CompilerParams(vmem_limit_bytes=12 << 20),
        name="pack",
    )(
        right_side[0],
        inverse_blocks[0],
        couple_x[0],
        couple_y[0],
        couple_z.reshape(128, 8),
    )

    def device(gx, gy):
        return gx * ny + gy

    parts = [outs[0]]
    for r in range(1, ROUNDS):
        pairs = [
            (device(gx, gy), device(gx ^ r, gy))
            for gx in range(nx)
            for gy in range(ny)
            if (gx ^ r) % 2 == 0
        ]
        parts.append(lax.ppermute(outs[r // 2], AXES, pairs))
    weights, rows = pl.pallas_call(
        prepare_kernel,
        out_shape=[
            jax.ShapeDtypeStruct((ROUNDS, 4, 128, 256), jnp.bfloat16),
            f32(ROUNDS, 4, 32, 128),
        ],
        in_specs=[VMEM] * ROUNDS,
        out_specs=[VMEM] * 2,
        compiler_params=pltpu.CompilerParams(vmem_limit_bytes=16 << 20),
        name="prepare",
    )(*parts)

    steps = nx // ROUNDS + ny + 4 - 2
    tile = jnp.zeros((ROUNDS, 4, 8, 128), jnp.float32)
    in_x = jnp.zeros((4, 8, 128), jnp.float32)
    in_y = jnp.zeros((ROUNDS, 2, 8, 128), jnp.float32)
    in_z = jnp.zeros((8, 128), jnp.float32)
    for step in range(steps):
        def body(*refs, step=step):
            step_kernel(step, *refs)

        tile, out_x, out_y, out_z = pl.pallas_call(
            body,
            out_shape=[
                f32(ROUNDS, 4, 8, 128),
                f32(4, 8, 128),
                f32(ROUNDS, 2, 8, 128),
                f32(8, 128),
            ],
            in_specs=[VMEM] * 6,
            out_specs=[VMEM] * 4,
            input_output_aliases={5: 0},
            compiler_params=pltpu.CompilerParams(vmem_limit_bytes=12 << 20),
            name=f"tile_step",
        )(weights, rows, in_x, in_y, in_z, tile)
        if step == steps - 1:
            break
        tiles = [
            (gx, gy)
            for gx in range(0, nx, 2)
            for gy in range(ny)
            if tile_level(gx, gy) % REPEAT == step % REPEAT
        ]
        to_x = [(device(gx, gy), device(gx + ROUNDS, gy)) for gx, gy in tiles if gx + ROUNDS < nx]
        to_y = [(device(gx, gy), device(gx, gy + 1)) for gx, gy in tiles if gy + 1 < ny]
        to_z = [(device(gx, gy), device(gx + 2, gy)) for gx, gy in tiles if gx % ROUNDS + 2 < ROUNDS]
        in_x = lax.ppermute(out_x, AXES, to_x)
        in_y = lax.ppermute(out_y, AXES, to_y)
        in_z = lax.ppermute(out_z, AXES, to_z)

    groups = [list(range(g, g + ROUNDS)) for g in range(0, nx, ROUNDS)]
    parts = lax.all_to_all(tile, "gx", 0, 0, axis_index_groups=groups, tiled=True)
    result = pl.pallas_call(
        unpack_kernel,
        out_shape=f32(2, 8, 8, 128),
        in_specs=[VMEM],
        out_specs=VMEM,
        name="unpack",
    )(parts)
    return result[None]


def solution(mesh):
    spec = P("gx", "gy", None, None, None)
    return jax.shard_map(
        local, mesh=mesh, in_specs=(spec,) * 5, out_specs=spec, check_vma=False
    )
```

time: 1150 us -> 219 us (0.19)
  the two profiles are of different devices: /device:TPU:510 before, /device:TPU:318 now
where the time goes in v1:
time: 219 us; the launch traced here: 218 us
  waiting for transfers between devices  120 us (55%)
  starting transfers between devices  52.8 us (24%)
  blocking collectives  32 us (15%)
  Pallas kernels  7.44 us (3%)
  local copies, waits for them, and re-layouts  4.6 us (2%)
    ppermute x17, waiting for transfers between devices, local(): in_x = lax.ppermute(out_x, AXES, to_x)  96.6 us
    all_to_all x1, blocking collectives, local(): lax.all_to_all(tile, 'gx', 0, 0, axis_index_groups=groups, tiled=True)  32 us
    ppermute x7, waiting for transfers between devices, local(): parts.append(lax.ppermute(outs[r // 2], AXES, pairs))  20.2 us
    ppermute x7, starting transfers between devices, local(): parts.append(lax.ppermute(outs[r // 2], AXES, pairs))  15.3 us
    ppermute x17, starting transfers between devices, local(): in_y = lax.ppermute(out_y, AXES, to_y)  12.5 us
    ppermute x17, starting transfers between devices, local(): in_x = lax.ppermute(out_x, AXES, to_x)  12.5 us
    ppermute x17, starting transfers between devices, local(): in_z = lax.ppermute(out_z, AXES, to_z)  12.5 us
    pallas_call x18, Pallas kernels, local(): pl.pallas_call(body, out_shape=[f32(ROUNDS, 4, 8, 128), f32(4, 8, 128), f...  4.65 us
  transfers between devices with their start and end apart: 58, of which 8 were waited for; matrix products, arithmetic and copies ran while one was open for 0% of the time, Pallas kernels for 0%

profile of v1, /device:TPU:318, one launch (start us, length us, event | category | flops | bytes accessed | tf_op | source)
XLA Modules:
  0.0 218.0 jit_solution(15474944714616114918)
XLA Ops:
  0.0 1.2 copy-done
  1.2 0.8 copy-done.1
  2.1 0.8 copy-done.2
  2.9 0.8 copy-done.3
  3.7 0.8 copy-done.4
  4.6 0.7 pack.1
  5.3 1.3 collective-permute-start
  6.6 3.4 %collective-permute-start.1 = (f32[4,160,128]{2,1,0:T(8,128)S(1)}, f32[4,160,128]{2,1,0:T(8,128)S(1)}, u32[]{:S(2)}, u32[]{:S(2)}) collective-permute-start(f32[4,160,128]{2,1,0:T(8,128)S(1)} %get-tuple-element.81), channel_id=1, source_target_pairs={{0,16},{1,17},{2,18},{3,19},{4,20},{5,21},{6,22},{7,23},{16,0},{17... | collective-permute-start | bytes 983048 | tf_op jit(solution)/shard_map/ppermute | solution.py:181
  10.0 1.3 collective-permute-start.2
  11.3 4.3 %collective-permute-start.3 = (f32[4,160,128]{2,1,0:T(8,128)S(1)}, f32[4,160,128]{2,1,0:T(8,128)S(1)}, u32[]{:S(2)}, u32[]{:S(2)}) collective-permute-start(f32[4,160,128]{2,1,0:T(8,128)S(1)} %get-tuple-element.82), channel_id=1, source_target_pairs={{0,32},{1,33},{2,34},{3,35},{4,36},{5,37},{6,38},{7,39},{16,48},{1... | collective-permute-start | bytes 983048 | tf_op jit(solution)/shard_map/ppermute | solution.py:181
  15.6 1.3 collective-permute-start.4
  16.9 2.4 %collective-permute-start.5 = (f32[4,160,128]{2,1,0:T(8,128)S(1)}, f32[4,160,128]{2,1,0:T(8,128)S(1)}, u32[]{:S(2)}, u32[]{:S(2)}) collective-permute-start(f32[4,160,128]{2,1,0:T(8,128)S(1)} %get-tuple-element.83), channel_id=1, source_target_pairs={{0,48},{1,49},{2,50},{3,51},{4,52},{5,53},{6,54},{7,55},{16,32},{1... | collective-permute-start | bytes 983048 | tf_op jit(solution)/shard_map/ppermute | solution.py:181
  19.4 1.3 collective-permute-start.6
  20.9 15.7 %collective-permute-done.3.refs_4_ = f32[4,160,128]{2,1,0:T(8,128)S(1)} collective-permute-done((f32[4,160,128]{2,1,0:T(8,128)S(1)}, f32[4,160,128]{2,1,0:T(8,128)S(1)}, u32[]{:S(2)}, u32[]{:S(2)}) %collective-permute-start.3) | collective-permute-done | bytes 327712 | tf_op jit(solution)/shard_map/ppermute | solution.py:181
  36.6 4.2 %collective-permute-done.4.refs_5_ = f32[4,160,128]{2,1,0:T(8,128)S(1)} collective-permute-done((f32[4,160,128]{2,1,0:T(8,128)S(1)}, f32[4,160,128]{2,1,0:T(8,128)S(1)}, u32[]{:S(2)}, u32[]{:S(2)}) %collective-permute-start.4) | collective-permute-done | bytes 327712 | tf_op jit(solution)/shard_map/ppermute | solution.py:181
  41.3 0.7 collective-permute-start.8
  42.0 0.7 collective-permute-start.7
  42.6 0.7 collective-permute-start.9
  43.4 0.7 collective-permute-start.11
  44.0 0.7 collective-permute-start.10
  44.7 0.7 collective-permute-start.12
  45.5 0.7 collective-permute-start.14
  46.1 0.7 collective-permute-start.13
  46.8 0.7 collective-permute-start.15
  47.5 0.7 collective-permute-start.17
  48.2 0.7 collective-permute-start.16
  48.9 0.7 collective-permute-start.18
  49.6 1.3 collective-permute-start.20
  50.9 1.3 collective-permute-start.19
  52.2 0.7 collective-permute-start.21
  52.9 26.0 %collective-permute-done.19.refs_2_ = f32[4,8,128]{2,1,0:T(8,128)S(1)} collective-permute-done((f32[4,8,128]{2,1,0:T(8,128)S(1)}, f32[4,8,128]{2,1,0:T(8,128)S(1)}, u32[]{:S(2)}, u32[]{:S(2)}) %collective-permute-start.19) | collective-permute-done | bytes 16416 | tf_op jit(solution)/shard_map/ppermute | solution.py:228
  79.6 0.7 collective-permute-start.22
  80.2 1.3 collective-permute-start.24
  81.5 1.3 collective-permute-done.24.refs_4_
  82.9 0.7 collective-permute-start.26
  83.5 0.7 collective-permute-start.25
  84.2 0.7 collective-permute-start.27
  85.0 0.7 collective-permute-start.29
  85.6 0.7 collective-permute-start.28
  86.3 0.7 collective-permute-start.30
  87.0 0.7 collective-permute-start.32
  87.7 0.7 collective-permute-start.31
  89.1 0.7 collective-permute-start.35
  89.8 0.7 collective-permute-start.34
  91.2 0.7 collective-permute-start.38
  91.9 0.7 collective-permute-start.37
  93.3 0.7 collective-permute-start.41
  94.0 0.7 collective-permute-start.40
  95.4 0.7 collective-permute-start.44
  96.0 0.7 collective-permute-start.43
  97.4 1.3 collective-permute-start.47
  98.7 1.3 collective-permute-start.46
  100.7 70.6 %collective-permute-done.46.refs_2_ = f32[4,8,128]{2,1,0:T(8,128)S(1)} collective-permute-done((f32[4,8,128]{2,1,0:T(8,128)S(1)}, f32[4,8,128]{2,1,0:T(8,128)S(1)}, u32[]{:S(2)}, u32[]{:S(2)}) %collective-permute-start.46) | collective-permute-done | bytes 16416 | tf_op jit(solution)/shard_map/ppermute | solution.py:228
  172.0 3.6 %tile_step.32 = (f32[8,4,8,128]{3,2,1,0:T(8,128)S(1)}, f32[4,8,128]{2,1,0:T(8,128)S(1)}, f32[8,2,8,128]{3,2,1,0:T(8,128)S(1)}, f32[8,128]{1,0:T(8,128)S(1)}) custom-call(bf16[8,4,128,256]{3,2,1,0:T(8,128)(2,1)S(1)} %get-tuple-element.84.refs_0_, f32[8,4,32,128]{3,2,1,0:T(8,128)S(1)} %get-tuple-element.85.refs_1_, ...), custom_call_target="tpu_custom_call", output_to_operand_aliasing={{0}: (5, {})} | custom-call | tf_op jit(solution)/shard_map/tile_step/pallas_call | solution.py:203
  175.5 0.7 collective-permute-start.50
  176.2 0.7 collective-permute-start.49
  176.9 1.3 collective-permute-start.51
  178.2 1.3 collective-permute-done.51.refs_4_
  179.5 0.7 collective-permute-start.53
  180.2 0.7 collective-permute-start.52
  181.6 0.7 collective-permute-start.56
  182.3 0.7 collective-permute-start.55
  184.3 32.0 %all_to_all.5.parts = f32[8,4,8,128]{3,2,1,0:T(8,128)} all-to-all(f32[8,4,8,128]{3,2,1,0:T(8,128)S(1)} %get-tuple-element.154), channel_id=1, replica_groups={{0,8,16,24,32,40,48,56},{64,72,80,88,96,104,112,120},{128,136,144,152,1..., dimensions={0} | all-to-all | bytes 262144 | tf_op jit(solution)/shard_map/all_to_all | solution.py:233
  216.3 1.7 unpack.1
  (88 shorter events, 8.4 us)
Async XLA Ops:
  0.0 1.2 copy-start
  1.2 0.8 copy-start.1
  2.1 0.8 copy-start.2
  2.9 0.8 copy-start.3
  3.7 0.8 copy-start.4
  5.3 11.6 %collective-permute-start = (f32[4,160,128]{2,1,0:T(8,128)S(1)}, f32[4,160,128]{2,1,0:T(8,128)S(1)}, u32[]{:S(2)}, u32[]{:S(2)}) collective-permute-start(f32[4,160,128]{2,1,0:T(8,128)S(1)} %get-tuple-element.80.refs_0_), channel_id=1, source_target_pairs={{8,0},{9,1},{10,2},{11,3},{12,4},{13,5},{14,6},{15,7},{24,16},{25,... | collective-permute-start | bytes 983048 | tf_op jit(solution)/shard_map/ppermute | solution.py:181
  6.6 12.7 %collective-permute-start.1 = (f32[4,160,128]{2,1,0:T(8,128)S(1)}, f32[4,160,128]{2,1,0:T(8,128)S(1)}, u32[]{:S(2)}, u32[]{:S(2)}) collective-permute-start(f32[4,160,128]{2,1,0:T(8,128)S(1)} %get-tuple-element.81), channel_id=1, source_target_pairs={{0,16},{1,17},{2,18},{3,19},{4,20},{5,21},{6,22},{7,23},{16,0},{17... | collective-permute-start | bytes 983048 | tf_op jit(solution)/shard_map/ppermute | solution.py:181
  10.0 10.9 %collective-permute-start.2 = (f32[4,160,128]{2,1,0:T(8,128)S(1)}, f32[4,160,128]{2,1,0:T(8,128)S(1)}, u32[]{:S(2)}, u32[]{:S(2)}) collective-permute-start(f32[4,160,128]{2,1,0:T(8,128)S(1)} %get-tuple-element.81), channel_id=1, source_target_pairs={{8,16},{9,17},{10,18},{11,19},{12,20},{13,21},{14,22},{15,23},{24,... | collective-permute-start | bytes 983048 | tf_op jit(solution)/shard_map/ppermute | solution.py:181
  11.3 25.3 %collective-permute-start.3 = (f32[4,160,128]{2,1,0:T(8,128)S(1)}, f32[4,160,128]{2,1,0:T(8,128)S(1)}, u32[]{:S(2)}, u32[]{:S(2)}) collective-permute-start(f32[4,160,128]{2,1,0:T(8,128)S(1)} %get-tuple-element.82), channel_id=1, source_target_pairs={{0,32},{1,33},{2,34},{3,35},{4,36},{5,37},{6,38},{7,39},{16,48},{1... | collective-permute-start | bytes 983048 | tf_op jit(solution)/shard_map/ppermute | solution.py:181
  15.6 25.2 %collective-permute-start.4 = (f32[4,160,128]{2,1,0:T(8,128)S(1)}, f32[4,160,128]{2,1,0:T(8,128)S(1)}, u32[]{:S(2)}, u32[]{:S(2)}) collective-permute-start(f32[4,160,128]{2,1,0:T(8,128)S(1)} %get-tuple-element.82), channel_id=1, source_target_pairs={{8,32},{9,33},{10,34},{11,35},{12,36},{13,37},{14,38},{15,39},{24,... | collective-permute-start | bytes 983048 | tf_op jit(solution)/shard_map/ppermute | solution.py:181
  16.9 23.9 %collective-permute-start.5 = (f32[4,160,128]{2,1,0:T(8,128)S(1)}, f32[4,160,128]{2,1,0:T(8,128)S(1)}, u32[]{:S(2)}, u32[]{:S(2)}) collective-permute-start(f32[4,160,128]{2,1,0:T(8,128)S(1)} %get-tuple-element.83), channel_id=1, source_target_pairs={{0,48},{1,49},{2,50},{3,51},{4,52},{5,53},{6,54},{7,55},{16,32},{1... | collective-permute-start | bytes 983048 | tf_op jit(solution)/shard_map/ppermute | solution.py:181
  19.4 21.5 %collective-permute-start.6 = (f32[4,160,128]{2,1,0:T(8,128)S(1)}, f32[4,160,128]{2,1,0:T(8,128)S(1)}, u32[]{:S(2)}, u32[]{:S(2)}) collective-permute-start(f32[4,160,128]{2,1,0:T(8,128)S(1)} %get-tuple-element.83), channel_id=1, source_target_pairs={{8,48},{9,49},{10,50},{11,51},{12,52},{13,53},{14,54},{15,55},{24,... | collective-permute-start | bytes 983048 | tf_op jit(solution)/shard_map/ppermute | solution.py:181
  41.3 2.0 collective-permute-start.8
  42.0 1.4 collective-permute-start.7
  42.6 0.7 collective-permute-start.9
  43.4 2.0 collective-permute-start.11
  44.0 1.4 collective-permute-start.10
  44.7 0.7 collective-permute-start.12
  45.5 2.0 collective-permute-start.14
  46.1 1.4 collective-permute-start.13
  46.8 0.7 collective-permute-start.15
  47.5 2.0 collective-permute-start.17
  48.2 1.4 collective-permute-start.16
  48.9 0.7 collective-permute-start.18
  49.6 29.3 %collective-permute-start.20 = (f32[8,2,8,128]{3,2,1,0:T(8,128)S(1)}, f32[8,2,8,128]{3,2,1,0:T(8,128)S(1)}, u32[]{:S(2)}, u32[]{:S(2)}) collective-permute-start(f32[8,2,8,128]{3,2,1,0:T(8,128)S(1)} %get-tuple-element.103), channel_id=1, source_target_pairs={{4,5},{19,20},{34,35},{49,50},{67,68},{82,83},{97,98},{112,113},{1... | collective-permute-start | bytes 196616 | tf_op jit(solution)/shard_map/ppermute | solution.py:229
  50.9 28.0 %collective-permute-start.19 = (f32[4,8,128]{2,1,0:T(8,128)S(1)}, f32[4,8,128]{2,1,0:T(8,128)S(1)}, u32[]{:S(2)}, u32[]{:S(2)}) collective-permute-start(f32[4,8,128]{2,1,0:T(8,128)S(1)} %get-tuple-element.102), channel_id=1, source_target_pairs={{4,68},{19,83},{34,98},{49,113},{67,131},{82,146},{97,161},{112,17... | collective-permute-start | bytes 49160 | tf_op jit(solution)/shard_map/ppermute | solution.py:228
  52.2 0.7 collective-permute-start.21
  78.9 3.9 %collective-permute-start.23 = (f32[8,2,8,128]{3,2,1,0:T(8,128)S(1)}, f32[8,2,8,128]{3,2,1,0:T(8,128)S(1)}, u32[]{:S(2)}, u32[]{:S(2)}) collective-permute-start(f32[8,2,8,128]{3,2,1,0:T(8,128)S(1)} %get-tuple-element.107), channel_id=1, source_target_pairs={{5,6},{20,21},{35,36},{50,51},{68,69},{83,84},{98,99},{113,114},{1... | collective-permute-start | bytes 196616 | tf_op jit(solution)/shard_map/ppermute | solution.py:229
  79.6 3.3 %collective-permute-start.22 = (f32[4,8,128]{2,1,0:T(8,128)S(1)}, f32[4,8,128]{2,1,0:T(8,128)S(1)}, u32[]{:S(2)}, u32[]{:S(2)}) collective-permute-start(f32[4,8,128]{2,1,0:T(8,128)S(1)} %get-tuple-element.106), channel_id=1, source_target_pairs={{5,69},{20,84},{35,99},{50,114},{68,132},{83,147},{98,162},{113,17... | collective-permute-start | bytes 49160 | tf_op jit(solution)/shard_map/ppermute | solution.py:228
  80.2 2.6 %collective-permute-start.24 = (f32[8,128]{1,0:T(8,128)S(1)}, f32[8,128]{1,0:T(8,128)S(1)}, u32[]{:S(2)}, u32[]{:S(2)}) collective-permute-start(f32[8,128]{1,0:T(8,128)S(1)} %get-tuple-element.108), channel_id=1, source_target_pairs={{5,21},{20,36},{35,51},{68,84},{83,99},{98,114},{131,147},{146,162... | collective-permute-start | bytes 12296 | tf_op jit(solution)/shard_map/ppermute | solution.py:230
  82.9 2.0 collective-permute-start.26
  83.5 1.4 collective-permute-start.25
  84.2 0.7 collective-permute-start.27
  85.0 2.0 collective-permute-start.29
  85.6 1.4 collective-permute-start.28
  86.3 0.7 collective-permute-start.30
  87.0 2.0 collective-permute-start.32
  87.7 1.4 collective-permute-start.31
  88.4 0.7 collective-permute-start.33
  89.1 2.0 collective-permute-start.35
  89.8 1.4 collective-permute-start.34
  90.5 0.7 collective-permute-start.36
  91.2 2.0 collective-permute-start.38
  91.9 1.4 collective-permute-start.37
  92.5 0.7 collective-permute-start.39
  93.3 2.0 collective-permute-start.41
  94.0 1.4 collective-permute-start.40
  94.6 0.7 collective-permute-start.42
  95.4 2.0 collective-permute-start.44
  96.0 1.4 collective-permute-start.43
  96.7 0.7 collective-permute-start.45
  97.4 74.5 %collective-permute-start.47 = (f32[8,2,8,128]{3,2,1,0:T(8,128)S(1)}, f32[8,2,8,128]{3,2,1,0:T(8,128)S(1)}, u32[]{:S(2)}, u32[]{:S(2)}) collective-permute-start(f32[8,2,8,128]{3,2,1,0:T(8,128)S(1)} %get-tuple-element.139), channel_id=1, source_target_pairs={{4,5},{19,20},{34,35},{49,50},{67,68},{82,83},{97,98},{112,113},{1... | collective-permute-start | bytes 196616 | tf_op jit(solution)/shard_map/ppermute | solution.py:229
  98.7 72.6 %collective-permute-start.46 = (f32[4,8,128]{2,1,0:T(8,128)S(1)}, f32[4,8,128]{2,1,0:T(8,128)S(1)}, u32[]{:S(2)}, u32[]{:S(2)}) collective-permute-start(f32[4,8,128]{2,1,0:T(8,128)S(1)} %get-tuple-element.138), channel_id=1, source_target_pairs={{4,68},{19,83},{34,98},{49,113},{67,131},{82,146},{97,161},{112,17... | collective-permute-start | bytes 49160 | tf_op jit(solution)/shard_map/ppermute | solution.py:228
  100.0 0.7 collective-permute-start.48
  175.5 4.0 %collective-permute-start.50 = (f32[8,2,8,128]{3,2,1,0:T(8,128)S(1)}, f32[8,2,8,128]{3,2,1,0:T(8,128)S(1)}, u32[]{:S(2)}, u32[]{:S(2)}) collective-permute-start(f32[8,2,8,128]{3,2,1,0:T(8,128)S(1)} %get-tuple-element.143), channel_id=1, source_target_pairs={{5,6},{20,21},{35,36},{50,51},{68,69},{83,84},{98,99},{113,114},{1... | collective-permute-start | bytes 196616 | tf_op jit(solution)/shard_map/ppermute | solution.py:229
  176.2 3.3 %collective-permute-start.49 = (f32[4,8,128]{2,1,0:T(8,128)S(1)}, f32[4,8,128]{2,1,0:T(8,128)S(1)}, u32[]{:S(2)}, u32[]{:S(2)}) collective-permute-start(f32[4,8,128]{2,1,0:T(8,128)S(1)} %get-tuple-element.142), channel_id=1, source_target_pairs={{5,69},{20,84},{35,99},{50,114},{68,132},{83,147},{98,162},{113,17... | collective-permute-start | bytes 49160 | tf_op jit(solution)/shard_map/ppermute | solution.py:228
  176.9 2.6 %collective-permute-start.51 = (f32[8,128]{1,0:T(8,128)S(1)}, f32[8,128]{1,0:T(8,128)S(1)}, u32[]{:S(2)}, u32[]{:S(2)}) collective-permute-start(f32[8,128]{1,0:T(8,128)S(1)} %get-tuple-element.144), channel_id=1, source_target_pairs={{5,21},{20,36},{35,51},{68,84},{83,99},{98,114},{131,147},{146,162... | collective-permute-start | bytes 12296 | tf_op jit(solution)/shard_map/ppermute | solution.py:230
  179.5 2.0 collective-permute-start.53
  180.2 1.4 collective-permute-start.52
  180.8 0.7 collective-permute-start.54
  181.6 2.0 collective-permute-start.56
  182.3 1.4 collective-permute-start.55
  182.9 0.7 collective-permute-start.57

commit v2 on v1

--- a/solution.py
+++ b/solution.py
@@ -9,7 +9,7 @@
 ROUNDS = 8
 REPEAT = 9
 VMEM = pl.BlockSpec(memory_space=pltpu.VMEM)
-ANY = pl.BlockSpec(memory_space=pl.ANY)
+HBM = pl.BlockSpec(memory_space=pltpu.HBM)
 
 
 def swap_groups(a):
@@ -23,8 +23,17 @@
     return out
 
 
-def pack_kernel(rhs, inverse, cx, cy, cz, *rest):
-    outs, small = rest[:4], rest[4]
+def pack_kernel(*refs):
+    sources, outs, small, held, arrived = refs[:5], refs[5:9], refs[9], refs[10:15], refs[15]
+    copies = [
+        pltpu.make_async_copy(source, target, arrived.at[i])
+        for i, (source, target) in enumerate(zip(sources, held))
+    ]
+    for copy in copies:
+        copy.start()
+    for copy in copies:
+        copy.wait()
+    rhs, inverse, cx, cy, cz = held
     chip = lax.rem(lax.axis_index("gx"), ROUNDS) // 2
     row = lax.broadcasted_iota(jnp.int32, (8, 128), 0)
     group = lax.broadcasted_iota(jnp.int32, (8, 128), 1) // 16
@@ -81,55 +90,48 @@
     def _():
         z_packed = in_z[...]
 
-        def advance(i, carry):
-            done, z_out = carry[:4], carry[4]
-            new = []
+        done = [in_x[b] for b in range(4)]
+        z_out = jnp.zeros((8, 128), jnp.float32)
+        for i in range(ROUNDS + 2):
+            before = list(done)
             for y in range(2):
                 for k in range(2):
-                    b = y * 2 + k
-                    x = i - y - k
-                    inside = (x >= 0) & (x < ROUNDS)
-                    xc = jnp.clip(x, 0, ROUNDS - 1)
-                    from_x = done[b]
-                    from_y = in_y[xc, k] if y == 0 else done[k]
+                    b, x = y * 2 + k, i - y - k
+                    if not 0 <= x < ROUNDS:
+                        continue
+                    from_y = in_y[x, k] if y == 0 else before[k]
                     if k == 0:
-                        from_z = pltpu.roll(z_packed, lax.rem(128 - (xc * 2 + y), 128), 1)
+                        place = x * 2 + y
+                        from_z = pltpu.roll(z_packed, 128 - place, 1) if place else z_packed
                     else:
-                        from_z = pltpu.roll(done[y * 2], 113, 1)
+                        from_z = pltpu.roll(before[y * 2], 113, 1)
                     terms = []
                     for m in range(8):
                         q = (
-                            rows[xc, b, 8 + m : 9 + m, :] * from_x
-                            + rows[xc, b, 16 + m : 17 + m, :] * from_y
-                            + rows[xc, b, 24 + m : 25 + m, :] * from_z
+                            rows[x, b, 8 + m : 9 + m, :] * before[b]
+                            + rows[x, b, 16 + m : 17 + m, :] * from_y
+                            + rows[x, b, 24 + m : 25 + m, :] * from_z
                         )
                         terms.append(pltpu.roll(q, 16 * m, 1) if m else q)
                     while len(terms) > 1:
                         terms = [u + v for u, v in zip(terms[::2], terms[1::2])]
-                    partial = rows[xc, b, 0:8, :] - terms[0]
+                    partial = rows[x, b, 0:8, :] - terms[0]
                     high = partial.astype(jnp.bfloat16).astype(jnp.float32)
                     both = jnp.concatenate([high, partial - high], axis=0).astype(jnp.bfloat16)
-                    product = jnp.dot(
-                        both, weights[xc, b], preferred_element_type=jnp.float32
-                    )
+                    product = jnp.dot(both, weights[x, b], preferred_element_type=jnp.float32)
                     solved = (product[0:8, 0:128] + product[8:16, 0:128]) + (
                         product[0:8, 128:256] + product[8:16, 128:256]
                     )
-                    solved = jnp.where(inside, solved, done[b])
-                    tile[xc, b] = solved
+                    tile[x, b] = solved
+                    done[b] = solved
                     if y == 1:
-                        out_y[xc, k] = solved
+                        out_y[x, k] = solved
                     if k == 1:
-                        kept = jnp.where(last_lane & inside, solved, 0.0)
-                        z_out = z_out + pltpu.roll(kept, lax.rem(xc * 2 + y + 113, 128), 1)
-                    new.append(solved)
-            return (*new, z_out)
-
-        carry = tuple(in_x[b] for b in range(4)) + (jnp.zeros((8, 128), jnp.float32),)
-        carry = lax.fori_loop(0, ROUNDS + 2, advance, carry)
+                        kept = jnp.where(last_lane, solved, 0.0)
+                        z_out = z_out + pltpu.roll(kept, (x * 2 + y + 113) % 128, 1)
         for b in range(4):
-            out_x[b] = carry[b]
-        out_z[...] = carry[4]
+            out_x[b] = done[b]
+        out_z[...] = z_out
 
 
 def unpack_kernel(parts, out):
@@ -154,9 +156,17 @@
     outs = pl.pallas_call(
         pack_kernel,
         out_shape=[f32(4, 160, 128)] * 4,
-        in_specs=[VMEM] * 5,
+        in_specs=[HBM] * 5,
         out_specs=[VMEM] * 4,
-        scratch_shapes=[pltpu.VMEM((2, 8, 32, 128), jnp.float32)],
+        scratch_shapes=[
+            pltpu.VMEM((2, 8, 32, 128), jnp.float32),
+            pltpu.VMEM((2, 8, 8, 128), jnp.float32),
+            pltpu.VMEM((2, 8, 128, 128), jnp.float32),
+            pltpu.VMEM((2, 8, 8, 128), jnp.float32),
+            pltpu.VMEM((2, 8, 8, 128), jnp.float32),
+            pltpu.VMEM((128, 8), jnp.float32),
+            pltpu.SemaphoreType.DMA((5,)),
+        ],
         compiler_params=pltpu.CompilerParams(vmem_limit_bytes=12 << 20),
         name="pack",
     )(
@@ -212,7 +222,7 @@
             out_specs=[VMEM] * 4,
             input_output_aliases={5: 0},
             compiler_params=pltpu.CompilerParams(vmem_limit_bytes=12 << 20),
-            name=f"tile_step",
+            name="tile_step",
         )(weights, rows, in_x, in_y, in_z, tile)
         if step == steps - 1:
             break

time: 219 us -> 195 us (0.89)
  the two profiles are of different devices: /device:TPU:318 before, /device:TPU:63 now
where the time goes in v2:
time: 195 us; the launch traced here: 194 us
  blocking collectives  121 us (62%)
  starting transfers between devices  56 us (29%)
  waiting for transfers between devices  6.28 us (3%)
  local copies, waits for them, and re-layouts  4.6 us (2%)
  Pallas kernels  4.57 us (2%)
    all_to_all x1, blocking collectives, local(): lax.all_to_all(tile, 'gx', 0, 0, axis_index_groups=groups, tiled=True)  121 us
    ppermute x7, starting transfers between devices, local(): parts.append(lax.ppermute(outs[r // 2], AXES, pairs))  22.2 us
    ppermute x17, starting transfers between devices, local(): in_y = lax.ppermute(out_y, AXES, to_y)  11.3 us
    ppermute x17, starting transfers between devices, local(): in_x = lax.ppermute(out_x, AXES, to_x)  11.3 us
    ppermute x17, starting transfers between devices, local(): in_z = lax.ppermute(out_z, AXES, to_z)  11.2 us
    ppermute x7, waiting for transfers between devices, local(): parts.append(lax.ppermute(outs[r // 2], AXES, pairs))  6.14 us
    unnamed x10, local copies, waits for them, and re-layouts  4.58 us
  transfers between devices with their start and end apart: 58, of which 2 were waited for; matrix products, arithmetic and copies ran while one was open for 0% of the time, Pallas kernels for 0%

profile of v2, /device:TPU:63, one launch (start us, length us, event | category | flops | bytes accessed | tf_op | source)
XLA Modules:
  0.0 193.8 jit_solution(16094248753560806865)
XLA Ops:
  0.0 1.2 copy-done
  1.2 0.8 copy-done.1
  2.1 0.8 copy-done.2
  2.9 0.8 copy-done.3
  3.7 0.8 copy-done.4
  4.6 1.1 pack.1
  5.7 2.6 %collective-permute-start = (f32[4,160,128]{2,1,0:T(8,128)S(1)}, f32[4,160,128]{2,1,0:T(8,128)S(1)}, u32[]{:S(2)}, u32[]{:S(2)}) collective-permute-start(f32[4,160,128]{2,1,0:T(8,128)S(1)} %get-tuple-element.80.refs_0_), channel_id=1, source_target_pairs={{8,0},{9,1},{10,2},{11,3},{12,4},{13,5},{14,6},{15,7},{24,16},{25,... | collective-permute-start | bytes 983048 | tf_op jit(solution)/shard_map/ppermute | solution.py:191
  8.3 0.7 collective-permute-start.1
  9.0 4.5 %collective-permute-start.2 = (f32[4,160,128]{2,1,0:T(8,128)S(1)}, f32[4,160,128]{2,1,0:T(8,128)S(1)}, u32[]{:S(2)}, u32[]{:S(2)}) collective-permute-start(f32[4,160,128]{2,1,0:T(8,128)S(1)} %get-tuple-element.81), channel_id=1, source_target_pairs={{8,16},{9,17},{10,18},{11,19},{12,20},{13,21},{14,22},{15,23},{24,... | collective-permute-start | bytes 983048 | tf_op jit(solution)/shard_map/ppermute | solution.py:191
  13.6 0.7 collective-permute-start.3
  14.2 6.7 %collective-permute-start.4 = (f32[4,160,128]{2,1,0:T(8,128)S(1)}, f32[4,160,128]{2,1,0:T(8,128)S(1)}, u32[]{:S(2)}, u32[]{:S(2)}) collective-permute-start(f32[4,160,128]{2,1,0:T(8,128)S(1)} %get-tuple-element.82), channel_id=1, source_target_pairs={{8,32},{9,33},{10,34},{11,35},{12,36},{13,37},{14,38},{15,39},{24,... | collective-permute-start | bytes 983048 | tf_op jit(solution)/shard_map/ppermute | solution.py:191
  21.0 0.7 collective-permute-start.5
  21.7 6.3 %collective-permute-start.6 = (f32[4,160,128]{2,1,0:T(8,128)S(1)}, f32[4,160,128]{2,1,0:T(8,128)S(1)}, u32[]{:S(2)}, u32[]{:S(2)}) collective-permute-start(f32[4,160,128]{2,1,0:T(8,128)S(1)} %get-tuple-element.83), channel_id=1, source_target_pairs={{8,48},{9,49},{10,50},{11,51},{12,52},{13,53},{14,54},{15,55},{24,... | collective-permute-start | bytes 983048 | tf_op jit(solution)/shard_map/ppermute | solution.py:191
  28.5 5.7 %collective-permute-done.6.refs_7_ = f32[4,160,128]{2,1,0:T(8,128)S(1)} collective-permute-done((f32[4,160,128]{2,1,0:T(8,128)S(1)}, f32[4,160,128]{2,1,0:T(8,128)S(1)}, u32[]{:S(2)}, u32[]{:S(2)}) %collective-permute-start.6) | collective-permute-done | bytes 327712 | tf_op jit(solution)/shard_map/ppermute | solution.py:191
  34.6 0.7 collective-permute-start.8
  35.3 0.7 collective-permute-start.7
  35.9 0.7 collective-permute-start.9
  36.7 0.7 collective-permute-start.11
  37.4 0.7 collective-permute-start.10
  38.0 0.7 collective-permute-start.12
  38.8 0.7 collective-permute-start.14
  39.4 0.7 collective-permute-start.13
  40.8 0.7 collective-permute-start.17
  41.5 0.7 collective-permute-start.16
  42.2 0.7 collective-permute-start.18
  42.9 0.7 collective-permute-start.20
  43.6 0.7 collective-permute-start.19
  44.3 0.7 collective-permute-start.21
  45.0 0.7 collective-permute-start.23
  45.7 0.7 collective-permute-start.22
  46.4 0.7 collective-permute-start.24
  47.1 0.7 collective-permute-start.26
  47.8 0.7 collective-permute-start.25
  48.4 0.7 collective-permute-start.27
  49.2 0.7 collective-permute-start.29
  49.8 0.7 collective-permute-start.28
  50.5 0.7 collective-permute-start.30
  51.3 0.7 collective-permute-start.32
  51.9 0.7 collective-permute-start.31
  52.6 0.7 collective-permute-start.33
  53.3 0.7 collective-permute-start.35
  54.0 0.7 collective-permute-start.34
  54.7 0.7 collective-permute-start.36
  55.6 0.7 collective-permute-start.38
  56.3 0.7 collective-permute-start.37
  56.9 0.7 collective-permute-start.39
  57.7 0.7 collective-permute-start.41
  58.4 0.7 collective-permute-start.40
  59.0 0.7 collective-permute-start.42
  59.8 0.7 collective-permute-start.44
  60.4 0.7 collective-permute-start.43
  61.1 0.7 collective-permute-start.45
  61.8 0.7 collective-permute-start.47
  62.5 0.7 collective-permute-start.46
  63.2 0.7 collective-permute-start.48
  63.9 0.7 collective-permute-start.50
  64.6 0.7 collective-permute-start.49
  65.3 0.7 collective-permute-start.51
  66.0 0.7 collective-permute-start.53
  66.7 0.7 collective-permute-start.52
  68.1 0.7 collective-permute-start.56
  68.8 0.7 collective-permute-start.55
  70.8 121.2 %all_to_all.5.parts = f32[8,4,8,128]{3,2,1,0:T(8,128)} all-to-all(f32[8,4,8,128]{3,2,1,0:T(8,128)S(1)} %get-tuple-element.154), channel_id=1, replica_groups={{0,8,16,24,32,40,48,56},{64,72,80,88,96,104,112,120},{128,136,144,152,1..., dimensions={0} | all-to-all | bytes 262144 | tf_op jit(solution)/shard_map/all_to_all | solution.py:243
  192.0 1.7 unpack.1
  (88 shorter events, 4.3 us)
Async XLA Ops:
  0.0 1.2 copy-start
  1.2 0.8 copy-start.1
  2.1 0.8 copy-start.2
  2.9 0.8 copy-start.3
  3.7 0.8 copy-start.4
  5.7 15.2 %collective-permute-start = (f32[4,160,128]{2,1,0:T(8,128)S(1)}, f32[4,160,128]{2,1,0:T(8,128)S(1)}, u32[]{:S(2)}, u32[]{:S(2)}) collective-permute-start(f32[4,160,128]{2,1,0:T(8,128)S(1)} %get-tuple-element.80.refs_0_), channel_id=1, source_target_pairs={{8,0},{9,1},{10,2},{11,3},{12,4},{13,5},{14,6},{15,7},{24,16},{25,... | collective-permute-start | bytes 983048 | tf_op jit(solution)/shard_map/ppermute | solution.py:191
  8.3 13.3 %collective-permute-start.1 = (f32[4,160,128]{2,1,0:T(8,128)S(1)}, f32[4,160,128]{2,1,0:T(8,128)S(1)}, u32[]{:S(2)}, u32[]{:S(2)}) collective-permute-start(f32[4,160,128]{2,1,0:T(8,128)S(1)} %get-tuple-element.81), channel_id=1, source_target_pairs={{0,16},{1,17},{2,18},{3,19},{4,20},{5,21},{6,22},{7,23},{16,0},{17... | collective-permute-start | bytes 983048 | tf_op jit(solution)/shard_map/ppermute | solution.py:191
  9.0 19.0 %collective-permute-start.2 = (f32[4,160,128]{2,1,0:T(8,128)S(1)}, f32[4,160,128]{2,1,0:T(8,128)S(1)}, u32[]{:S(2)}, u32[]{:S(2)}) collective-permute-start(f32[4,160,128]{2,1,0:T(8,128)S(1)} %get-tuple-element.81), channel_id=1, source_target_pairs={{8,16},{9,17},{10,18},{11,19},{12,20},{13,21},{14,22},{15,23},{24,... | collective-permute-start | bytes 983048 | tf_op jit(solution)/shard_map/ppermute | solution.py:191
  13.6 14.5 %collective-permute-start.3 = (f32[4,160,128]{2,1,0:T(8,128)S(1)}, f32[4,160,128]{2,1,0:T(8,128)S(1)}, u32[]{:S(2)}, u32[]{:S(2)}) collective-permute-start(f32[4,160,128]{2,1,0:T(8,128)S(1)} %get-tuple-element.82), channel_id=1, source_target_pairs={{0,32},{1,33},{2,34},{3,35},{4,36},{5,37},{6,38},{7,39},{16,48},{1... | collective-permute-start | bytes 983048 | tf_op jit(solution)/shard_map/ppermute | solution.py:191
  14.2 14.2 %collective-permute-start.4 = (f32[4,160,128]{2,1,0:T(8,128)S(1)}, f32[4,160,128]{2,1,0:T(8,128)S(1)}, u32[]{:S(2)}, u32[]{:S(2)}) collective-permute-start(f32[4,160,128]{2,1,0:T(8,128)S(1)} %get-tuple-element.82), channel_id=1, source_target_pairs={{8,32},{9,33},{10,34},{11,35},{12,36},{13,37},{14,38},{15,39},{24,... | collective-permute-start | bytes 983048 | tf_op jit(solution)/shard_map/ppermute | solution.py:191
  21.0 7.5 %collective-permute-start.5 = (f32[4,160,128]{2,1,0:T(8,128)S(1)}, f32[4,160,128]{2,1,0:T(8,128)S(1)}, u32[]{:S(2)}, u32[]{:S(2)}) collective-permute-start(f32[4,160,128]{2,1,0:T(8,128)S(1)} %get-tuple-element.83), channel_id=1, source_target_pairs={{0,48},{1,49},{2,50},{3,51},{4,52},{5,53},{6,54},{7,55},{16,32},{1... | collective-permute-start | bytes 983048 | tf_op jit(solution)/shard_map/ppermute | solution.py:191
  21.7 12.5 %collective-permute-start.6 = (f32[4,160,128]{2,1,0:T(8,128)S(1)}, f32[4,160,128]{2,1,0:T(8,128)S(1)}, u32[]{:S(2)}, u32[]{:S(2)}) collective-permute-start(f32[4,160,128]{2,1,0:T(8,128)S(1)} %get-tuple-element.83), channel_id=1, source_target_pairs={{8,48},{9,49},{10,50},{11,51},{12,52},{13,53},{14,54},{15,55},{24,... | collective-permute-start | bytes 983048 | tf_op jit(solution)/shard_map/ppermute | solution.py:191
  34.6 2.0 %collective-permute-start.8 = (f32[8,2,8,128]{3,2,1,0:T(8,128)S(1)}, f32[8,2,8,128]{3,2,1,0:T(8,128)S(1)}, u32[]{:S(2)}, u32[]{:S(2)}) collective-permute-start(f32[8,2,8,128]{3,2,1,0:T(8,128)S(1)} %get-tuple-element.87), channel_id=1, source_target_pairs={{0,1},{54,55},{102,103},{117,118},{150,151},{165,166},{180,181},{1... | collective-permute-start | bytes 196616 | tf_op jit(solution)/shard_map/ppermute | solution.py:239
  35.3 1.4 collective-permute-start.7
  35.9 0.7 collective-permute-start.9
  36.7 2.0 %collective-permute-start.11 = (f32[8,2,8,128]{3,2,1,0:T(8,128)S(1)}, f32[8,2,8,128]{3,2,1,0:T(8,128)S(1)}, u32[]{:S(2)}, u32[]{:S(2)}) collective-permute-start(f32[8,2,8,128]{3,2,1,0:T(8,128)S(1)} %get-tuple-element.91), channel_id=1, source_target_pairs={{1,2},{16,17},{64,65},{118,119},{166,167},{181,182},{214,215},{229... | collective-permute-start | bytes 196616 | tf_op jit(solution)/shard_map/ppermute | solution.py:239
  37.4 1.4 collective-permute-start.10
  38.0 0.7 collective-permute-start.12
  38.8 2.0 %collective-permute-start.14 = (f32[8,2,8,128]{3,2,1,0:T(8,128)S(1)}, f32[8,2,8,128]{3,2,1,0:T(8,128)S(1)}, u32[]{:S(2)}, u32[]{:S(2)}) collective-permute-start(f32[8,2,8,128]{3,2,1,0:T(8,128)S(1)} %get-tuple-element.95), channel_id=1, source_target_pairs={{2,3},{17,18},{32,33},{65,66},{80,81},{128,129},{182,183},{230,231... | collective-permute-start | bytes 196616 | tf_op jit(solution)/shard_map/ppermute | solution.py:239
  39.4 1.4 collective-permute-start.13
  40.1 0.7 collective-permute-start.15
  40.8 2.0 %collective-permute-start.17 = (f32[8,2,8,128]{3,2,1,0:T(8,128)S(1)}, f32[8,2,8,128]{3,2,1,0:T(8,128)S(1)}, u32[]{:S(2)}, u32[]{:S(2)}) collective-permute-start(f32[8,2,8,128]{3,2,1,0:T(8,128)S(1)} %get-tuple-element.99), channel_id=1, source_target_pairs={{3,4},{18,19},{33,34},{48,49},{66,67},{81,82},{96,97},{129,130},{1... | collective-permute-start | bytes 196616 | tf_op jit(solution)/shard_map/ppermute | solution.py:239
  41.5 1.4 collective-permute-start.16
  42.2 0.7 collective-permute-start.18
  42.9 2.0 %collective-permute-start.20 = (f32[8,2,8,128]{3,2,1,0:T(8,128)S(1)}, f32[8,2,8,128]{3,2,1,0:T(8,128)S(1)}, u32[]{:S(2)}, u32[]{:S(2)}) collective-permute-start(f32[8,2,8,128]{3,2,1,0:T(8,128)S(1)} %get-tuple-element.103), channel_id=1, source_target_pairs={{4,5},{19,20},{34,35},{49,50},{67,68},{82,83},{97,98},{112,113},{1... | collective-permute-start | bytes 196616 | tf_op jit(solution)/shard_map/ppermute | solution.py:239
  43.6 1.4 collective-permute-start.19
  44.3 0.7 collective-permute-start.21
  45.0 2.0 %collective-permute-start.23 = (f32[8,2,8,128]{3,2,1,0:T(8,128)S(1)}, f32[8,2,8,128]{3,2,1,0:T(8,128)S(1)}, u32[]{:S(2)}, u32[]{:S(2)}) collective-permute-start(f32[8,2,8,128]{3,2,1,0:T(8,128)S(1)} %get-tuple-element.107), channel_id=1, source_target_pairs={{5,6},{20,21},{35,36},{50,51},{68,69},{83,84},{98,99},{113,114},{1... | collective-permute-start | bytes 196616 | tf_op jit(solution)/shard_map/ppermute | solution.py:239
  45.7 1.4 collective-permute-start.22
  46.4 0.7 collective-permute-start.24
  47.1 2.0 %collective-permute-start.26 = (f32[8,2,8,128]{3,2,1,0:T(8,128)S(1)}, f32[8,2,8,128]{3,2,1,0:T(8,128)S(1)}, u32[]{:S(2)}, u32[]{:S(2)}) collective-permute-start(f32[8,2,8,128]{3,2,1,0:T(8,128)S(1)} %get-tuple-element.111), channel_id=1, source_target_pairs={{6,7},{21,22},{36,37},{51,52},{69,70},{84,85},{99,100},{114,115},{... | collective-permute-start | bytes 196616 | tf_op jit(solution)/shard_map/ppermute | solution.py:239
  47.8 1.4 collective-permute-start.25
  48.4 0.7 collective-permute-start.27
  49.2 2.0 %collective-permute-start.29 = (f32[8,2,8,128]{3,2,1,0:T(8,128)S(1)}, f32[8,2,8,128]{3,2,1,0:T(8,128)S(1)}, u32[]{:S(2)}, u32[]{:S(2)}) collective-permute-start(f32[8,2,8,128]{3,2,1,0:T(8,128)S(1)} %get-tuple-element.115), channel_id=1, source_target_pairs={{22,23},{37,38},{52,53},{70,71},{85,86},{100,101},{115,116},{133,1... | collective-permute-start | bytes 196616 | tf_op jit(solution)/shard_map/ppermute | solution.py:239
  49.8 1.4 collective-permute-start.28
  50.5 0.7 collective-permute-start.30
  51.3 2.0 %collective-permute-start.32 = (f32[8,2,8,128]{3,2,1,0:T(8,128)S(1)}, f32[8,2,8,128]{3,2,1,0:T(8,128)S(1)}, u32[]{:S(2)}, u32[]{:S(2)}) collective-permute-start(f32[8,2,8,128]{3,2,1,0:T(8,128)S(1)} %get-tuple-element.119), channel_id=1, source_target_pairs={{38,39},{53,54},{86,87},{101,102},{116,117},{134,135},{149,150},{1... | collective-permute-start | bytes 196616 | tf_op jit(solution)/shard_map/ppermute | solution.py:239
  51.9 1.4 collective-permute-start.31
  52.6 0.7 collective-permute-start.33
  53.3 2.0 %collective-permute-start.35 = (f32[8,2,8,128]{3,2,1,0:T(8,128)S(1)}, f32[8,2,8,128]{3,2,1,0:T(8,128)S(1)}, u32[]{:S(2)}, u32[]{:S(2)}) collective-permute-start(f32[8,2,8,128]{3,2,1,0:T(8,128)S(1)} %get-tuple-element.123), channel_id=1, source_target_pairs={{0,1},{54,55},{102,103},{117,118},{150,151},{165,166},{180,181},{1... | collective-permute-start | bytes 196616 | tf_op jit(solution)/shard_map/ppermute | solution.py:239
  54.0 1.4 collective-permute-start.34
  54.7 0.7 collective-permute-start.36
  55.6 2.0 %collective-permute-start.38 = (f32[8,2,8,128]{3,2,1,0:T(8,128)S(1)}, f32[8,2,8,128]{3,2,1,0:T(8,128)S(1)}, u32[]{:S(2)}, u32[]{:S(2)}) collective-permute-start(f32[8,2,8,128]{3,2,1,0:T(8,128)S(1)} %get-tuple-element.127), channel_id=1, source_target_pairs={{1,2},{16,17},{64,65},{118,119},{166,167},{181,182},{214,215},{229... | collective-permute-start | bytes 196616 | tf_op jit(solution)/shard_map/ppermute | solution.py:239
  56.3 1.4 collective-permute-start.37
  56.9 0.7 collective-permute-start.39
  57.7 2.0 %collective-permute-start.41 = (f32[8,2,8,128]{3,2,1,0:T(8,128)S(1)}, f32[8,2,8,128]{3,2,1,0:T(8,128)S(1)}, u32[]{:S(2)}, u32[]{:S(2)}) collective-permute-start(f32[8,2,8,128]{3,2,1,0:T(8,128)S(1)} %get-tuple-element.131), channel_id=1, source_target_pairs={{2,3},{17,18},{32,33},{65,66},{80,81},{128,129},{182,183},{230,231... | collective-permute-start | bytes 196616 | tf_op jit(solution)/shard_map/ppermute | solution.py:239
  58.4 1.4 collective-permute-start.40
  59.0 0.7 collective-permute-start.42
  59.8 2.0 %collective-permute-start.44 = (f32[8,2,8,128]{3,2,1,0:T(8,128)S(1)}, f32[8,2,8,128]{3,2,1,0:T(8,128)S(1)}, u32[]{:S(2)}, u32[]{:S(2)}) collective-permute-start(f32[8,2,8,128]{3,2,1,0:T(8,128)S(1)} %get-tuple-element.135), channel_id=1, source_target_pairs={{3,4},{18,19},{33,34},{48,49},{66,67},{81,82},{96,97},{129,130},{1... | collective-permute-start | bytes 196616 | tf_op jit(solution)/shard_map/ppermute | solution.py:239
  60.4 1.4 collective-permute-start.43
  61.1 0.7 collective-permute-start.45
  61.8 2.0 %collective-permute-start.47 = (f32[8,2,8,128]{3,2,1,0:T(8,128)S(1)}, f32[8,2,8,128]{3,2,1,0:T(8,128)S(1)}, u32[]{:S(2)}, u32[]{:S(2)}) collective-permute-start(f32[8,2,8,128]{3,2,1,0:T(8,128)S(1)} %get-tuple-element.139), channel_id=1, source_target_pairs={{4,5},{19,20},{34,35},{49,50},{67,68},{82,83},{97,98},{112,113},{1... | collective-permute-start | bytes 196616 | tf_op jit(solution)/shard_map/ppermute | solution.py:239
  62.5 1.4 collective-permute-start.46
  63.2 0.7 collective-permute-start.48
  63.9 2.0 %collective-permute-start.50 = (f32[8,2,8,128]{3,2,1,0:T(8,128)S(1)}, f32[8,2,8,128]{3,2,1,0:T(8,128)S(1)}, u32[]{:S(2)}, u32[]{:S(2)}) collective-permute-start(f32[8,2,8,128]{3,2,1,0:T(8,128)S(1)} %get-tuple-element.143), channel_id=1, source_target_pairs={{5,6},{20,21},{35,36},{50,51},{68,69},{83,84},{98,99},{113,114},{1... | collective-permute-start | bytes 196616 | tf_op jit(solution)/shard_map/ppermute | solution.py:239
  64.6 1.4 collective-permute-start.49
  65.3 0.7 collective-permute-start.51
  66.0 2.0 %collective-permute-start.53 = (f32[8,2,8,128]{3,2,1,0:T(8,128)S(1)}, f32[8,2,8,128]{3,2,1,0:T(8,128)S(1)}, u32[]{:S(2)}, u32[]{:S(2)}) collective-permute-start(f32[8,2,8,128]{3,2,1,0:T(8,128)S(1)} %get-tuple-element.147), channel_id=1, source_target_pairs={{6,7},{21,22},{36,37},{51,52},{69,70},{84,85},{99,100},{114,115},{... | collective-permute-start | bytes 196616 | tf_op jit(solution)/shard_map/ppermute | solution.py:239
  66.7 1.4 collective-permute-start.52
  67.3 0.7 collective-permute-start.54
  68.1 2.0 %collective-permute-start.56 = (f32[8,2,8,128]{3,2,1,0:T(8,128)S(1)}, f32[8,2,8,128]{3,2,1,0:T(8,128)S(1)}, u32[]{:S(2)}, u32[]{:S(2)}) collective-permute-start(f32[8,2,8,128]{3,2,1,0:T(8,128)S(1)} %get-tuple-element.151), channel_id=1, source_target_pairs={{22,23},{37,38},{52,53},{70,71},{85,86},{100,101},{115,116},{133,1... | collective-permute-start | bytes 196616 | tf_op jit(solution)/shard_map/ppermute | solution.py:239
  68.8 1.4 collective-permute-start.55
  69.4 0.7 collective-permute-start.57

commit v3 on v2

v3 whole, which is shorter than its diff:
```python
import jax
import jax.numpy as jnp
from jax import lax
from jax.experimental import pallas as pl
from jax.experimental.pallas import tpu as pltpu
from jax.sharding import PartitionSpec as P

AXES = ("gx", "gy")
TILE_X = 8
TILE_Y = 4
ROUNDS = 16
OWNERS = (2, 4)
REPEAT = 6
VMEM = pl.BlockSpec(memory_space=pltpu.VMEM)
HBM = pl.BlockSpec(memory_space=pltpu.HBM)


def swap_groups(a):
    row = lax.broadcasted_iota(jnp.int32, a.shape, 0)
    group = lax.broadcasted_iota(jnp.int32, a.shape, 1) // 16
    ahead = (group - row) & 7
    out = a
    for d in range(1, 8):
        moved = pltpu.roll(pltpu.roll(a, 8 - d, 0), 16 * d, 1)
        out = jnp.where(ahead == d, moved, out)
    return out


def pack_kernel(*refs):
    sources, outs, small, held, arrived = refs[:5], refs[5:9], refs[9], refs[10:15], refs[15]
    copies = [
        pltpu.make_async_copy(source, target, arrived.at[i])
        for i, (source, target) in enumerate(zip(sources, held))
    ]
    for copy in copies:
        copy.start()
    for copy in copies:
        copy.wait()
    rhs, inverse, cx, cy, cz = held
    right = lax.rem(lax.axis_index("gx"), TILE_X) // 4
    upper = lax.rem(lax.axis_index("gy"), 2)
    row = lax.broadcasted_iota(jnp.int32, (8, 128), 0)
    group = lax.broadcasted_iota(jnp.int32, (8, 128), 1) // 16
    spread_row = lax.broadcasted_iota(jnp.int32, (8, 128), 0)
    spread_lane = lax.broadcasted_iota(jnp.int32, (8, 128), 1)
    spread = jnp.where(spread_lane == 16 * spread_row, 1.0, 0.0)
    heads = jnp.dot(
        cz[...], spread, precision=lax.Precision.HIGHEST, preferred_element_type=jnp.float32
    )
    for y in range(2):
        for n in range(8):
            small[y, :, n, :] = swap_groups(rhs[y, n])
        for ref, base in ((cx, 8), (cy, 16)):
            for m in range(8):
                a = ref[y, m]
                for c in range(8):
                    if c != m:
                        a = jnp.where(row == (c - m) % 8, ref[y, c], a)
                small[y, :, base + m, :] = swap_groups(a)
        for s in range(8):
            t = heads[(y * 8 + s) * 8 : (y * 8 + s + 1) * 8]
            out = t
            for d in range(1, 8):
                out = jnp.where(group == d, pltpu.roll(t, 8 - d, 0), out)
            small[y, s, 24:32, :] = out
    for q in range(4):
        first = 4 * (upper ^ (q // 2)) + 2 * (right ^ (q % 2))
        for y in range(2):
            for k in range(2):
                outs[q][y * 2 + k, 0:128, :] = inverse[y, first + k].T
                outs[q][y * 2 + k, 128:160, :] = small[y, first + k]


def prepare_kernel(*refs):
    parts, weights, rows = refs[:ROUNDS], refs[ROUNDS], refs[ROUNDS + 1]
    place = lax.rem(lax.axis_index("gx"), TILE_X)
    upper = lax.rem(lax.axis_index("gy"), 2)
    for r in range(ROUNDS):
        x, half = place ^ (r % TILE_X), upper ^ (r // TILE_X)
        for b in range(4):
            full = parts[r][b, 0:128, :]
            high = full.astype(jnp.bfloat16)
            low = (full - high.astype(jnp.float32)).astype(jnp.bfloat16)
            weights[x, half, b, :, 0:128] = high
            weights[x, half, b, :, 128:256] = low
            rows[x, half, b] = parts[r][b, 128:160, :]


def tile_level(gx, gy):
    return gx // TILE_X + gy // 2 + 2 * (gy % 2) + (gx % TILE_X) // 4


def step_kernel(step, weights, rows, in_x, in_y, in_z, _, tile, out_x, out_y, out_z):
    gx, gy = lax.axis_index("gx"), lax.axis_index("gy")
    place = lax.rem(gx, TILE_X)
    owner = (place == OWNERS[0]) | (place == OWNERS[1])
    level = gx // TILE_X + gy // 2 + 2 * lax.rem(gy, 2) + place // 4
    last_lane = lax.rem(lax.broadcasted_iota(jnp.int32, (8, 128), 1), 16) == 15

    @pl.when(owner & (level == step))
    def _():
        z_in = [in_z[h] for h in range(2)]
        z_out = [jnp.zeros((8, 128), jnp.float32) for h in range(2)]
        done = [in_x[b] for b in range(2 * TILE_Y)]
        for i in range(TILE_X + TILE_Y):
            before = list(done)
            for y in range(TILE_Y):
                for k in range(2):
                    b, x = y * 2 + k, i - y - k
                    if not 0 <= x < TILE_X:
                        continue
                    half, j = b // 4, b % 4
                    word, lane = (x * TILE_Y + y) // 16, (x * TILE_Y + y) % 16
                    from_y = in_y[x, k] if y == 0 else before[b - 2]
                    if k == 1:
                        from_z = pltpu.roll(before[b - 1], 113, 1)
                    else:
                        from_z = pltpu.roll(z_in[word], 128 - lane, 1) if lane else z_in[word]
                    terms = []
                    for m in range(8):
                        q = (
                            rows[x, half, j, 8 + m : 9 + m, :] * before[b]
                            + rows[x, half, j, 16 + m : 17 + m, :] * from_y
                            + rows[x, half, j, 24 + m : 25 + m, :] * from_z
                        )
                        terms.append(pltpu.roll(q, 16 * m, 1) if m else q)
                    while len(terms) > 1:
                        terms = [u + v for u, v in zip(terms[::2], terms[1::2])]
                    partial = rows[x, half, j, 0:8, :] - terms[0]
                    high = partial.astype(jnp.bfloat16).astype(jnp.float32)
                    both = jnp.concatenate([high, partial - high], axis=0).astype(jnp.bfloat16)
                    product = jnp.dot(
                        both, weights[x, half, j], preferred_element_type=jnp.float32
                    )
                    solved = (product[0:8, 0:128] + product[8:16, 0:128]) + (
                        product[0:8, 128:256] + product[8:16, 128:256]
                    )
                    tile[x, half, j] = solved
                    done[b] = solved
                    if y == TILE_Y - 1:
                        out_y[x, k] = solved
                    if k == 1:
                        kept = jnp.where(last_lane, solved, 0.0)
                        z_out[word] = z_out[word] + pltpu.roll(kept, (lane + 113) % 128, 1)
        for b in range(2 * TILE_Y):
            out_x[b] = done[b]
        for h in range(2):
            out_z[h] = z_out[h]


def unpack_kernel(parts, out):
    for y in range(2):
        for n in range(8):
            rows = jnp.concatenate(
                [
                    parts[2 * OWNERS[s // 2 % 2] + s // 4, y * 2 + s % 2, n : n + 1, :]
                    for s in range(8)
                ],
                axis=0,
            )
            out[y, n] = swap_groups(rows)


def f32(*shape):
    return jax.ShapeDtypeStruct(shape, jnp.float32)


def local(right_side, inverse_blocks, couple_x, couple_y, couple_z):
    nx, ny = lax.axis_size("gx"), lax.axis_size("gy")
    outs = pl.pallas_call(
        pack_kernel,
        out_shape=[f32(4, 160, 128)] * 4,
        in_specs=[HBM] * 5,
        out_specs=[VMEM] * 4,
        scratch_shapes=[
            pltpu.VMEM((2, 8, 32, 128), jnp.float32),
            pltpu.VMEM((2, 8, 8, 128), jnp.float32),
            pltpu.VMEM((2, 8, 128, 128), jnp.float32),
            pltpu.VMEM((2, 8, 8, 128), jnp.float32),
            pltpu.VMEM((2, 8, 8, 128), jnp.float32),
            pltpu.VMEM((128, 8), jnp.float32),
            pltpu.SemaphoreType.DMA((5,)),
        ],
        compiler_params=pltpu.CompilerParams(vmem_limit_bytes=12 << 20),
        name="pack",
    )(
        *(
            pltpu.with_memory_space_constraint(source, pltpu.HBM)
            for source in (
                right_side[0],
                inverse_blocks[0],
                couple_x[0],
                couple_y[0],
                couple_z.reshape(128, 8),
            )
        )
    )

    def device(gx, gy):
        return gx * ny + gy

    owners = [(gx, gy) for gx in range(nx) for gy in range(ny) if gx % TILE_X in OWNERS]
    parts = [outs[0]]
    for r in range(1, ROUNDS):
        across, along = r // TILE_X, r % TILE_X
        pairs = [(device(gx ^ along, gy ^ across), device(gx, gy)) for gx, gy in owners]
        parts.append(lax.ppermute(outs[2 * across + along // 4], AXES, pairs))
    weights, rows = pl.pallas_call(
        prepare_kernel,
        out_shape=[
            jax.ShapeDtypeStruct((TILE_X, 2, 4, 128, 256), jnp.bfloat16),
            f32(TILE_X, 2, 4, 32, 128),
        ],
        in_specs=[VMEM] * ROUNDS,
        out_specs=[VMEM] * 2,
        compiler_params=pltpu.CompilerParams(vmem_limit_bytes=16 << 20),
        name="prepare",
    )(*parts)

    steps = nx // TILE_X + ny // 2 + 4 - 2
    tile = jnp.zeros((TILE_X, 2, 4, 8, 128), jnp.float32)
    in_x = jnp.zeros((2 * TILE_Y, 8, 128), jnp.float32)
    in_y = jnp.zeros((TILE_X, 2, 8, 128), jnp.float32)
    in_z = jnp.zeros((2, 8, 128), jnp.float32)
    for step in range(steps):

        def body(*refs, step=step):
            step_kernel(step, *refs)

        tile, out_x, out_y, out_z = pl.pallas_call(
            body,
            out_shape=[f32(*tile.shape), f32(*in_x.shape), f32(*in_y.shape), f32(*in_z.shape)],
            in_specs=[VMEM] * 6,
            out_specs=[VMEM] * 4,
            input_output_aliases={5: 0},
            compiler_params=pltpu.CompilerParams(vmem_limit_bytes=12 << 20),
            name="tile_step",
        )(weights, rows, in_x, in_y, in_z, tile)
        if step == steps - 1:
            break
        to_x, to_y, to_z = [], [], []
        for gx, gy in owners:
            if tile_level(gx, gy) % REPEAT != step % REPEAT:
                continue
            here = device(gx, gy)
            if gx + TILE_X < nx:
                to_x.append((here, device(gx + TILE_X, gy)))
            if gy + 2 < ny:
                to_y.append((here, device(gx, gy + 2)))
            if gx % TILE_X == OWNERS[0]:
                to_z.append((here, device(gx + 2, gy)))
            elif gy % 2 == 0:
                to_z.append((here, device(gx - 2, gy + 1)))
        in_x = lax.ppermute(out_x, AXES, to_x)
        in_y = lax.ppermute(out_y, AXES, to_y)
        in_z = lax.ppermute(out_z, AXES, to_z)

    groups = [
        [device(gx + i, gy + j) for i in range(TILE_X) for j in range(2)]
        for gx in range(0, nx, TILE_X)
        for gy in range(0, ny, 2)
    ]
    parts = lax.all_to_all(
        tile.reshape(ROUNDS, 4, 8, 128), AXES, 0, 0, axis_index_groups=groups, tiled=True
    )
    result = pl.pallas_call(
        unpack_kernel,
        out_shape=f32(2, 8, 8, 128),
        in_specs=[VMEM],
        out_specs=VMEM,
        name="unpack",
    )(parts)
    return result[None]


def solution(mesh):
    spec = P("gx", "gy", None, None, None)
    return jax.shard_map(
        local, mesh=mesh, in_specs=(spec,) * 5, out_specs=spec, check_vma=False
    )
```

time: 195 us -> 189 us (0.969)
  the two profiles are of different devices: /device:TPU:63 before, /device:TPU:319 now
where the time goes in v3:
time: 189 us; the launch traced here: 188 us
  blocking collectives  120 us (63%)
  starting transfers between devices  56.8 us (30%)
  Pallas kernels  6.01 us (3%)
  waiting for transfers between devices  4.14 us (2%)
    all_to_all x1, blocking collectives, local(): lax.all_to_all(tile.reshape(ROUNDS, 4, 8, 128), AXES, 0, 0, axis_index_gr...  120 us
    ppermute x15, starting transfers between devices, local(): parts.append(lax.ppermute(outs[2 * across + along // 4], AXES, pairs))  31 us
    ppermute x13, starting transfers between devices, local(): in_y = lax.ppermute(out_y, AXES, to_y)  8.64 us
    ppermute x13, starting transfers between devices, local(): in_x = lax.ppermute(out_x, AXES, to_x)  8.62 us
    ppermute x13, starting transfers between devices, local(): in_z = lax.ppermute(out_z, AXES, to_z)  8.6 us
    ppermute x15, waiting for transfers between devices, local(): parts.append(lax.ppermute(outs[2 * across + along // 4], AXES, pairs))  4.04 us
  transfers between devices with their start and end apart: 54, of which 1 were waited for; matrix products, arithmetic and copies ran while one was open for 0% of the time, Pallas kernels for 0%

profile of v3, /device:TPU:319, one launch (start us, length us, event | category | flops | bytes accessed | tf_op | source)
XLA Modules:
  0.0 188.3 jit_solution(3375208637094157216)
XLA Ops:
  0.0 2.0 %pack.1 = (f32[4,160,128]{2,1,0:T(8,128)S(1)}, f32[4,160,128]{2,1,0:T(8,128)S(1)}, f32[4,160,128]{2,1,0:T(8,128)S(1)}, f32[4,160,128]{2,1,0:T(8,128)S(1)}) custom-call(f32[2,8,8,128]{3,2,1,0:T(8,128)} %bitcast.9, f32[2,8,128,128]{3,2,1,0:T(8,128)} %bitcast.8, f32[2,8,8,128]{3,2,1,0:T(8,128)} %bitcast.10, f32[2,8,8,128]{3,2,1,0:T(8,128)} %bitcast.11, ...), custom_call_target="tpu_custom_call" | custom-call | tf_op jit(solution)/shard_map/pack/pallas_call | solution.py:170
  2.0 0.7 collective-permute-start
  2.7 0.7 collective-permute-start.1
  3.4 5.7 %collective-permute-start.10 = (f32[4,160,128]{2,1,0:T(8,128)S(1)}, f32[4,160,128]{2,1,0:T(8,128)S(1)}, u32[]{:S(2)}, u32[]{:S(2)}) collective-permute-start(f32[4,160,128]{2,1,0:T(8,128)S(1)} %get-tuple-element.66), channel_id=1, source_target_pairs={{9,16},{8,17},{11,18},{10,19},{13,20},{12,21},{15,22},{14,23},{57,... | collective-permute-start | bytes 983048 | tf_op jit(solution)/shard_map/ppermute | solution.py:207
  9.1 0.7 collective-permute-start.11
  9.8 2.8 %collective-permute-start.12 = (f32[4,160,128]{2,1,0:T(8,128)S(1)}, f32[4,160,128]{2,1,0:T(8,128)S(1)}, u32[]{:S(2)}, u32[]{:S(2)}) collective-permute-start(f32[4,160,128]{2,1,0:T(8,128)S(1)} %get-tuple-element.67), channel_id=1, source_target_pairs={{57,16},{56,17},{59,18},{58,19},{61,20},{60,21},{63,22},{62,23},{9... | collective-permute-start | bytes 983048 | tf_op jit(solution)/shard_map/ppermute | solution.py:207
  12.6 0.7 collective-permute-start.13
  13.3 0.7 collective-permute-start.14
  14.0 10.7 %collective-permute-start.2 = (f32[4,160,128]{2,1,0:T(8,128)S(1)}, f32[4,160,128]{2,1,0:T(8,128)S(1)}, u32[]{:S(2)}, u32[]{:S(2)}) collective-permute-start(f32[4,160,128]{2,1,0:T(8,128)S(1)} %get-tuple-element.64.refs_0_), channel_id=1, source_target_pairs={{8,16},{9,17},{10,18},{11,19},{12,20},{13,21},{14,22},{15,23},{56,... | collective-permute-start | bytes 983048 | tf_op jit(solution)/shard_map/ppermute | solution.py:207
  24.8 0.7 collective-permute-start.3
  25.5 4.3 %collective-permute-start.4 = (f32[4,160,128]{2,1,0:T(8,128)S(1)}, f32[4,160,128]{2,1,0:T(8,128)S(1)}, u32[]{:S(2)}, u32[]{:S(2)}) collective-permute-start(f32[4,160,128]{2,1,0:T(8,128)S(1)} %get-tuple-element.65), channel_id=1, source_target_pairs={{56,16},{57,17},{58,18},{59,19},{60,20},{61,21},{62,22},{63,23},{8... | collective-permute-start | bytes 983048 | tf_op jit(solution)/shard_map/ppermute | solution.py:207
  29.8 0.7 collective-permute-start.5
  30.5 0.7 collective-permute-start.6
  31.2 0.7 collective-permute-start.7
  31.9 0.7 collective-permute-start.8
  32.5 4.0 %collective-permute-done.4.refs_5_ = f32[4,160,128]{2,1,0:T(8,128)S(1)} collective-permute-done((f32[4,160,128]{2,1,0:T(8,128)S(1)}, f32[4,160,128]{2,1,0:T(8,128)S(1)}, u32[]{:S(2)}, u32[]{:S(2)}) %collective-permute-start.4) | collective-permute-done | bytes 327712 | tf_op jit(solution)/shard_map/ppermute | solution.py:207
  36.5 0.7 collective-permute-start.9
  37.2 0.0 collective-permute-done.5.refs_6_
  37.2 0.0 collective-permute-done.6.refs_7_
  37.3 0.7 prepare.1
  38.1 0.7 collective-permute-start.16
  38.8 0.7 collective-permute-start.15
  39.4 0.7 collective-permute-start.17
  40.2 0.7 collective-permute-start.19
  40.8 0.7 collective-permute-start.18
  41.5 0.7 collective-permute-start.20
  42.3 0.7 collective-permute-start.22
  42.9 0.7 collective-permute-start.21
  43.6 0.7 collective-permute-start.23
  44.3 0.7 collective-permute-start.25
  45.0 0.7 collective-permute-start.24
  45.7 0.7 collective-permute-start.26
  46.4 0.7 collective-permute-start.28
  47.1 0.7 collective-permute-start.27
  47.8 0.7 collective-permute-start.29
  48.5 0.2 tile_step.19
  48.7 0.7 collective-permute-start.31
  49.4 0.7 collective-permute-start.30
  50.0 0.7 collective-permute-start.32
  50.8 0.7 collective-permute-start.34
  51.5 0.7 collective-permute-start.33
  52.1 0.7 collective-permute-start.35
  52.9 0.7 collective-permute-start.37
  53.5 0.7 collective-permute-start.36
  54.2 0.7 collective-permute-start.38
  55.0 0.7 collective-permute-start.40
  55.6 0.7 collective-permute-start.39
  56.3 0.7 collective-permute-start.41
  57.0 0.7 collective-permute-start.43
  57.7 0.7 collective-permute-start.42
  58.4 0.7 collective-permute-start.44
  59.1 0.7 collective-permute-start.46
  59.8 0.7 collective-permute-start.45
  60.5 0.7 collective-permute-start.47
  61.2 0.7 collective-permute-start.49
  61.9 0.7 collective-permute-start.48
  62.6 0.7 collective-permute-start.50
  63.3 0.3 tile_step.26
  63.5 0.7 collective-permute-start.52
  64.2 0.7 collective-permute-start.51
  64.9 0.7 collective-permute-start.53
  65.6 0.7 tile_step.27
  66.2 120.3 %all_to_all.5.parts = f32[16,4,8,128]{3,2,1,0:T(8,128)} all-to-all(f32[16,4,8,128]{3,2,1,0:T(8,128)S(1)} %bitcast.7), channel_id=1, replica_groups={{0,1,8,9,16,17,24,25,32,33,40,41,48,49,56,57},{2,3,10,11,18,19,26,27,34..., dimensions={0} | all-to-all | bytes 524288 | tf_op jit(solution)/shard_map/all_to_all | solution.py:263
  186.5 1.8 unpack.1
  (66 shorter events, 0.5 us)
Async XLA Ops:
  2.0 10.6 %collective-permute-start = (f32[4,160,128]{2,1,0:T(8,128)S(1)}, f32[4,160,128]{2,1,0:T(8,128)S(1)}, u32[]{:S(2)}, u32[]{:S(2)}) collective-permute-start(f32[4,160,128]{2,1,0:T(8,128)S(1)} %get-tuple-element.64.refs_0_), channel_id=1, source_target_pairs={{24,16},{25,17},{26,18},{27,19},{28,20},{29,21},{30,22},{31,23},{4... | collective-permute-start | bytes 983048 | tf_op jit(solution)/shard_map/ppermute | solution.py:207
  2.7 10.6 %collective-permute-start.1 = (f32[4,160,128]{2,1,0:T(8,128)S(1)}, f32[4,160,128]{2,1,0:T(8,128)S(1)}, u32[]{:S(2)}, u32[]{:S(2)}) collective-permute-start(f32[4,160,128]{2,1,0:T(8,128)S(1)} %get-tuple-element.64.refs_0_), channel_id=1, source_target_pairs={{0,16},{1,17},{2,18},{3,19},{4,20},{5,21},{6,22},{7,23},{48,32},{4... | collective-permute-start | bytes 983048 | tf_op jit(solution)/shard_map/ppermute | solution.py:207
  3.4 10.6 %collective-permute-start.10 = (f32[4,160,128]{2,1,0:T(8,128)S(1)}, f32[4,160,128]{2,1,0:T(8,128)S(1)}, u32[]{:S(2)}, u32[]{:S(2)}) collective-permute-start(f32[4,160,128]{2,1,0:T(8,128)S(1)} %get-tuple-element.66), channel_id=1, source_target_pairs={{9,16},{8,17},{11,18},{10,19},{13,20},{12,21},{15,22},{14,23},{57,... | collective-permute-start | bytes 983048 | tf_op jit(solution)/shard_map/ppermute | solution.py:207
  9.1 15.7 %collective-permute-start.11 = (f32[4,160,128]{2,1,0:T(8,128)S(1)}, f32[4,160,128]{2,1,0:T(8,128)S(1)}, u32[]{:S(2)}, u32[]{:S(2)}) collective-permute-start(f32[4,160,128]{2,1,0:T(8,128)S(1)} %get-tuple-element.67), channel_id=1, source_target_pairs={{49,16},{48,17},{51,18},{50,19},{53,20},{52,21},{55,22},{54,23},{1... | collective-permute-start | bytes 983048 | tf_op jit(solution)/shard_map/ppermute | solution.py:207
  9.8 15.7 %collective-permute-start.12 = (f32[4,160,128]{2,1,0:T(8,128)S(1)}, f32[4,160,128]{2,1,0:T(8,128)S(1)}, u32[]{:S(2)}, u32[]{:S(2)}) collective-permute-start(f32[4,160,128]{2,1,0:T(8,128)S(1)} %get-tuple-element.67), channel_id=1, source_target_pairs={{57,16},{56,17},{59,18},{58,19},{61,20},{60,21},{63,22},{62,23},{9... | collective-permute-start | bytes 983048 | tf_op jit(solution)/shard_map/ppermute | solution.py:207
  12.6 17.1 %collective-permute-start.13 = (f32[4,160,128]{2,1,0:T(8,128)S(1)}, f32[4,160,128]{2,1,0:T(8,128)S(1)}, u32[]{:S(2)}, u32[]{:S(2)}) collective-permute-start(f32[4,160,128]{2,1,0:T(8,128)S(1)} %get-tuple-element.67), channel_id=1, source_target_pairs={{33,16},{32,17},{35,18},{34,19},{37,20},{36,21},{39,22},{38,23},{1... | collective-permute-start | bytes 983048 | tf_op jit(solution)/shard_map/ppermute | solution.py:207
  13.3 17.1 %collective-permute-start.14 = (f32[4,160,128]{2,1,0:T(8,128)S(1)}, f32[4,160,128]{2,1,0:T(8,128)S(1)}, u32[]{:S(2)}, u32[]{:S(2)}) collective-permute-start(f32[4,160,128]{2,1,0:T(8,128)S(1)} %get-tuple-element.67), channel_id=1, source_target_pairs={{41,16},{40,17},{43,18},{42,19},{45,20},{44,21},{47,22},{46,23},{2... | collective-permute-start | bytes 983048 | tf_op jit(solution)/shard_map/ppermute | solution.py:207
  14.0 17.1 %collective-permute-start.2 = (f32[4,160,128]{2,1,0:T(8,128)S(1)}, f32[4,160,128]{2,1,0:T(8,128)S(1)}, u32[]{:S(2)}, u32[]{:S(2)}) collective-permute-start(f32[4,160,128]{2,1,0:T(8,128)S(1)} %get-tuple-element.64.refs_0_), channel_id=1, source_target_pairs={{8,16},{9,17},{10,18},{11,19},{12,20},{13,21},{14,22},{15,23},{56,... | collective-permute-start | bytes 983048 | tf_op jit(solution)/shard_map/ppermute | solution.py:207
  24.8 7.1 %collective-permute-start.3 = (f32[4,160,128]{2,1,0:T(8,128)S(1)}, f32[4,160,128]{2,1,0:T(8,128)S(1)}, u32[]{:S(2)}, u32[]{:S(2)}) collective-permute-start(f32[4,160,128]{2,1,0:T(8,128)S(1)} %get-tuple-element.65), channel_id=1, source_target_pairs={{48,16},{49,17},{50,18},{51,19},{52,20},{53,21},{54,22},{55,23},{0... | collective-permute-start | bytes 983048 | tf_op jit(solution)/shard_map/ppermute | solution.py:207
  25.5 11.1 %collective-permute-start.4 = (f32[4,160,128]{2,1,0:T(8,128)S(1)}, f32[4,160,128]{2,1,0:T(8,128)S(1)}, u32[]{:S(2)}, u32[]{:S(2)}) collective-permute-start(f32[4,160,128]{2,1,0:T(8,128)S(1)} %get-tuple-element.65), channel_id=1, source_target_pairs={{56,16},{57,17},{58,18},{59,19},{60,20},{61,21},{62,22},{63,23},{8... | collective-permute-start | bytes 983048 | tf_op jit(solution)/shard_map/ppermute | solution.py:207
  29.8 7.5 %collective-permute-start.5 = (f32[4,160,128]{2,1,0:T(8,128)S(1)}, f32[4,160,128]{2,1,0:T(8,128)S(1)}, u32[]{:S(2)}, u32[]{:S(2)}) collective-permute-start(f32[4,160,128]{2,1,0:T(8,128)S(1)} %get-tuple-element.65), channel_id=1, source_target_pairs={{32,16},{33,17},{34,18},{35,19},{36,20},{37,21},{38,22},{39,23},{1... | collective-permute-start | bytes 983048 | tf_op jit(solution)/shard_map/ppermute | solution.py:207
  30.5 6.8 %collective-permute-start.6 = (f32[4,160,128]{2,1,0:T(8,128)S(1)}, f32[4,160,128]{2,1,0:T(8,128)S(1)}, u32[]{:S(2)}, u32[]{:S(2)}) collective-permute-start(f32[4,160,128]{2,1,0:T(8,128)S(1)} %get-tuple-element.65), channel_id=1, source_target_pairs={{40,16},{41,17},{42,18},{43,19},{44,20},{45,21},{46,22},{47,23},{2... | collective-permute-start | bytes 983048 | tf_op jit(solution)/shard_map/ppermute | solution.py:207
  31.2 6.1 %collective-permute-start.7 = (f32[4,160,128]{2,1,0:T(8,128)S(1)}, f32[4,160,128]{2,1,0:T(8,128)S(1)}, u32[]{:S(2)}, u32[]{:S(2)}) collective-permute-start(f32[4,160,128]{2,1,0:T(8,128)S(1)} %get-tuple-element.66), channel_id=1, source_target_pairs={{17,16},{16,17},{19,18},{18,19},{21,20},{20,21},{23,22},{22,23},{3... | collective-permute-start | bytes 983048 | tf_op jit(solution)/shard_map/ppermute | solution.py:207
  31.9 5.4 %collective-permute-start.8 = (f32[4,160,128]{2,1,0:T(8,128)S(1)}, f32[4,160,128]{2,1,0:T(8,128)S(1)}, u32[]{:S(2)}, u32[]{:S(2)}) collective-permute-start(f32[4,160,128]{2,1,0:T(8,128)S(1)} %get-tuple-element.66), channel_id=1, source_target_pairs={{25,16},{24,17},{27,18},{26,19},{29,20},{28,21},{31,22},{30,23},{4... | collective-permute-start | bytes 983048 | tf_op jit(solution)/shard_map/ppermute | solution.py:207
  36.5 0.7 collective-permute-start.9
  38.1 2.0 %collective-permute-start.16 = (f32[8,2,8,128]{3,2,1,0:T(8,128)S(1)}, f32[8,2,8,128]{3,2,1,0:T(8,128)S(1)}, u32[]{:S(2)}, u32[]{:S(2)}) collective-permute-start(f32[8,2,8,128]{3,2,1,0:T(8,128)S(1)} %get-tuple-element.71), channel_id=1, source_target_pairs={{16,18},{101,103},{149,151},{163,165},{211,213},{225,227},{228,230... | collective-permute-start | bytes 196616 | tf_op jit(solution)/shard_map/ppermute | solution.py:255
  38.8 1.4 collective-permute-start.15
  39.4 0.7 collective-permute-start.17
  40.2 2.0 %collective-permute-start.19 = (f32[8,2,8,128]{3,2,1,0:T(8,128)S(1)}, f32[8,2,8,128]{3,2,1,0:T(8,128)S(1)}, u32[]{:S(2)}, u32[]{:S(2)}) collective-permute-start(f32[8,2,8,128]{3,2,1,0:T(8,128)S(1)} %get-tuple-element.75), channel_id=1, source_target_pairs={{18,20},{32,34},{80,82},{165,167},{213,215},{227,229},{275,277},{2... | collective-permute-start | bytes 196616 | tf_op jit(solution)/shard_map/ppermute | solution.py:255
  40.8 1.4 collective-permute-start.18
  41.5 0.7 collective-permute-start.20
  42.3 2.0 %collective-permute-start.22 = (f32[8,2,8,128]{3,2,1,0:T(8,128)S(1)}, f32[8,2,8,128]{3,2,1,0:T(8,128)S(1)}, u32[]{:S(2)}, u32[]{:S(2)}) collective-permute-start(f32[8,2,8,128]{3,2,1,0:T(8,128)S(1)} %get-tuple-element.79), channel_id=1, source_target_pairs={{17,19},{20,22},{34,36},{82,84},{96,98},{144,146},{229,231},{277,2... | collective-permute-start | bytes 196616 | tf_op jit(solution)/shard_map/ppermute | solution.py:255
  42.9 1.4 collective-permute-start.21
  43.6 0.7 collective-permute-start.23
  44.3 2.0 %collective-permute-start.25 = (f32[8,2,8,128]{3,2,1,0:T(8,128)S(1)}, f32[8,2,8,128]{3,2,1,0:T(8,128)S(1)}, u32[]{:S(2)}, u32[]{:S(2)}) collective-permute-start(f32[8,2,8,128]{3,2,1,0:T(8,128)S(1)} %get-tuple-element.83), channel_id=1, source_target_pairs={{19,21},{33,35},{36,38},{81,83},{84,86},{98,100},{146,148},{160,16... | collective-permute-start | bytes 196616 | tf_op jit(solution)/shard_map/ppermute | solution.py:255
  45.0 1.4 collective-permute-start.24
  45.7 0.7 collective-permute-start.26
  46.4 2.0 %collective-permute-start.28 = (f32[8,2,8,128]{3,2,1,0:T(8,128)S(1)}, f32[8,2,8,128]{3,2,1,0:T(8,128)S(1)}, u32[]{:S(2)}, u32[]{:S(2)}) collective-permute-start(f32[8,2,8,128]{3,2,1,0:T(8,128)S(1)} %get-tuple-element.87), channel_id=1, source_target_pairs={{21,23},{35,37},{83,85},{97,99},{100,102},{145,147},{148,150},{162... | collective-permute-start | bytes 196616 | tf_op jit(solution)/shard_map/ppermute | solution.py:255
  47.1 1.4 collective-permute-start.27
  47.8 0.7 collective-permute-start.29
  48.7 2.0 %collective-permute-start.31 = (f32[8,2,8,128]{3,2,1,0:T(8,128)S(1)}, f32[8,2,8,128]{3,2,1,0:T(8,128)S(1)}, u32[]{:S(2)}, u32[]{:S(2)}) collective-permute-start(f32[8,2,8,128]{3,2,1,0:T(8,128)S(1)} %get-tuple-element.91), channel_id=1, source_target_pairs={{37,39},{85,87},{99,101},{147,149},{161,163},{164,166},{209,211},{... | collective-permute-start | bytes 196616 | tf_op jit(solution)/shard_map/ppermute | solution.py:255
  49.4 1.4 collective-permute-start.30
  50.0 0.7 collective-permute-start.32
  50.8 2.0 %collective-permute-start.34 = (f32[8,2,8,128]{3,2,1,0:T(8,128)S(1)}, f32[8,2,8,128]{3,2,1,0:T(8,128)S(1)}, u32[]{:S(2)}, u32[]{:S(2)}) collective-permute-start(f32[8,2,8,128]{3,2,1,0:T(8,128)S(1)} %get-tuple-element.95), channel_id=1, source_target_pairs={{16,18},{101,103},{149,151},{163,165},{211,213},{225,227},{228,230... | collective-permute-start | bytes 196616 | tf_op jit(solution)/shard_map/ppermute | solution.py:255
  51.5 1.4 collective-permute-start.33
  52.1 0.7 collective-permute-start.35
  52.9 2.0 %collective-permute-start.37 = (f32[8,2,8,128]{3,2,1,0:T(8,128)S(1)}, f32[8,2,8,128]{3,2,1,0:T(8,128)S(1)}, u32[]{:S(2)}, u32[]{:S(2)}) collective-permute-start(f32[8,2,8,128]{3,2,1,0:T(8,128)S(1)} %get-tuple-element.99), channel_id=1, source_target_pairs={{18,20},{32,34},{80,82},{165,167},{213,215},{227,229},{275,277},{2... | collective-permute-start | bytes 196616 | tf_op jit(solution)/shard_map/ppermute | solution.py:255
  53.5 1.4 collective-permute-start.36
  54.2 0.7 collective-permute-start.38
  55.0 2.0 %collective-permute-start.40 = (f32[8,2,8,128]{3,2,1,0:T(8,128)S(1)}, f32[8,2,8,128]{3,2,1,0:T(8,128)S(1)}, u32[]{:S(2)}, u32[]{:S(2)}) collective-permute-start(f32[8,2,8,128]{3,2,1,0:T(8,128)S(1)} %get-tuple-element.103), channel_id=1, source_target_pairs={{17,19},{20,22},{34,36},{82,84},{96,98},{144,146},{229,231},{277,2... | collective-permute-start | bytes 196616 | tf_op jit(solution)/shard_map/ppermute | solution.py:255
  55.6 1.4 collective-permute-start.39
  56.3 0.7 collective-permute-start.41
  57.0 2.0 %collective-permute-start.43 = (f32[8,2,8,128]{3,2,1,0:T(8,128)S(1)}, f32[8,2,8,128]{3,2,1,0:T(8,128)S(1)}, u32[]{:S(2)}, u32[]{:S(2)}) collective-permute-start(f32[8,2,8,128]{3,2,1,0:T(8,128)S(1)} %get-tuple-element.107), channel_id=1, source_target_pairs={{19,21},{33,35},{36,38},{81,83},{84,86},{98,100},{146,148},{160,16... | collective-permute-start | bytes 196616 | tf_op jit(solution)/shard_map/ppermute | solution.py:255
  57.7 1.4 collective-permute-start.42
  58.4 0.7 collective-permute-start.44
  59.1 2.0 %collective-permute-start.46 = (f32[8,2,8,128]{3,2,1,0:T(8,128)S(1)}, f32[8,2,8,128]{3,2,1,0:T(8,128)S(1)}, u32[]{:S(2)}, u32[]{:S(2)}) collective-permute-start(f32[8,2,8,128]{3,2,1,0:T(8,128)S(1)} %get-tuple-element.111), channel_id=1, source_target_pairs={{21,23},{35,37},{83,85},{97,99},{100,102},{145,147},{148,150},{162... | collective-permute-start | bytes 196616 | tf_op jit(solution)/shard_map/ppermute | solution.py:255
  59.8 1.4 collective-permute-start.45
  60.5 0.7 collective-permute-start.47
  61.2 2.0 %collective-permute-start.49 = (f32[8,2,8,128]{3,2,1,0:T(8,128)S(1)}, f32[8,2,8,128]{3,2,1,0:T(8,128)S(1)}, u32[]{:S(2)}, u32[]{:S(2)}) collective-permute-start(f32[8,2,8,128]{3,2,1,0:T(8,128)S(1)} %get-tuple-element.115), channel_id=1, source_target_pairs={{37,39},{85,87},{99,101},{147,149},{161,163},{164,166},{209,211},{... | collective-permute-start | bytes 196616 | tf_op jit(solution)/shard_map/ppermute | solution.py:255
  61.9 1.4 collective-permute-start.48
  62.6 0.7 collective-permute-start.50
  63.5 2.0 %collective-permute-start.52 = (f32[8,2,8,128]{3,2,1,0:T(8,128)S(1)}, f32[8,2,8,128]{3,2,1,0:T(8,128)S(1)}, u32[]{:S(2)}, u32[]{:S(2)}) collective-permute-start(f32[8,2,8,128]{3,2,1,0:T(8,128)S(1)} %get-tuple-element.119), channel_id=1, source_target_pairs={{16,18},{101,103},{149,151},{163,165},{211,213},{225,227},{228,230... | collective-permute-start | bytes 196616 | tf_op jit(solution)/shard_map/ppermute | solution.py:255
  64.2 1.4 collective-permute-start.51
  64.9 0.7 collective-permute-start.53

commit v4 on v3

--- a/solution.py
+++ b/solution.py
@@ -8,9 +8,10 @@
 AXES = ("gx", "gy")
 TILE_X = 8
 TILE_Y = 4
-ROUNDS = 16
+MEMBERS = 16
+ROUNDS = ((0, 0), (1, 0), (0, 1), (1, 1), (0, 2), (1, 2), (0, 3), (1, 3))
 OWNERS = (2, 4)
-REPEAT = 6
+REPEAT = 8
 VMEM = pl.BlockSpec(memory_space=pltpu.VMEM)
 HBM = pl.BlockSpec(memory_space=pltpu.HBM)
 
@@ -27,7 +28,7 @@
 
 
 def pack_kernel(*refs):
-    sources, outs, small, held, arrived = refs[:5], refs[5:9], refs[9], refs[10:15], refs[15]
+    sources, outs, small, held, arrived = refs[:5], refs[5:8], refs[8], refs[9:14], refs[14]
     copies = [
         pltpu.make_async_copy(source, target, arrived.at[i])
         for i, (source, target) in enumerate(zip(sources, held))
@@ -37,7 +38,9 @@
     for copy in copies:
         copy.wait()
     rhs, inverse, cx, cy, cz = held
-    right = lax.rem(lax.axis_index("gx"), TILE_X) // 4
+    gx = lax.axis_index("gx")
+    core = lax.rem(gx, 2)
+    pair = (lax.rem(gx, TILE_X) // 4) ^ lax.rem(gx // TILE_X, 2)
     upper = lax.rem(lax.axis_index("gy"), 2)
     row = lax.broadcasted_iota(jnp.int32, (8, 128), 0)
     group = lax.broadcasted_iota(jnp.int32, (8, 128), 1) // 16
@@ -63,38 +66,42 @@
             for d in range(1, 8):
                 out = jnp.where(group == d, pltpu.roll(t, 8 - d, 0), out)
             small[y, s, 24:32, :] = out
-    for q in range(4):
-        first = 4 * (upper ^ (q // 2)) + 2 * (right ^ (q % 2))
-        for y in range(2):
-            for k in range(2):
-                outs[q][y * 2 + k, 0:128, :] = inverse[y, first + k].T
-                outs[q][y * 2 + k, 128:160, :] = small[y, first + k]
+    for across in range(2):
+        for given in range(2):
+            out = outs[2].at[across] if given else outs[across]
+            first = 4 * (upper ^ across) + 2 * (pair ^ core ^ given)
+            for y in range(2):
+                for k in range(2):
+                    out[y * 2 + k, 0:128, :] = inverse[y, first + k].T
+                    out[y * 2 + k, 128:160, :] = small[y, first + k]
 
 
 def prepare_kernel(*refs):
-    parts, weights, rows = refs[:ROUNDS], refs[ROUNDS], refs[ROUNDS + 1]
-    place = lax.rem(lax.axis_index("gx"), TILE_X)
+    parts, (weights, rows) = refs[: len(ROUNDS)], refs[len(ROUNDS) :]
+    chip = lax.rem(lax.axis_index("gx"), TILE_X) // 2
     upper = lax.rem(lax.axis_index("gy"), 2)
-    for r in range(ROUNDS):
-        x, half = place ^ (r % TILE_X), upper ^ (r // TILE_X)
-        for b in range(4):
-            full = parts[r][b, 0:128, :]
-            high = full.astype(jnp.bfloat16)
-            low = (full - high.astype(jnp.float32)).astype(jnp.bfloat16)
-            weights[x, half, b, :, 0:128] = high
-            weights[x, half, b, :, 128:256] = low
-            rows[x, half, b] = parts[r][b, 128:160, :]
+    for part, (across, along) in zip(parts, ROUNDS):
+        for i in range(2):
+            x, half = 2 * (chip ^ along) + (i ^ (along // 2)), upper ^ across
+            for b in range(4):
+                full = part[i, b, 0:128, :]
+                high = full.astype(jnp.bfloat16)
+                low = (full - high.astype(jnp.float32)).astype(jnp.bfloat16)
+                weights[x, half, b, :, 0:128] = high
+                weights[x, half, b, :, 128:256] = low
+                rows[x, half, b] = part[i, b, 128:160, :]
 
 
 def tile_level(gx, gy):
-    return gx // TILE_X + gy // 2 + 2 * (gy % 2) + (gx % TILE_X) // 4
+    return gx // TILE_X + gy // 2 + 2 * (gy % 2) + ((gx % TILE_X) // 4 ^ (gx // TILE_X % 2))
 
 
 def step_kernel(step, weights, rows, in_x, in_y, in_z, _, tile, out_x, out_y, out_z):
     gx, gy = lax.axis_index("gx"), lax.axis_index("gy")
     place = lax.rem(gx, TILE_X)
     owner = (place == OWNERS[0]) | (place == OWNERS[1])
-    level = gx // TILE_X + gy // 2 + 2 * lax.rem(gy, 2) + place // 4
+    pair = (place // 4) ^ lax.rem(gx // TILE_X, 2)
+    level = gx // TILE_X + gy // 2 + 2 * lax.rem(gy, 2) + pair
     last_lane = lax.rem(lax.broadcasted_iota(jnp.int32, (8, 128), 1), 16) == 15
 
     @pl.when(owner & (level == step))
@@ -149,11 +156,13 @@
 
 
 def unpack_kernel(parts, out):
+    odd = lax.rem(lax.axis_index("gx") // TILE_X, 2)
+    senders = [2 * (OWNERS[0] + 2 * (odd ^ (s % 2))) + s // 2 for s in range(4)]
     for y in range(2):
         for n in range(8):
             rows = jnp.concatenate(
                 [
-                    parts[2 * OWNERS[s // 2 % 2] + s // 4, y * 2 + s % 2, n : n + 1, :]
+                    parts[senders[s // 2], y * 2 + s % 2, n : n + 1, :]
                     for s in range(8)
                 ],
                 axis=0,
@@ -169,9 +178,9 @@
     nx, ny = lax.axis_size("gx"), lax.axis_size("gy")
     outs = pl.pallas_call(
         pack_kernel,
-        out_shape=[f32(4, 160, 128)] * 4,
+        out_shape=[f32(4, 160, 128)] * 2 + [f32(2, 4, 160, 128)],
         in_specs=[HBM] * 5,
-        out_specs=[VMEM] * 4,
+        out_specs=[VMEM] * 3,
         scratch_shapes=[
             pltpu.VMEM((2, 8, 32, 128), jnp.float32),
             pltpu.VMEM((2, 8, 8, 128), jnp.float32),
@@ -200,18 +209,24 @@
         return gx * ny + gy
 
     owners = [(gx, gy) for gx in range(nx) for gy in range(ny) if gx % TILE_X in OWNERS]
-    parts = [outs[0]]
-    for r in range(1, ROUNDS):
-        across, along = r // TILE_X, r % TILE_X
-        pairs = [(device(gx ^ along, gy ^ across), device(gx, gy)) for gx, gy in owners]
-        parts.append(lax.ppermute(outs[2 * across + along // 4], AXES, pairs))
+    everyone = [(gx, gy) for gx in range(nx) for gy in range(ny)]
+    swap = [(device(gx, gy), device(gx ^ 1, gy)) for gx, gy in everyone]
+    got = lax.ppermute(outs[2], AXES, swap)
+    messages = [jnp.stack([outs[i], got[i]]) for i in range(2)]
+    parts = [messages[0]]
+    for across, along in ROUNDS[1:]:
+        pairs = [
+            (device((gx ^ 2 * along) + along // 2, gy ^ across), device(gx, gy))
+            for gx, gy in owners
+        ]
+        parts.append(lax.ppermute(messages[across], AXES, pairs))
     weights, rows = pl.pallas_call(
         prepare_kernel,
         out_shape=[
             jax.ShapeDtypeStruct((TILE_X, 2, 4, 128, 256), jnp.bfloat16),
             f32(TILE_X, 2, 4, 32, 128),
         ],
-        in_specs=[VMEM] * ROUNDS,
+        in_specs=[VMEM] * len(ROUNDS),
         out_specs=[VMEM] * 2,
         compiler_params=pltpu.CompilerParams(vmem_limit_bytes=16 << 20),
         name="prepare",
@@ -243,14 +258,15 @@
             if tile_level(gx, gy) % REPEAT != step % REPEAT:
                 continue
             here = device(gx, gy)
+            other = gx // TILE_X * TILE_X + sum(OWNERS) - gx % TILE_X
             if gx + TILE_X < nx:
-                to_x.append((here, device(gx + TILE_X, gy)))
+                to_x.append((here, device(other + TILE_X, gy)))
             if gy + 2 < ny:
                 to_y.append((here, device(gx, gy + 2)))
-            if gx % TILE_X == OWNERS[0]:
-                to_z.append((here, device(gx + 2, gy)))
+            if (gx % TILE_X == OWNERS[0]) == (gx // TILE_X % 2 == 0):
+                to_z.append((here, device(other, gy)))
             elif gy % 2 == 0:
-                to_z.append((here, device(gx - 2, gy + 1)))
+                to_z.append((here, device(other, gy + 1)))
         in_x = lax.ppermute(out_x, AXES, to_x)
         in_y = lax.ppermute(out_y, AXES, to_y)
         in_z = lax.ppermute(out_z, AXES, to_z)
@@ -261,7 +277,7 @@
         for gy in range(0, ny, 2)
     ]
     parts = lax.all_to_all(
-        tile.reshape(ROUNDS, 4, 8, 128), AXES, 0, 0, axis_index_groups=groups, tiled=True
+        tile.reshape(MEMBERS, 4, 8, 128), AXES, 0, 0, axis_index_groups=groups, tiled=True
     )
     result = pl.pallas_call(
         unpack_kernel,

time: 189 us -> 185 us (0.979)
  the two profiles are of different devices: /device:TPU:319 before, /device:TPU:63 now
where the time goes in v4:
time: 185 us; the launch traced here: 184 us
  blocking collectives  107 us (58%)
  starting transfers between devices  50.2 us (27%)
  waiting for transfers between devices  19.4 us (10%)
  Pallas kernels  6.03 us (3%)
    all_to_all x1, blocking collectives, local(): lax.all_to_all(tile.reshape(MEMBERS, 4, 8, 128), AXES, 0, 0, axis_index_g...  107 us
    ppermute x7, starting transfers between devices, local(): parts.append(lax.ppermute(messages[across], AXES, pairs))  21.7 us
    ppermute x7, waiting for transfers between devices, local(): parts.append(lax.ppermute(messages[across], AXES, pairs))  17.6 us
    ppermute x13, starting transfers between devices, local(): in_y = lax.ppermute(out_y, AXES, to_y)  8.64 us
    ppermute x13, starting transfers between devices, local(): in_x = lax.ppermute(out_x, AXES, to_x)  8.62 us
    ppermute x13, starting transfers between devices, local(): in_z = lax.ppermute(out_z, AXES, to_z)  8.6 us
  transfers between devices with their start and end apart: 47, of which 3 were waited for; matrix products, arithmetic and copies ran while one was open for 0% of the time, Pallas kernels for 0%

profile of v4, /device:TPU:63, one launch (start us, length us, event | category | flops | bytes accessed | tf_op | source)
XLA Modules:
  0.0 184.1 jit_solution(1141195387324518507)
XLA Ops:
  0.0 2.0 %pack.1 = (f32[4,160,128]{2,1,0:T(8,128)S(1)}, f32[4,160,128]{2,1,0:T(8,128)S(1)}, f32[2,4,160,128]{3,2,1,0:T(8,128)S(1)}) custom-call(f32[2,8,8,128]{3,2,1,0:T(8,128)} %bitcast.13, f32[2,8,128,128]{3,2,1,0:T(8,128)} %bitcast.12, f32[2,8,8,128]{3,2,1,0:T(8,128)} %bitcast.14, f32[2,8,8,128]{3,2,1,0:T(8,128)} %bitcast.15, f32[128,8]{1,0:T(8,128)} %bitcast.16), custom_call_target="tpu_custom_call" | custom-call | tf_op jit(solution)/shard_map/pack/pallas_call | solution.py:179
  2.0 2.6 %collective-permute-start = (f32[2,4,160,128]{3,2,1,0:T(8,128)S(1)}, f32[2,4,160,128]{3,2,1,0:T(8,128)S(1)}, u32[]{:S(2)}, u32[]{:S(2)}) collective-permute-start(f32[2,4,160,128]{3,2,1,0:T(8,128)S(1)} %get-tuple-element.64), channel_id=1, source_target_pairs={{0,8},{1,9},{2,10},{3,11},{4,12},{5,13},{6,14},{7,15},{8,0},{9,1},... | collective-permute-start | bytes 1966088 | tf_op jit(solution)/shard_map/ppermute | solution.py:214
  4.6 1.7 collective-permute-done
  6.4 0.7 collective-permute-start.1
  7.1 0.7 collective-permute-start.3
  7.9 9.4 %collective-permute-start.5 = (f32[2,4,160,128]{3,2,1,0:T(8,128)S(1)}, f32[2,4,160,128]{3,2,1,0:T(8,128)S(1)}, u32[]{:S(2)}, u32[]{:S(2)}) collective-permute-start(f32[2,4,160,128]{3,2,1,0:T(8,128)S(1)} %pad_maximum_fusion.1), channel_id=1, source_target_pairs={{57,16},{56,17},{59,18},{58,19},{61,20},{60,21},{63,22},{62,23},{9... | collective-permute-start | bytes 1966088 | tf_op jit(solution)/shard_map/ppermute | solution.py:222
  17.2 0.7 collective-permute-start.7
  18.0 0.7 collective-permute-start.2
  18.7 8.9 %collective-permute-start.4 = (f32[2,4,160,128]{3,2,1,0:T(8,128)S(1)}, f32[2,4,160,128]{3,2,1,0:T(8,128)S(1)}, u32[]{:S(2)}, u32[]{:S(2)}) collective-permute-start(f32[2,4,160,128]{3,2,1,0:T(8,128)S(1)} %pad_maximum_fusion.refs_0_), channel_id=1, source_target_pairs={{56,16},{57,17},{58,18},{59,19},{60,20},{61,21},{62,22},{63,23},{8... | collective-permute-start | bytes 1966088 | tf_op jit(solution)/shard_map/ppermute | solution.py:222
  27.6 0.7 collective-permute-start.6
  28.3 2.3 %collective-permute-done.5.refs_5_ = f32[2,4,160,128]{3,2,1,0:T(8,128)S(1)} collective-permute-done((f32[2,4,160,128]{3,2,1,0:T(8,128)S(1)}, f32[2,4,160,128]{3,2,1,0:T(8,128)S(1)}, u32[]{:S(2)}, u32[]{:S(2)}) %collective-permute-start.5) | collective-permute-done | bytes 655392 | tf_op jit(solution)/shard_map/ppermute | solution.py:222
  30.6 0.0 collective-permute-done.2.refs_2_
  30.6 15.3 %collective-permute-done.4.refs_4_ = f32[2,4,160,128]{3,2,1,0:T(8,128)S(1)} collective-permute-done((f32[2,4,160,128]{3,2,1,0:T(8,128)S(1)}, f32[2,4,160,128]{3,2,1,0:T(8,128)S(1)}, u32[]{:S(2)}, u32[]{:S(2)}) %collective-permute-start.4) | collective-permute-done | bytes 655392 | tf_op jit(solution)/shard_map/ppermute | solution.py:222
  45.9 0.0 collective-permute-done.6.refs_6_
  45.9 0.7 prepare.1
  46.7 0.7 collective-permute-start.9
  47.4 0.7 collective-permute-start.8
  48.0 0.7 collective-permute-start.10
  48.7 0.0 collective-permute-done.8.refs_2_
  48.7 0.0 collective-permute-done.9.refs_3_
  48.8 0.7 collective-permute-start.12
  49.5 0.7 collective-permute-start.11
  50.1 0.7 collective-permute-start.13
  50.8 0.0 collective-permute-done.13.refs_4_
  50.8 0.0 collective-permute-done.11.refs_2_
  50.9 0.7 collective-permute-start.15
  51.5 0.7 collective-permute-start.14
  52.2 0.7 collective-permute-start.16
  52.9 0.0 collective-permute-done.16.refs_4_
  53.0 0.7 collective-permute-start.18
  53.6 0.7 collective-permute-start.17
  54.3 0.7 collective-permute-start.19
  55.0 0.7 collective-permute-start.21
  55.7 0.7 collective-permute-start.20
  56.4 0.7 collective-permute-start.22
  57.1 0.2 tile_step.19
  57.3 0.7 collective-permute-start.24
  58.0 0.7 collective-permute-start.23
  58.7 0.7 collective-permute-start.25
  59.4 0.7 collective-permute-start.27
  60.1 0.7 collective-permute-start.26
  60.7 0.7 collective-permute-start.28
  61.5 0.7 collective-permute-start.30
  62.2 0.7 collective-permute-start.29
  62.8 0.7 collective-permute-start.31
  63.6 0.7 collective-permute-start.33
  64.3 0.7 collective-permute-start.32
  64.9 0.7 collective-permute-start.34
  65.7 0.7 collective-permute-start.36
  66.3 0.7 collective-permute-start.35
  67.0 0.7 collective-permute-start.37
  67.8 0.7 collective-permute-start.39
  68.4 0.7 collective-permute-start.38
  69.1 0.7 collective-permute-start.40
  69.8 0.7 collective-permute-start.42
  70.5 0.7 collective-permute-start.41
  71.2 0.7 collective-permute-start.43
  71.9 0.3 tile_step.26
  72.1 0.7 collective-permute-start.45
  72.8 0.7 collective-permute-start.44
  73.5 0.7 collective-permute-start.46
  74.2 0.7 tile_step.27
  74.9 107.5 %all_to_all.5.parts = f32[16,4,8,128]{3,2,1,0:T(8,128)} all-to-all(f32[16,4,8,128]{3,2,1,0:T(8,128)S(1)} %bitcast.9), channel_id=1, replica_groups={{0,1,8,9,16,17,24,25,32,33,40,41,48,49,56,57},{2,3,10,11,18,19,26,27,34..., dimensions={0} | all-to-all | bytes 524288 | tf_op jit(solution)/shard_map/all_to_all | solution.py:279
  182.3 1.8 unpack.1
  (55 shorter events, 0.6 us)
Async XLA Ops:
  2.0 4.3 %collective-permute-start = (f32[2,4,160,128]{3,2,1,0:T(8,128)S(1)}, f32[2,4,160,128]{3,2,1,0:T(8,128)S(1)}, u32[]{:S(2)}, u32[]{:S(2)}) collective-permute-start(f32[2,4,160,128]{3,2,1,0:T(8,128)S(1)} %get-tuple-element.64), channel_id=1, source_target_pairs={{0,8},{1,9},{2,10},{3,11},{4,12},{5,13},{6,14},{7,15},{8,0},{9,1},... | collective-permute-start | bytes 1966088 | tf_op jit(solution)/shard_map/ppermute | solution.py:214
  6.4 12.3 %collective-permute-start.1 = (f32[2,4,160,128]{3,2,1,0:T(8,128)S(1)}, f32[2,4,160,128]{3,2,1,0:T(8,128)S(1)}, u32[]{:S(2)}, u32[]{:S(2)}) collective-permute-start(f32[2,4,160,128]{3,2,1,0:T(8,128)S(1)} %pad_maximum_fusion.1), channel_id=1, source_target_pairs={{17,16},{16,17},{19,18},{18,19},{21,20},{20,21},{23,22},{22,23},{3... | collective-permute-start | bytes 1966088 | tf_op jit(solution)/shard_map/ppermute | solution.py:222
  7.1 20.4 %collective-permute-start.3 = (f32[2,4,160,128]{3,2,1,0:T(8,128)S(1)}, f32[2,4,160,128]{3,2,1,0:T(8,128)S(1)}, u32[]{:S(2)}, u32[]{:S(2)}) collective-permute-start(f32[2,4,160,128]{3,2,1,0:T(8,128)S(1)} %pad_maximum_fusion.1), channel_id=1, source_target_pairs={{1,16},{0,17},{3,18},{2,19},{5,20},{4,21},{7,22},{6,23},{49,32},{4... | collective-permute-start | bytes 1966088 | tf_op jit(solution)/shard_map/ppermute | solution.py:222
  7.9 22.8 %collective-permute-start.5 = (f32[2,4,160,128]{3,2,1,0:T(8,128)S(1)}, f32[2,4,160,128]{3,2,1,0:T(8,128)S(1)}, u32[]{:S(2)}, u32[]{:S(2)}) collective-permute-start(f32[2,4,160,128]{3,2,1,0:T(8,128)S(1)} %pad_maximum_fusion.1), channel_id=1, source_target_pairs={{57,16},{56,17},{59,18},{58,19},{61,20},{60,21},{63,22},{62,23},{9... | collective-permute-start | bytes 1966088 | tf_op jit(solution)/shard_map/ppermute | solution.py:222
  17.2 13.4 %collective-permute-start.7 = (f32[2,4,160,128]{3,2,1,0:T(8,128)S(1)}, f32[2,4,160,128]{3,2,1,0:T(8,128)S(1)}, u32[]{:S(2)}, u32[]{:S(2)}) collective-permute-start(f32[2,4,160,128]{3,2,1,0:T(8,128)S(1)} %pad_maximum_fusion.1), channel_id=1, source_target_pairs={{41,16},{40,17},{43,18},{42,19},{45,20},{44,21},{47,22},{46,23},{2... | collective-permute-start | bytes 1966088 | tf_op jit(solution)/shard_map/ppermute | solution.py:222
  18.0 12.6 %collective-permute-start.2 = (f32[2,4,160,128]{3,2,1,0:T(8,128)S(1)}, f32[2,4,160,128]{3,2,1,0:T(8,128)S(1)}, u32[]{:S(2)}, u32[]{:S(2)}) collective-permute-start(f32[2,4,160,128]{3,2,1,0:T(8,128)S(1)} %pad_maximum_fusion.refs_0_), channel_id=1, source_target_pairs={{0,16},{1,17},{2,18},{3,19},{4,20},{5,21},{6,22},{7,23},{48,32},{4... | collective-permute-start | bytes 1966088 | tf_op jit(solution)/shard_map/ppermute | solution.py:222
  18.7 27.2 %collective-permute-start.4 = (f32[2,4,160,128]{3,2,1,0:T(8,128)S(1)}, f32[2,4,160,128]{3,2,1,0:T(8,128)S(1)}, u32[]{:S(2)}, u32[]{:S(2)}) collective-permute-start(f32[2,4,160,128]{3,2,1,0:T(8,128)S(1)} %pad_maximum_fusion.refs_0_), channel_id=1, source_target_pairs={{56,16},{57,17},{58,18},{59,19},{60,20},{61,21},{62,22},{63,23},{8... | collective-permute-start | bytes 1966088 | tf_op jit(solution)/shard_map/ppermute | solution.py:222
  27.6 18.3 %collective-permute-start.6 = (f32[2,4,160,128]{3,2,1,0:T(8,128)S(1)}, f32[2,4,160,128]{3,2,1,0:T(8,128)S(1)}, u32[]{:S(2)}, u32[]{:S(2)}) collective-permute-start(f32[2,4,160,128]{3,2,1,0:T(8,128)S(1)} %pad_maximum_fusion.refs_0_), channel_id=1, source_target_pairs={{40,16},{41,17},{42,18},{43,19},{44,20},{45,21},{46,22},{47,23},{2... | collective-permute-start | bytes 1966088 | tf_op jit(solution)/shard_map/ppermute | solution.py:222
  46.7 2.0 %collective-permute-start.9 = (f32[8,2,8,128]{3,2,1,0:T(8,128)S(1)}, f32[8,2,8,128]{3,2,1,0:T(8,128)S(1)}, u32[]{:S(2)}, u32[]{:S(2)}) collective-permute-start(f32[8,2,8,128]{3,2,1,0:T(8,128)S(1)} %get-tuple-element.69), channel_id=1, source_target_pairs={{16,18},{213,215},{277,279},{291,293},{337,339},{340,342},{355,357... | collective-permute-start | bytes 196616 | tf_op jit(solution)/shard_map/ppermute | solution.py:271
  47.4 1.4 collective-permute-start.8
  48.0 0.7 collective-permute-start.10
  48.8 2.0 %collective-permute-start.12 = (f32[8,2,8,128]{3,2,1,0:T(8,128)S(1)}, f32[8,2,8,128]{3,2,1,0:T(8,128)S(1)}, u32[]{:S(2)}, u32[]{:S(2)}) collective-permute-start(f32[8,2,8,128]{3,2,1,0:T(8,128)S(1)} %get-tuple-element.73), channel_id=1, source_target_pairs={{18,20},{32,34},{96,98},{293,295},{339,341},{357,359},{403,405},{4... | collective-permute-start | bytes 196616 | tf_op jit(solution)/shard_map/ppermute | solution.py:271
  49.5 1.4 collective-permute-start.11
  50.1 0.7 collective-permute-start.13
  50.9 2.0 %collective-permute-start.15 = (f32[8,2,8,128]{3,2,1,0:T(8,128)S(1)}, f32[8,2,8,128]{3,2,1,0:T(8,128)S(1)}, u32[]{:S(2)}, u32[]{:S(2)}) collective-permute-start(f32[8,2,8,128]{3,2,1,0:T(8,128)S(1)} %get-tuple-element.77), channel_id=1, source_target_pairs={{17,19},{20,22},{34,36},{80,82},{98,100},{144,146},{341,343},{405,... | collective-permute-start | bytes 196616 | tf_op jit(solution)/shard_map/ppermute | solution.py:271
  51.5 1.4 collective-permute-start.14
  52.2 0.7 collective-permute-start.16
  53.0 2.0 %collective-permute-start.18 = (f32[8,2,8,128]{3,2,1,0:T(8,128)S(1)}, f32[8,2,8,128]{3,2,1,0:T(8,128)S(1)}, u32[]{:S(2)}, u32[]{:S(2)}) collective-permute-start(f32[8,2,8,128]{3,2,1,0:T(8,128)S(1)} %get-tuple-element.81), channel_id=1, source_target_pairs={{19,21},{33,35},{36,38},{82,84},{97,99},{100,102},{146,148},{160,1... | collective-permute-start | bytes 196616 | tf_op jit(solution)/shard_map/ppermute | solution.py:271
  53.6 1.4 collective-permute-start.17
  54.3 0.7 collective-permute-start.19
  55.0 2.0 %collective-permute-start.21 = (f32[8,2,8,128]{3,2,1,0:T(8,128)S(1)}, f32[8,2,8,128]{3,2,1,0:T(8,128)S(1)}, u32[]{:S(2)}, u32[]{:S(2)}) collective-permute-start(f32[8,2,8,128]{3,2,1,0:T(8,128)S(1)} %get-tuple-element.85), channel_id=1, source_target_pairs={{21,23},{35,37},{81,83},{84,86},{99,101},{145,147},{148,150},{162,... | collective-permute-start | bytes 196616 | tf_op jit(solution)/shard_map/ppermute | solution.py:271
  55.7 1.4 collective-permute-start.20
  56.4 0.7 collective-permute-start.22
  57.3 2.0 %collective-permute-start.24 = (f32[8,2,8,128]{3,2,1,0:T(8,128)S(1)}, f32[8,2,8,128]{3,2,1,0:T(8,128)S(1)}, u32[]{:S(2)}, u32[]{:S(2)}) collective-permute-start(f32[8,2,8,128]{3,2,1,0:T(8,128)S(1)} %get-tuple-element.89), channel_id=1, source_target_pairs={{37,39},{83,85},{101,103},{147,149},{161,163},{164,166},{210,212},... | collective-permute-start | bytes 196616 | tf_op jit(solution)/shard_map/ppermute | solution.py:271
  58.0 1.4 collective-permute-start.23
  58.7 0.7 collective-permute-start.25
  59.4 2.0 %collective-permute-start.27 = (f32[8,2,8,128]{3,2,1,0:T(8,128)S(1)}, f32[8,2,8,128]{3,2,1,0:T(8,128)S(1)}, u32[]{:S(2)}, u32[]{:S(2)}) collective-permute-start(f32[8,2,8,128]{3,2,1,0:T(8,128)S(1)} %get-tuple-element.93), channel_id=1, source_target_pairs={{85,87},{149,151},{163,165},{209,211},{212,214},{227,229},{273,275... | collective-permute-start | bytes 196616 | tf_op jit(solution)/shard_map/ppermute | solution.py:271
  60.1 1.4 collective-permute-start.26
  60.7 0.7 collective-permute-start.28
  61.5 2.0 %collective-permute-start.30 = (f32[8,2,8,128]{3,2,1,0:T(8,128)S(1)}, f32[8,2,8,128]{3,2,1,0:T(8,128)S(1)}, u32[]{:S(2)}, u32[]{:S(2)}) collective-permute-start(f32[8,2,8,128]{3,2,1,0:T(8,128)S(1)} %get-tuple-element.97), channel_id=1, source_target_pairs={{165,167},{211,213},{229,231},{275,277},{289,291},{292,294},{338,3... | collective-permute-start | bytes 196616 | tf_op jit(solution)/shard_map/ppermute | solution.py:271
  62.2 1.4 collective-permute-start.29
  62.8 0.7 collective-permute-start.31
  63.6 2.0 %collective-permute-start.33 = (f32[8,2,8,128]{3,2,1,0:T(8,128)S(1)}, f32[8,2,8,128]{3,2,1,0:T(8,128)S(1)}, u32[]{:S(2)}, u32[]{:S(2)}) collective-permute-start(f32[8,2,8,128]{3,2,1,0:T(8,128)S(1)} %get-tuple-element.101), channel_id=1, source_target_pairs={{16,18},{213,215},{277,279},{291,293},{337,339},{340,342},{355,357... | collective-permute-start | bytes 196616 | tf_op jit(solution)/shard_map/ppermute | solution.py:271
  64.3 1.4 collective-permute-start.32
  64.9 0.7 collective-permute-start.34
  65.7 2.0 %collective-permute-start.36 = (f32[8,2,8,128]{3,2,1,0:T(8,128)S(1)}, f32[8,2,8,128]{3,2,1,0:T(8,128)S(1)}, u32[]{:S(2)}, u32[]{:S(2)}) collective-permute-start(f32[8,2,8,128]{3,2,1,0:T(8,128)S(1)} %get-tuple-element.105), channel_id=1, source_target_pairs={{18,20},{32,34},{96,98},{293,295},{339,341},{357,359},{403,405},{4... | collective-permute-start | bytes 196616 | tf_op jit(solution)/shard_map/ppermute | solution.py:271
  66.3 1.4 collective-permute-start.35
  67.0 0.7 collective-permute-start.37
  67.8 2.0 %collective-permute-start.39 = (f32[8,2,8,128]{3,2,1,0:T(8,128)S(1)}, f32[8,2,8,128]{3,2,1,0:T(8,128)S(1)}, u32[]{:S(2)}, u32[]{:S(2)}) collective-permute-start(f32[8,2,8,128]{3,2,1,0:T(8,128)S(1)} %get-tuple-element.109), channel_id=1, source_target_pairs={{17,19},{20,22},{34,36},{80,82},{98,100},{144,146},{341,343},{405,... | collective-permute-start | bytes 196616 | tf_op jit(solution)/shard_map/ppermute | solution.py:271
  68.4 1.4 collective-permute-start.38
  69.1 0.7 collective-permute-start.40
  69.8 2.0 %collective-permute-start.42 = (f32[8,2,8,128]{3,2,1,0:T(8,128)S(1)}, f32[8,2,8,128]{3,2,1,0:T(8,128)S(1)}, u32[]{:S(2)}, u32[]{:S(2)}) collective-permute-start(f32[8,2,8,128]{3,2,1,0:T(8,128)S(1)} %get-tuple-element.113), channel_id=1, source_target_pairs={{19,21},{33,35},{36,38},{82,84},{97,99},{100,102},{146,148},{160,1... | collective-permute-start | bytes 196616 | tf_op jit(solution)/shard_map/ppermute | solution.py:271
  70.5 1.4 collective-permute-start.41
  71.2 0.7 collective-permute-start.43
  72.1 2.0 %collective-permute-start.45 = (f32[8,2,8,128]{3,2,1,0:T(8,128)S(1)}, f32[8,2,8,128]{3,2,1,0:T(8,128)S(1)}, u32[]{:S(2)}, u32[]{:S(2)}) collective-permute-start(f32[8,2,8,128]{3,2,1,0:T(8,128)S(1)} %get-tuple-element.117), channel_id=1, source_target_pairs={{21,23},{35,37},{81,83},{84,86},{99,101},{145,147},{148,150},{162,... | collective-permute-start | bytes 196616 | tf_op jit(solution)/shard_map/ppermute | solution.py:271
  72.8 1.4 collective-permute-start.44
  73.5 0.7 collective-permute-start.46

commit v5 on v4

--- a/solution.py
+++ b/solution.py
@@ -9,7 +9,8 @@
 TILE_X = 8
 TILE_Y = 4
 MEMBERS = 16
-ROUNDS = ((0, 0), (1, 0), (0, 1), (1, 1), (0, 2), (1, 2), (0, 3), (1, 3))
+ROUNDS = ((0, 0), (1, 0), (1, 1), (1, 2), (1, 3), (0, 2), (0, 3), (0, 1))
+SENT_X = 17
 OWNERS = (2, 4)
 REPEAT = 8
 VMEM = pl.BlockSpec(memory_space=pltpu.VMEM)
@@ -155,19 +156,15 @@
             out_z[h] = z_out[h]
 
 
-def unpack_kernel(parts, out):
+def unpack_kernel(parts, out, blocks):
     odd = lax.rem(lax.axis_index("gx") // TILE_X, 2)
     senders = [2 * (OWNERS[0] + 2 * (odd ^ (s % 2))) + s // 2 for s in range(4)]
     for y in range(2):
+        for s in range(8):
+            blocks[y, s] = parts[senders[s // 2], y * 2 + s % 2]
+    for y in range(2):
         for n in range(8):
-            rows = jnp.concatenate(
-                [
-                    parts[senders[s // 2], y * 2 + s % 2, n : n + 1, :]
-                    for s in range(8)
-                ],
-                axis=0,
-            )
-            out[y, n] = swap_groups(rows)
+            out[y, n] = swap_groups(blocks[y, :, n, :])
 
 
 def f32(*shape):
@@ -234,7 +231,7 @@
 
     steps = nx // TILE_X + ny // 2 + 4 - 2
     tile = jnp.zeros((TILE_X, 2, 4, 8, 128), jnp.float32)
-    in_x = jnp.zeros((2 * TILE_Y, 8, 128), jnp.float32)
+    in_x = jnp.zeros((SENT_X, 8, 128), jnp.float32)
     in_y = jnp.zeros((TILE_X, 2, 8, 128), jnp.float32)
     in_z = jnp.zeros((2, 8, 128), jnp.float32)
     for step in range(steps):
@@ -284,6 +281,7 @@
         out_shape=f32(2, 8, 8, 128),
         in_specs=[VMEM],
         out_specs=VMEM,
+        scratch_shapes=[pltpu.VMEM((2, 8, 8, 128), jnp.float32)],
         name="unpack",
     )(parts)
     return result[None]

time: 185 us -> 183 us (0.989)
  waiting for transfers between devices: 19.4 us -> 26.7 us
  starting transfers between devices: 50.2 us -> 43.1 us
  blocking collectives: 107 us -> 105 us
    ppermute x7, waiting for transfers between devices: 17.6 us -> 24.9 us  [local(): parts.append(lax.ppermute(messages[across], AXES, pairs))]
    ppermute x7, starting transfers between devices: 21.7 us -> 14.6 us  [local(): parts.append(lax.ppermute(messages[across], AXES, pairs))]
    all_to_all x1, blocking collectives: 107 us -> 105 us  [local(): lax.all_to_all(tile.reshape(MEMBERS, 4, 8, 128), AXES, 0, 0, axis_index_g...]
where the time goes in v5:
time: 183 us; the launch traced here: 182 us
  blocking collectives  105 us (57%)
  starting transfers between devices  43.1 us (24%)
  waiting for transfers between devices  26.7 us (15%)
  Pallas kernels  6.05 us (3%)
    all_to_all x1, blocking collectives, local(): lax.all_to_all(tile.reshape(MEMBERS, 4, 8, 128), AXES, 0, 0, axis_index_g...  105 us
    ppermute x7, waiting for transfers between devices, local(): parts.append(lax.ppermute(messages[across], AXES, pairs))  24.9 us
    ppermute x7, starting transfers between devices, local(): parts.append(lax.ppermute(messages[across], AXES, pairs))  14.6 us
    ppermute x13, starting transfers between devices, local(): in_x = lax.ppermute(out_x, AXES, to_x)  8.65 us
    ppermute x13, starting transfers between devices, local(): in_y = lax.ppermute(out_y, AXES, to_y)  8.64 us
    ppermute x13, starting transfers between devices, local(): in_z = lax.ppermute(out_z, AXES, to_z)  8.6 us
  transfers between devices with their start and end apart: 47, of which 3 were waited for; matrix products, arithmetic and copies ran while one was open for 0% of the time, Pallas kernels for 0%

profile of v5, /device:TPU:63, one launch (start us, length us, event | category | flops | bytes accessed | tf_op | source)
XLA Modules:
  0.0 181.9 jit_solution(2266568097873935471)
XLA Ops:
  0.0 2.0 %pack.1 = (f32[4,160,128]{2,1,0:T(8,128)S(1)}, f32[4,160,128]{2,1,0:T(8,128)S(1)}, f32[2,4,160,128]{3,2,1,0:T(8,128)S(1)}) custom-call(f32[2,8,8,128]{3,2,1,0:T(8,128)} %bitcast.13, f32[2,8,128,128]{3,2,1,0:T(8,128)} %bitcast.12, f32[2,8,8,128]{3,2,1,0:T(8,128)} %bitcast.14, f32[2,8,8,128]{3,2,1,0:T(8,128)} %bitcast.15, f32[128,8]{1,0:T(8,128)} %bitcast.16), custom_call_target="tpu_custom_call" | custom-call | tf_op jit(solution)/shard_map/pack/pallas_call | solution.py:176
  2.0 2.6 %collective-permute-start = (f32[2,4,160,128]{3,2,1,0:T(8,128)S(1)}, f32[2,4,160,128]{3,2,1,0:T(8,128)S(1)}, u32[]{:S(2)}, u32[]{:S(2)}) collective-permute-start(f32[2,4,160,128]{3,2,1,0:T(8,128)S(1)} %get-tuple-element.64), channel_id=1, source_target_pairs={{0,8},{1,9},{2,10},{3,11},{4,12},{5,13},{6,14},{7,15},{8,0},{9,1},... | collective-permute-start | bytes 1966088 | tf_op jit(solution)/shard_map/ppermute | solution.py:211
  4.6 1.7 collective-permute-done
  6.4 0.7 collective-permute-start.1
  7.1 0.7 collective-permute-start.2
  7.9 9.4 %collective-permute-start.3 = (f32[2,4,160,128]{3,2,1,0:T(8,128)S(1)}, f32[2,4,160,128]{3,2,1,0:T(8,128)S(1)}, u32[]{:S(2)}, u32[]{:S(2)}) collective-permute-start(f32[2,4,160,128]{3,2,1,0:T(8,128)S(1)} %pad_maximum_fusion.1), channel_id=1, source_target_pairs={{57,16},{56,17},{59,18},{58,19},{61,20},{60,21},{63,22},{62,23},{9... | collective-permute-start | bytes 1966088 | tf_op jit(solution)/shard_map/ppermute | solution.py:219
  17.2 0.7 collective-permute-start.4
  17.9 0.1 pad_maximum_fusion.refs_0_
  18.0 1.8 collective-permute-start.5
  19.8 0.7 collective-permute-start.6
  20.5 0.0 collective-permute-done.2.refs_2_
  20.5 0.7 collective-permute-start.7
  21.2 9.5 %collective-permute-done.3.refs_3_ = f32[2,4,160,128]{3,2,1,0:T(8,128)S(1)} collective-permute-done((f32[2,4,160,128]{3,2,1,0:T(8,128)S(1)}, f32[2,4,160,128]{3,2,1,0:T(8,128)S(1)}, u32[]{:S(2)}, u32[]{:S(2)}) %collective-permute-start.3) | collective-permute-done | bytes 655392 | tf_op jit(solution)/shard_map/ppermute | solution.py:219
  30.7 0.0 collective-permute-done.4.refs_4_
  30.7 15.4 %collective-permute-done.5.refs_5_ = f32[2,4,160,128]{3,2,1,0:T(8,128)S(1)} collective-permute-done((f32[2,4,160,128]{3,2,1,0:T(8,128)S(1)}, f32[2,4,160,128]{3,2,1,0:T(8,128)S(1)}, u32[]{:S(2)}, u32[]{:S(2)}) %collective-permute-start.5) | collective-permute-done | bytes 655392 | tf_op jit(solution)/shard_map/ppermute | solution.py:219
  46.1 0.0 collective-permute-done.6.refs_6_
  46.1 0.0 collective-permute-done.7.refs_7_
  46.1 0.7 prepare.1
  46.9 0.7 collective-permute-start.8
  47.6 0.7 collective-permute-start.9
  48.3 0.7 collective-permute-start.10
  49.0 0.0 collective-permute-done.10.refs_4_
  49.0 0.0 collective-permute-done.8.refs_2_
  49.0 0.7 collective-permute-start.11
  49.7 0.7 collective-permute-start.12
  50.4 0.7 collective-permute-start.13
  51.1 0.7 collective-permute-start.14
  51.8 0.7 collective-permute-start.15
  52.5 0.7 collective-permute-start.16
  53.2 0.7 collective-permute-start.17
  53.9 0.7 collective-permute-start.18
  54.6 0.7 collective-permute-start.19
  55.3 0.7 collective-permute-start.20
  56.0 0.7 collective-permute-start.21
  56.6 0.7 collective-permute-start.22
  57.3 0.2 tile_step.19
  57.6 0.7 collective-permute-start.23
  58.2 0.7 collective-permute-start.24
  58.9 0.7 collective-permute-start.25
  59.7 0.7 collective-permute-start.26
  60.3 0.7 collective-permute-start.27
  61.0 0.7 collective-permute-start.28
  61.7 0.7 collective-permute-start.29
  62.4 0.7 collective-permute-start.30
  63.1 0.7 collective-permute-start.31
  63.8 0.7 collective-permute-start.32
  64.5 0.7 collective-permute-start.33
  65.2 0.7 collective-permute-start.34
  65.9 0.7 collective-permute-start.35
  66.6 0.7 collective-permute-start.36
  67.3 0.7 collective-permute-start.37
  68.0 0.7 collective-permute-start.38
  68.7 0.7 collective-permute-start.39
  69.4 0.7 collective-permute-start.40
  70.1 0.7 collective-permute-start.41
  70.8 0.7 collective-permute-start.42
  71.4 0.7 collective-permute-start.43
  72.1 0.3 tile_step.26
  72.4 0.7 collective-permute-start.44
  73.1 0.7 collective-permute-start.45
  73.8 0.7 collective-permute-start.46
  74.5 0.7 tile_step.27
  75.2 105.0 %all_to_all.5.parts = f32[16,4,8,128]{3,2,1,0:T(8,128)} all-to-all(f32[16,4,8,128]{3,2,1,0:T(8,128)S(1)} %bitcast.9), channel_id=1, replica_groups={{0,1,8,9,16,17,24,25,32,33,40,41,48,49,56,57},{2,3,10,11,18,19,26,27,34..., dimensions={0} | all-to-all | bytes 524288 | tf_op jit(solution)/shard_map/all_to_all | solution.py:276
  180.1 1.8 unpack.1
  (55 shorter events, 0.6 us)
Async XLA Ops:
  2.0 4.3 %collective-permute-start = (f32[2,4,160,128]{3,2,1,0:T(8,128)S(1)}, f32[2,4,160,128]{3,2,1,0:T(8,128)S(1)}, u32[]{:S(2)}, u32[]{:S(2)}) collective-permute-start(f32[2,4,160,128]{3,2,1,0:T(8,128)S(1)} %get-tuple-element.64), channel_id=1, source_target_pairs={{0,8},{1,9},{2,10},{3,11},{4,12},{5,13},{6,14},{7,15},{8,0},{9,1},... | collective-permute-start | bytes 1966088 | tf_op jit(solution)/shard_map/ppermute | solution.py:211
  6.4 13.3 %collective-permute-start.1 = (f32[2,4,160,128]{3,2,1,0:T(8,128)S(1)}, f32[2,4,160,128]{3,2,1,0:T(8,128)S(1)}, u32[]{:S(2)}, u32[]{:S(2)}) collective-permute-start(f32[2,4,160,128]{3,2,1,0:T(8,128)S(1)} %pad_maximum_fusion.1), channel_id=1, source_target_pairs={{17,16},{16,17},{19,18},{18,19},{21,20},{20,21},{23,22},{22,23},{3... | collective-permute-start | bytes 1966088 | tf_op jit(solution)/shard_map/ppermute | solution.py:219
  7.1 13.4 %collective-permute-start.2 = (f32[2,4,160,128]{3,2,1,0:T(8,128)S(1)}, f32[2,4,160,128]{3,2,1,0:T(8,128)S(1)}, u32[]{:S(2)}, u32[]{:S(2)}) collective-permute-start(f32[2,4,160,128]{3,2,1,0:T(8,128)S(1)} %pad_maximum_fusion.1), channel_id=1, source_target_pairs={{1,16},{0,17},{3,18},{2,19},{5,20},{4,21},{7,22},{6,23},{49,32},{4... | collective-permute-start | bytes 1966088 | tf_op jit(solution)/shard_map/ppermute | solution.py:219
  7.9 22.9 %collective-permute-start.3 = (f32[2,4,160,128]{3,2,1,0:T(8,128)S(1)}, f32[2,4,160,128]{3,2,1,0:T(8,128)S(1)}, u32[]{:S(2)}, u32[]{:S(2)}) collective-permute-start(f32[2,4,160,128]{3,2,1,0:T(8,128)S(1)} %pad_maximum_fusion.1), channel_id=1, source_target_pairs={{57,16},{56,17},{59,18},{58,19},{61,20},{60,21},{63,22},{62,23},{9... | collective-permute-start | bytes 1966088 | tf_op jit(solution)/shard_map/ppermute | solution.py:219
  17.2 13.5 %collective-permute-start.4 = (f32[2,4,160,128]{3,2,1,0:T(8,128)S(1)}, f32[2,4,160,128]{3,2,1,0:T(8,128)S(1)}, u32[]{:S(2)}, u32[]{:S(2)}) collective-permute-start(f32[2,4,160,128]{3,2,1,0:T(8,128)S(1)} %pad_maximum_fusion.1), channel_id=1, source_target_pairs={{41,16},{40,17},{43,18},{42,19},{45,20},{44,21},{47,22},{46,23},{2... | collective-permute-start | bytes 1966088 | tf_op jit(solution)/shard_map/ppermute | solution.py:219
  18.0 28.1 %collective-permute-start.5 = (f32[2,4,160,128]{3,2,1,0:T(8,128)S(1)}, f32[2,4,160,128]{3,2,1,0:T(8,128)S(1)}, u32[]{:S(2)}, u32[]{:S(2)}) collective-permute-start(f32[2,4,160,128]{3,2,1,0:T(8,128)S(1)} %pad_maximum_fusion.refs_0_), channel_id=1, source_target_pairs={{56,16},{57,17},{58,18},{59,19},{60,20},{61,21},{62,22},{63,23},{8... | collective-permute-start | bytes 1966088 | tf_op jit(solution)/shard_map/ppermute | solution.py:219
  19.8 26.3 %collective-permute-start.6 = (f32[2,4,160,128]{3,2,1,0:T(8,128)S(1)}, f32[2,4,160,128]{3,2,1,0:T(8,128)S(1)}, u32[]{:S(2)}, u32[]{:S(2)}) collective-permute-start(f32[2,4,160,128]{3,2,1,0:T(8,128)S(1)} %pad_maximum_fusion.refs_0_), channel_id=1, source_target_pairs={{40,16},{41,17},{42,18},{43,19},{44,20},{45,21},{46,22},{47,23},{2... | collective-permute-start | bytes 1966088 | tf_op jit(solution)/shard_map/ppermute | solution.py:219
  20.5 25.6 %collective-permute-start.7 = (f32[2,4,160,128]{3,2,1,0:T(8,128)S(1)}, f32[2,4,160,128]{3,2,1,0:T(8,128)S(1)}, u32[]{:S(2)}, u32[]{:S(2)}) collective-permute-start(f32[2,4,160,128]{3,2,1,0:T(8,128)S(1)} %pad_maximum_fusion.refs_0_), channel_id=1, source_target_pairs={{0,16},{1,17},{2,18},{3,19},{4,20},{5,21},{6,22},{7,23},{48,32},{4... | collective-permute-start | bytes 1966088 | tf_op jit(solution)/shard_map/ppermute | solution.py:219
  46.9 2.0 %collective-permute-start.8 = (f32[17,8,128]{2,1,0:T(8,128)S(1)}, f32[17,8,128]{2,1,0:T(8,128)S(1)}, u32[]{:S(2)}, u32[]{:S(2)}) collective-permute-start(f32[17,8,128]{2,1,0:T(8,128)S(1)} %get-tuple-element.68), channel_id=1, source_target_pairs={{16,96},{167,215},{213,293},{231,279},{277,357},{291,339},{294,342... | collective-permute-start | bytes 208904 | tf_op jit(solution)/shard_map/ppermute | solution.py:267
  47.6 1.4 collective-permute-start.9
  48.3 0.7 collective-permute-start.10
  49.0 2.0 %collective-permute-start.11 = (f32[17,8,128]{2,1,0:T(8,128)S(1)}, f32[17,8,128]{2,1,0:T(8,128)S(1)}, u32[]{:S(2)}, u32[]{:S(2)}) collective-permute-start(f32[17,8,128]{2,1,0:T(8,128)S(1)} %get-tuple-element.72), channel_id=1, source_target_pairs={{18,98},{32,80},{96,144},{215,295},{279,359},{293,341},{339,419},{... | collective-permute-start | bytes 208904 | tf_op jit(solution)/shard_map/ppermute | solution.py:267
  49.7 1.4 collective-permute-start.12
  50.4 0.7 collective-permute-start.13
  51.1 2.0 %collective-permute-start.14 = (f32[17,8,128]{2,1,0:T(8,128)S(1)}, f32[17,8,128]{2,1,0:T(8,128)S(1)}, u32[]{:S(2)}, u32[]{:S(2)}) collective-permute-start(f32[17,8,128]{2,1,0:T(8,128)S(1)} %get-tuple-element.76), channel_id=1, source_target_pairs={{17,97},{20,100},{34,82},{80,160},{98,146},{144,224},{295,343},{34... | collective-permute-start | bytes 208904 | tf_op jit(solution)/shard_map/ppermute | solution.py:267
  51.8 1.4 collective-permute-start.15
  52.5 0.7 collective-permute-start.16
  53.2 2.0 %collective-permute-start.17 = (f32[17,8,128]{2,1,0:T(8,128)S(1)}, f32[17,8,128]{2,1,0:T(8,128)S(1)}, u32[]{:S(2)}, u32[]{:S(2)}) collective-permute-start(f32[17,8,128]{2,1,0:T(8,128)S(1)} %get-tuple-element.80), channel_id=1, source_target_pairs={{19,99},{22,102},{33,81},{36,84},{82,162},{97,145},{100,148},{146,... | collective-permute-start | bytes 208904 | tf_op jit(solution)/shard_map/ppermute | solution.py:267
  53.9 1.4 collective-permute-start.18
  54.6 0.7 collective-permute-start.19
  55.3 2.0 %collective-permute-start.20 = (f32[17,8,128]{2,1,0:T(8,128)S(1)}, f32[17,8,128]{2,1,0:T(8,128)S(1)}, u32[]{:S(2)}, u32[]{:S(2)}) collective-permute-start(f32[17,8,128]{2,1,0:T(8,128)S(1)} %get-tuple-element.84), channel_id=1, source_target_pairs={{21,101},{35,83},{38,86},{81,161},{84,164},{99,147},{102,150},{145... | collective-permute-start | bytes 208904 | tf_op jit(solution)/shard_map/ppermute | solution.py:267
  56.0 1.4 collective-permute-start.21
  56.6 0.7 collective-permute-start.22
  57.6 2.0 %collective-permute-start.23 = (f32[17,8,128]{2,1,0:T(8,128)S(1)}, f32[17,8,128]{2,1,0:T(8,128)S(1)}, u32[]{:S(2)}, u32[]{:S(2)}) collective-permute-start(f32[17,8,128]{2,1,0:T(8,128)S(1)} %get-tuple-element.88), channel_id=1, source_target_pairs={{23,103},{37,85},{83,163},{86,166},{101,149},{147,227},{150,230},{... | collective-permute-start | bytes 208904 | tf_op jit(solution)/shard_map/ppermute | solution.py:267
  58.2 1.4 collective-permute-start.24
  58.9 0.7 collective-permute-start.25
  59.7 2.0 %collective-permute-start.26 = (f32[17,8,128]{2,1,0:T(8,128)S(1)}, f32[17,8,128]{2,1,0:T(8,128)S(1)}, u32[]{:S(2)}, u32[]{:S(2)}) collective-permute-start(f32[17,8,128]{2,1,0:T(8,128)S(1)} %get-tuple-element.92), channel_id=1, source_target_pairs={{39,87},{85,165},{103,151},{149,229},{163,211},{166,214},{209,289}... | collective-permute-start | bytes 208904 | tf_op jit(solution)/shard_map/ppermute | solution.py:267
  60.3 1.4 collective-permute-start.27
  61.0 0.7 collective-permute-start.28
  61.7 2.0 %collective-permute-start.29 = (f32[17,8,128]{2,1,0:T(8,128)S(1)}, f32[17,8,128]{2,1,0:T(8,128)S(1)}, u32[]{:S(2)}, u32[]{:S(2)}) collective-permute-start(f32[17,8,128]{2,1,0:T(8,128)S(1)} %get-tuple-element.96), channel_id=1, source_target_pairs={{87,167},{151,231},{165,213},{211,291},{214,294},{229,277},{275,35... | collective-permute-start | bytes 208904 | tf_op jit(solution)/shard_map/ppermute | solution.py:267
  62.4 1.4 collective-permute-start.30
  63.1 0.7 collective-permute-start.31
  63.8 2.0 %collective-permute-start.32 = (f32[17,8,128]{2,1,0:T(8,128)S(1)}, f32[17,8,128]{2,1,0:T(8,128)S(1)}, u32[]{:S(2)}, u32[]{:S(2)}) collective-permute-start(f32[17,8,128]{2,1,0:T(8,128)S(1)} %get-tuple-element.100), channel_id=1, source_target_pairs={{16,96},{167,215},{213,293},{231,279},{277,357},{291,339},{294,342... | collective-permute-start | bytes 208904 | tf_op jit(solution)/shard_map/ppermute | solution.py:267
  64.5 1.4 collective-permute-start.33
  65.2 0.7 collective-permute-start.34
  65.9 2.0 %collective-permute-start.35 = (f32[17,8,128]{2,1,0:T(8,128)S(1)}, f32[17,8,128]{2,1,0:T(8,128)S(1)}, u32[]{:S(2)}, u32[]{:S(2)}) collective-permute-start(f32[17,8,128]{2,1,0:T(8,128)S(1)} %get-tuple-element.104), channel_id=1, source_target_pairs={{18,98},{32,80},{96,144},{215,295},{279,359},{293,341},{339,419},{... | collective-permute-start | bytes 208904 | tf_op jit(solution)/shard_map/ppermute | solution.py:267
  66.6 1.4 collective-permute-start.36
  67.3 0.7 collective-permute-start.37
  68.0 2.0 %collective-permute-start.38 = (f32[17,8,128]{2,1,0:T(8,128)S(1)}, f32[17,8,128]{2,1,0:T(8,128)S(1)}, u32[]{:S(2)}, u32[]{:S(2)}) collective-permute-start(f32[17,8,128]{2,1,0:T(8,128)S(1)} %get-tuple-element.108), channel_id=1, source_target_pairs={{17,97},{20,100},{34,82},{80,160},{98,146},{144,224},{295,343},{34... | collective-permute-start | bytes 208904 | tf_op jit(solution)/shard_map/ppermute | solution.py:267
  68.7 1.4 collective-permute-start.39
  69.4 0.7 collective-permute-start.40
  70.1 2.0 %collective-permute-start.41 = (f32[17,8,128]{2,1,0:T(8,128)S(1)}, f32[17,8,128]{2,1,0:T(8,128)S(1)}, u32[]{:S(2)}, u32[]{:S(2)}) collective-permute-start(f32[17,8,128]{2,1,0:T(8,128)S(1)} %get-tuple-element.112), channel_id=1, source_target_pairs={{19,99},{22,102},{33,81},{36,84},{82,162},{97,145},{100,148},{146,... | collective-permute-start | bytes 208904 | tf_op jit(solution)/shard_map/ppermute | solution.py:267
  70.8 1.4 collective-permute-start.42
  71.4 0.7 collective-permute-start.43
  72.4 2.0 %collective-permute-start.44 = (f32[17,8,128]{2,1,0:T(8,128)S(1)}, f32[17,8,128]{2,1,0:T(8,128)S(1)}, u32[]{:S(2)}, u32[]{:S(2)}) collective-permute-start(f32[17,8,128]{2,1,0:T(8,128)S(1)} %get-tuple-element.116), channel_id=1, source_target_pairs={{21,101},{35,83},{38,86},{81,161},{84,164},{99,147},{102,150},{145... | collective-permute-start | bytes 208904 | tf_op jit(solution)/shard_map/ppermute | solution.py:267
  73.1 1.4 collective-permute-start.45
  73.8 0.7 collective-permute-start.46

commit v6 on v5

--- a/solution.py
+++ b/solution.py
@@ -9,7 +9,7 @@
 TILE_X = 8
 TILE_Y = 4
 MEMBERS = 16
-ROUNDS = ((0, 0), (1, 0), (1, 1), (1, 2), (1, 3), (0, 2), (0, 3), (0, 1))
+ROUNDS = ((0, 0), (1, 0), (1, 1), (1, 3), (0, 3), (0, 1), (1, 2), (0, 2))
 SENT_X = 17
 OWNERS = (2, 4)
 REPEAT = 8
@@ -36,8 +36,8 @@
     ]
     for copy in copies:
         copy.start()
-    for copy in copies:
-        copy.wait()
+    for i in (0, 2, 3, 4):
+        copies[i].wait()
     rhs, inverse, cx, cy, cz = held
     gx = lax.axis_index("gx")
     core = lax.rem(gx, 2)
@@ -67,6 +67,7 @@
             for d in range(1, 8):
                 out = jnp.where(group == d, pltpu.roll(t, 8 - d, 0), out)
             small[y, s, 24:32, :] = out
+    copies[1].wait()
     for across in range(2):
         for given in range(2):
             out = outs[2].at[across] if given else outs[across]
@@ -216,7 +217,10 @@
             (device((gx ^ 2 * along) + along // 2, gy ^ across), device(gx, gy))
             for gx, gy in owners
         ]
-        parts.append(lax.ppermute(messages[across], AXES, pairs))
+        message = messages[across]
+        if along == 2:
+            message, _ = lax.optimization_barrier((message, parts[1 + (across == 0)]))
+        parts.append(lax.ppermute(message, AXES, pairs))
     weights, rows = pl.pallas_call(
         prepare_kernel,
         out_shape=[

time: 183 us -> 182 us (level)
  waiting for transfers between devices: 26.7 us -> 9.98 us
  starting transfers between devices: 43.1 us -> 54.9 us
  blocking collectives: 105 us -> 109 us
    ppermute x7, waiting for transfers between devices: 24.9 us -> 8.18 us  [local(): parts.append(lax.ppermute(message, AXES, pairs))]
    ppermute x7, starting transfers between devices: 14.6 us -> 26.4 us  [local(): parts.append(lax.ppermute(message, AXES, pairs))]
    all_to_all x1, blocking collectives: 105 us -> 109 us  [local(): lax.all_to_all(tile.reshape(MEMBERS, 4, 8, 128), AXES, 0, 0, axis_index_g...]
  transfers between devices with their start and end apart: 47 -> 47, of which waited for: 3 -> 2; matrix products, arithmetic and copies ran while one was open for 0% -> 0% of each run, Pallas kernels for 0% -> 0%
where the time goes in v6:
time: 182 us; the launch traced here: 181 us
  blocking collectives  109 us (60%)
  starting transfers between devices  54.9 us (30%)
  waiting for transfers between devices  9.98 us (5%)
  Pallas kernels  6.12 us (3%)
    all_to_all x1, blocking collectives, local(): lax.all_to_all(tile.reshape(MEMBERS, 4, 8, 128), AXES, 0, 0, axis_index_g...  109 us
    ppermute x7, starting transfers between devices, local(): parts.append(lax.ppermute(message, AXES, pairs))  26.4 us
    ppermute x13, starting transfers between devices, local(): in_x = lax.ppermute(out_x, AXES, to_x)  8.65 us
    ppermute x13, starting transfers between devices, local(): in_y = lax.ppermute(out_y, AXES, to_y)  8.64 us
    ppermute x13, starting transfers between devices, local(): in_z = lax.ppermute(out_z, AXES, to_z)  8.6 us
    ppermute x7, waiting for transfers between devices, local(): parts.append(lax.ppermute(message, AXES, pairs))  8.18 us
  transfers between devices with their start and end apart: 47, of which 2 were waited for; matrix products, arithmetic and copies ran while one was open for 0% of the time, Pallas kernels for 0%

profile of v6, /device:TPU:63, one launch (start us, length us, event | category | flops | bytes accessed | tf_op | source)
XLA Modules:
  0.0 181.1 jit_solution(9392556038464040381)
XLA Ops:
  0.0 2.1 %pack.1 = (f32[4,160,128]{2,1,0:T(8,128)S(1)}, f32[4,160,128]{2,1,0:T(8,128)S(1)}, f32[2,4,160,128]{3,2,1,0:T(8,128)S(1)}) custom-call(f32[2,8,8,128]{3,2,1,0:T(8,128)} %bitcast.13, f32[2,8,128,128]{3,2,1,0:T(8,128)} %bitcast.12, f32[2,8,8,128]{3,2,1,0:T(8,128)} %bitcast.14, f32[2,8,8,128]{3,2,1,0:T(8,128)} %bitcast.15, f32[128,8]{1,0:T(8,128)} %bitcast.16), custom_call_target="tpu_custom_call" | custom-call | tf_op jit(solution)/shard_map/pack/pallas_call | solution.py:177
  2.1 2.6 %collective-permute-start = (f32[2,4,160,128]{3,2,1,0:T(8,128)S(1)}, f32[2,4,160,128]{3,2,1,0:T(8,128)S(1)}, u32[]{:S(2)}, u32[]{:S(2)}) collective-permute-start(f32[2,4,160,128]{3,2,1,0:T(8,128)S(1)} %get-tuple-element.66), channel_id=1, source_target_pairs={{0,8},{1,9},{2,10},{3,11},{4,12},{5,13},{6,14},{7,15},{8,0},{9,1},... | collective-permute-start | bytes 1966088 | tf_op jit(solution)/shard_map/ppermute | solution.py:212
  4.7 1.7 collective-permute-done
  6.5 0.7 collective-permute-start.2
  7.2 0.7 collective-permute-start.1
  7.9 0.7 collective-permute-start.3
  8.6 0.1 pad_maximum_fusion.refs_0_
  8.7 0.7 collective-permute-start.4
  9.4 0.7 collective-permute-start.5
  10.1 15.9 %collective-permute-start.7 = (f32[2,4,160,128]{3,2,1,0:T(8,128)S(1)}, f32[2,4,160,128]{3,2,1,0:T(8,128)S(1)}, u32[]{:S(2)}, u32[]{:S(2)}) collective-permute-start(f32[2,4,160,128]{3,2,1,0:T(8,128)S(1)} %pad_maximum_fusion.refs_0_), channel_id=1, source_target_pairs={{56,16},{57,17},{58,18},{59,19},{60,20},{61,21},{62,22},{63,23},{8... | collective-permute-start | bytes 1966088 | tf_op jit(solution)/shard_map/ppermute | solution.py:223
  26.1 7.0 %collective-permute-start.6 = (f32[2,4,160,128]{3,2,1,0:T(8,128)S(1)}, f32[2,4,160,128]{3,2,1,0:T(8,128)S(1)}, u32[]{:S(2)}, u32[]{:S(2)}) collective-permute-start(f32[2,4,160,128]{3,2,1,0:T(8,128)S(1)} %pad_maximum_fusion.1), channel_id=1, source_target_pairs={{57,16},{56,17},{59,18},{58,19},{61,20},{60,21},{63,22},{62,23},{9... | collective-permute-start | bytes 1966088 | tf_op jit(solution)/shard_map/ppermute | solution.py:223
  33.1 0.0 collective-permute-done.3.refs_3_
  33.1 0.0 collective-permute-done.4.refs_4_
  33.1 8.2 %collective-permute-done.7.refs_7_ = f32[2,4,160,128]{3,2,1,0:T(8,128)S(1)} collective-permute-done((f32[2,4,160,128]{3,2,1,0:T(8,128)S(1)}, f32[2,4,160,128]{3,2,1,0:T(8,128)S(1)}, u32[]{:S(2)}, u32[]{:S(2)}) %collective-permute-start.7) | collective-permute-done | bytes 655392 | tf_op jit(solution)/shard_map/ppermute | solution.py:223
  41.3 0.0 collective-permute-done.6.refs_6_
  41.3 0.7 prepare.1
  42.1 0.7 collective-permute-start.8
  42.7 0.7 collective-permute-start.9
  43.4 0.7 collective-permute-start.10
  44.1 0.0 collective-permute-done.10.refs_4_
  44.1 0.0 collective-permute-done.9.refs_3_
  44.2 0.7 collective-permute-start.11
  44.8 0.7 collective-permute-start.12
  45.5 0.7 collective-permute-start.13
  46.2 0.0 collective-permute-done.12.refs_3_
  46.2 0.0 collective-permute-done.11.refs_2_
  46.3 0.7 collective-permute-start.14
  46.9 0.7 collective-permute-start.15
  47.6 0.7 collective-permute-start.16
  48.3 0.7 collective-permute-start.17
  49.0 0.7 collective-permute-start.18
  49.7 0.7 collective-permute-start.19
  50.4 0.7 collective-permute-start.20
  51.1 0.7 collective-permute-start.21
  51.8 0.7 collective-permute-start.22
  52.5 0.2 tile_step.19
  52.7 0.7 collective-permute-start.23
  53.4 0.7 collective-permute-start.24
  54.0 0.7 collective-permute-start.25
  54.8 0.7 collective-permute-start.26
  55.5 0.7 collective-permute-start.27
  56.1 0.7 collective-permute-start.28
  56.9 0.7 collective-permute-start.29
  57.6 0.7 collective-permute-start.30
  58.2 0.7 collective-permute-start.31
  59.0 0.7 collective-permute-start.32
  59.6 0.7 collective-permute-start.33
  60.3 0.7 collective-permute-start.34
  61.1 0.7 collective-permute-start.35
  61.7 0.7 collective-permute-start.36
  62.4 0.7 collective-permute-start.37
  63.2 0.7 collective-permute-start.38
  63.8 0.7 collective-permute-start.39
  64.5 0.7 collective-permute-start.40
  65.2 0.7 collective-permute-start.41
  65.9 0.7 collective-permute-start.42
  66.6 0.7 collective-permute-start.43
  67.3 0.3 tile_step.26
  67.6 0.7 collective-permute-start.44
  68.2 0.7 collective-permute-start.45
  68.9 0.7 collective-permute-start.46
  69.6 0.7 tile_step.27
  70.3 109.0 %all_to_all.5.parts = f32[16,4,8,128]{3,2,1,0:T(8,128)} all-to-all(f32[16,4,8,128]{3,2,1,0:T(8,128)S(1)} %bitcast.9), channel_id=1, replica_groups={{0,1,8,9,16,17,24,25,32,33,40,41,48,49,56,57},{2,3,10,11,18,19,26,27,34..., dimensions={0} | all-to-all | bytes 524288 | tf_op jit(solution)/shard_map/all_to_all | solution.py:280
  179.3 1.8 unpack.1
  (55 shorter events, 0.6 us)
Async XLA Ops:
  2.1 4.3 %collective-permute-start = (f32[2,4,160,128]{3,2,1,0:T(8,128)S(1)}, f32[2,4,160,128]{3,2,1,0:T(8,128)S(1)}, u32[]{:S(2)}, u32[]{:S(2)}) collective-permute-start(f32[2,4,160,128]{3,2,1,0:T(8,128)S(1)} %get-tuple-element.66), channel_id=1, source_target_pairs={{0,8},{1,9},{2,10},{3,11},{4,12},{5,13},{6,14},{7,15},{8,0},{9,1},... | collective-permute-start | bytes 1966088 | tf_op jit(solution)/shard_map/ppermute | solution.py:212
  6.5 3.6 %collective-permute-start.2 = (f32[2,4,160,128]{3,2,1,0:T(8,128)S(1)}, f32[2,4,160,128]{3,2,1,0:T(8,128)S(1)}, u32[]{:S(2)}, u32[]{:S(2)}) collective-permute-start(f32[2,4,160,128]{3,2,1,0:T(8,128)S(1)} %pad_maximum_fusion.1), channel_id=1, source_target_pairs={{1,16},{0,17},{3,18},{2,19},{5,20},{4,21},{7,22},{6,23},{49,32},{4... | collective-permute-start | bytes 1966088 | tf_op jit(solution)/shard_map/ppermute | solution.py:223
  7.2 18.8 %collective-permute-start.1 = (f32[2,4,160,128]{3,2,1,0:T(8,128)S(1)}, f32[2,4,160,128]{3,2,1,0:T(8,128)S(1)}, u32[]{:S(2)}, u32[]{:S(2)}) collective-permute-start(f32[2,4,160,128]{3,2,1,0:T(8,128)S(1)} %pad_maximum_fusion.1), channel_id=1, source_target_pairs={{17,16},{16,17},{19,18},{18,19},{21,20},{20,21},{23,22},{22,23},{3... | collective-permute-start | bytes 1966088 | tf_op jit(solution)/shard_map/ppermute | solution.py:223
  7.9 25.1 %collective-permute-start.3 = (f32[2,4,160,128]{3,2,1,0:T(8,128)S(1)}, f32[2,4,160,128]{3,2,1,0:T(8,128)S(1)}, u32[]{:S(2)}, u32[]{:S(2)}) collective-permute-start(f32[2,4,160,128]{3,2,1,0:T(8,128)S(1)} %pad_maximum_fusion.1), channel_id=1, source_target_pairs={{41,16},{40,17},{43,18},{42,19},{45,20},{44,21},{47,22},{46,23},{2... | collective-permute-start | bytes 1966088 | tf_op jit(solution)/shard_map/ppermute | solution.py:223
  8.7 24.4 %collective-permute-start.4 = (f32[2,4,160,128]{3,2,1,0:T(8,128)S(1)}, f32[2,4,160,128]{3,2,1,0:T(8,128)S(1)}, u32[]{:S(2)}, u32[]{:S(2)}) collective-permute-start(f32[2,4,160,128]{3,2,1,0:T(8,128)S(1)} %pad_maximum_fusion.refs_0_), channel_id=1, source_target_pairs={{40,16},{41,17},{42,18},{43,19},{44,20},{45,21},{46,22},{47,23},{2... | collective-permute-start | bytes 1966088 | tf_op jit(solution)/shard_map/ppermute | solution.py:223
  9.4 23.7 %collective-permute-start.5 = (f32[2,4,160,128]{3,2,1,0:T(8,128)S(1)}, f32[2,4,160,128]{3,2,1,0:T(8,128)S(1)}, u32[]{:S(2)}, u32[]{:S(2)}) collective-permute-start(f32[2,4,160,128]{3,2,1,0:T(8,128)S(1)} %pad_maximum_fusion.refs_0_), channel_id=1, source_target_pairs={{0,16},{1,17},{2,18},{3,19},{4,20},{5,21},{6,22},{7,23},{48,32},{4... | collective-permute-start | bytes 1966088 | tf_op jit(solution)/shard_map/ppermute | solution.py:223
  10.1 31.1 %collective-permute-start.7 = (f32[2,4,160,128]{3,2,1,0:T(8,128)S(1)}, f32[2,4,160,128]{3,2,1,0:T(8,128)S(1)}, u32[]{:S(2)}, u32[]{:S(2)}) collective-permute-start(f32[2,4,160,128]{3,2,1,0:T(8,128)S(1)} %pad_maximum_fusion.refs_0_), channel_id=1, source_target_pairs={{56,16},{57,17},{58,18},{59,19},{60,20},{61,21},{62,22},{63,23},{8... | collective-permute-start | bytes 1966088 | tf_op jit(solution)/shard_map/ppermute | solution.py:223
  26.1 15.2 %collective-permute-start.6 = (f32[2,4,160,128]{3,2,1,0:T(8,128)S(1)}, f32[2,4,160,128]{3,2,1,0:T(8,128)S(1)}, u32[]{:S(2)}, u32[]{:S(2)}) collective-permute-start(f32[2,4,160,128]{3,2,1,0:T(8,128)S(1)} %pad_maximum_fusion.1), channel_id=1, source_target_pairs={{57,16},{56,17},{59,18},{58,19},{61,20},{60,21},{63,22},{62,23},{9... | collective-permute-start | bytes 1966088 | tf_op jit(solution)/shard_map/ppermute | solution.py:223
  42.1 2.0 %collective-permute-start.8 = (f32[17,8,128]{2,1,0:T(8,128)S(1)}, f32[17,8,128]{2,1,0:T(8,128)S(1)}, u32[]{:S(2)}, u32[]{:S(2)}) collective-permute-start(f32[17,8,128]{2,1,0:T(8,128)S(1)} %get-tuple-element.72), channel_id=1, source_target_pairs={{16,96},{167,215},{213,293},{231,279},{277,357},{291,339},{294,342... | collective-permute-start | bytes 208904 | tf_op jit(solution)/shard_map/ppermute | solution.py:271
  42.7 1.4 collective-permute-start.9
  43.4 0.7 collective-permute-start.10
  44.2 2.0 %collective-permute-start.11 = (f32[17,8,128]{2,1,0:T(8,128)S(1)}, f32[17,8,128]{2,1,0:T(8,128)S(1)}, u32[]{:S(2)}, u32[]{:S(2)}) collective-permute-start(f32[17,8,128]{2,1,0:T(8,128)S(1)} %get-tuple-element.76), channel_id=1, source_target_pairs={{18,98},{32,80},{96,144},{215,295},{279,359},{293,341},{339,419},{... | collective-permute-start | bytes 208904 | tf_op jit(solution)/shard_map/ppermute | solution.py:271
  44.8 1.4 collective-permute-start.12
  45.5 0.7 collective-permute-start.13
  46.3 2.0 %collective-permute-start.14 = (f32[17,8,128]{2,1,0:T(8,128)S(1)}, f32[17,8,128]{2,1,0:T(8,128)S(1)}, u32[]{:S(2)}, u32[]{:S(2)}) collective-permute-start(f32[17,8,128]{2,1,0:T(8,128)S(1)} %get-tuple-element.80), channel_id=1, source_target_pairs={{17,97},{20,100},{34,82},{80,160},{98,146},{144,224},{295,343},{34... | collective-permute-start | bytes 208904 | tf_op jit(solution)/shard_map/ppermute | solution.py:271
  46.9 1.4 collective-permute-start.15
  47.6 0.7 collective-permute-start.16
  48.3 2.0 %collective-permute-start.17 = (f32[17,8,128]{2,1,0:T(8,128)S(1)}, f32[17,8,128]{2,1,0:T(8,128)S(1)}, u32[]{:S(2)}, u32[]{:S(2)}) collective-permute-start(f32[17,8,128]{2,1,0:T(8,128)S(1)} %get-tuple-element.84), channel_id=1, source_target_pairs={{19,99},{22,102},{33,81},{36,84},{82,162},{97,145},{100,148},{146,... | collective-permute-start | bytes 208904 | tf_op jit(solution)/shard_map/ppermute | solution.py:271
  49.0 1.4 collective-permute-start.18
  49.7 0.7 collective-permute-start.19
  50.4 2.0 %collective-permute-start.20 = (f32[17,8,128]{2,1,0:T(8,128)S(1)}, f32[17,8,128]{2,1,0:T(8,128)S(1)}, u32[]{:S(2)}, u32[]{:S(2)}) collective-permute-start(f32[17,8,128]{2,1,0:T(8,128)S(1)} %get-tuple-element.88), channel_id=1, source_target_pairs={{21,101},{35,83},{38,86},{81,161},{84,164},{99,147},{102,150},{145... | collective-permute-start | bytes 208904 | tf_op jit(solution)/shard_map/ppermute | solution.py:271
  51.1 1.4 collective-permute-start.21
  51.8 0.7 collective-permute-start.22
  52.7 2.0 %collective-permute-start.23 = (f32[17,8,128]{2,1,0:T(8,128)S(1)}, f32[17,8,128]{2,1,0:T(8,128)S(1)}, u32[]{:S(2)}, u32[]{:S(2)}) collective-permute-start(f32[17,8,128]{2,1,0:T(8,128)S(1)} %get-tuple-element.92), channel_id=1, source_target_pairs={{23,103},{37,85},{83,163},{86,166},{101,149},{147,227},{150,230},{... | collective-permute-start | bytes 208904 | tf_op jit(solution)/shard_map/ppermute | solution.py:271
  53.4 1.4 collective-permute-start.24
  54.0 0.7 collective-permute-start.25
  54.8 2.0 %collective-permute-start.26 = (f32[17,8,128]{2,1,0:T(8,128)S(1)}, f32[17,8,128]{2,1,0:T(8,128)S(1)}, u32[]{:S(2)}, u32[]{:S(2)}) collective-permute-start(f32[17,8,128]{2,1,0:T(8,128)S(1)} %get-tuple-element.96), channel_id=1, source_target_pairs={{39,87},{85,165},{103,151},{149,229},{163,211},{166,214},{209,289}... | collective-permute-start | bytes 208904 | tf_op jit(solution)/shard_map/ppermute | solution.py:271
  55.5 1.4 collective-permute-start.27
  56.1 0.7 collective-permute-start.28
  56.9 2.0 %collective-permute-start.29 = (f32[17,8,128]{2,1,0:T(8,128)S(1)}, f32[17,8,128]{2,1,0:T(8,128)S(1)}, u32[]{:S(2)}, u32[]{:S(2)}) collective-permute-start(f32[17,8,128]{2,1,0:T(8,128)S(1)} %get-tuple-element.100), channel_id=1, source_target_pairs={{87,167},{151,231},{165,213},{211,291},{214,294},{229,277},{275,35... | collective-permute-start | bytes 208904 | tf_op jit(solution)/shard_map/ppermute | solution.py:271
  57.6 1.4 collective-permute-start.30
  58.2 0.7 collective-permute-start.31
  59.0 2.0 %collective-permute-start.32 = (f32[17,8,128]{2,1,0:T(8,128)S(1)}, f32[17,8,128]{2,1,0:T(8,128)S(1)}, u32[]{:S(2)}, u32[]{:S(2)}) collective-permute-start(f32[17,8,128]{2,1,0:T(8,128)S(1)} %get-tuple-element.104), channel_id=1, source_target_pairs={{16,96},{167,215},{213,293},{231,279},{277,357},{291,339},{294,342... | collective-permute-start | bytes 208904 | tf_op jit(solution)/shard_map/ppermute | solution.py:271
  59.6 1.4 collective-permute-start.33
  60.3 0.7 collective-permute-start.34
  61.1 2.0 %collective-permute-start.35 = (f32[17,8,128]{2,1,0:T(8,128)S(1)}, f32[17,8,128]{2,1,0:T(8,128)S(1)}, u32[]{:S(2)}, u32[]{:S(2)}) collective-permute-start(f32[17,8,128]{2,1,0:T(8,128)S(1)} %get-tuple-element.108), channel_id=1, source_target_pairs={{18,98},{32,80},{96,144},{215,295},{279,359},{293,341},{339,419},{... | collective-permute-start | bytes 208904 | tf_op jit(solution)/shard_map/ppermute | solution.py:271
  61.7 1.4 collective-permute-start.36
  62.4 0.7 collective-permute-start.37
  63.2 2.0 %collective-permute-start.38 = (f32[17,8,128]{2,1,0:T(8,128)S(1)}, f32[17,8,128]{2,1,0:T(8,128)S(1)}, u32[]{:S(2)}, u32[]{:S(2)}) collective-permute-start(f32[17,8,128]{2,1,0:T(8,128)S(1)} %get-tuple-element.112), channel_id=1, source_target_pairs={{17,97},{20,100},{34,82},{80,160},{98,146},{144,224},{295,343},{34... | collective-permute-start | bytes 208904 | tf_op jit(solution)/shard_map/ppermute | solution.py:271
  63.8 1.4 collective-permute-start.39
  64.5 0.7 collective-permute-start.40
  65.2 2.0 %collective-permute-start.41 = (f32[17,8,128]{2,1,0:T(8,128)S(1)}, f32[17,8,128]{2,1,0:T(8,128)S(1)}, u32[]{:S(2)}, u32[]{:S(2)}) collective-permute-start(f32[17,8,128]{2,1,0:T(8,128)S(1)} %get-tuple-element.116), channel_id=1, source_target_pairs={{19,99},{22,102},{33,81},{36,84},{82,162},{97,145},{100,148},{146,... | collective-permute-start | bytes 208904 | tf_op jit(solution)/shard_map/ppermute | solution.py:271
  65.9 1.4 collective-permute-start.42
  66.6 0.7 collective-permute-start.43
  67.6 2.0 %collective-permute-start.44 = (f32[17,8,128]{2,1,0:T(8,128)S(1)}, f32[17,8,128]{2,1,0:T(8,128)S(1)}, u32[]{:S(2)}, u32[]{:S(2)}) collective-permute-start(f32[17,8,128]{2,1,0:T(8,128)S(1)} %get-tuple-element.120), channel_id=1, source_target_pairs={{21,101},{35,83},{38,86},{81,161},{84,164},{99,147},{102,150},{145... | collective-permute-start | bytes 208904 | tf_op jit(solution)/shard_map/ppermute | solution.py:271
  68.2 1.4 collective-permute-start.45
  68.9 0.7 collective-permute-start.46

commit v7 on v6

--- a/solution.py
+++ b/solution.py
@@ -286,6 +286,7 @@
         in_specs=[VMEM],
         out_specs=VMEM,
         scratch_shapes=[pltpu.VMEM((2, 8, 8, 128), jnp.float32)],
+        compiler_params=pltpu.CompilerParams(vmem_limit_bytes=4 << 20),
         name="unpack",
     )(parts)
     return result[None]

time: 182 us -> 181 us (level)
  no operation moved by 1% of the time
where the time goes in v7:
time: 181 us; the launch traced here: 180 us
  blocking collectives  109 us (60%)
  starting transfers between devices  54.9 us (30%)
  waiting for transfers between devices  9.98 us (6%)
  Pallas kernels  5.17 us (3%)
    all_to_all x1, blocking collectives, local(): lax.all_to_all(tile.reshape(MEMBERS, 4, 8, 128), AXES, 0, 0, axis_index_g...  109 us
    ppermute x7, starting transfers between devices, local(): parts.append(lax.ppermute(message, AXES, pairs))  26.4 us
    ppermute x13, starting transfers between devices, local(): in_x = lax.ppermute(out_x, AXES, to_x)  8.65 us
    ppermute x13, starting transfers between devices, local(): in_y = lax.ppermute(out_y, AXES, to_y)  8.64 us
    ppermute x13, starting transfers between devices, local(): in_z = lax.ppermute(out_z, AXES, to_z)  8.6 us
    ppermute x7, waiting for transfers between devices, local(): parts.append(lax.ppermute(message, AXES, pairs))  8.18 us
  transfers between devices with their start and end apart: 47, of which 2 were waited for; matrix products, arithmetic and copies ran while one was open for 0% of the time, Pallas kernels for 0%

profile of v7, /device:TPU:63, one launch (start us, length us, event | category | flops | bytes accessed | tf_op | source)
XLA Modules:
  0.0 180.0 jit_solution(10654843361588574055)
XLA Ops:
  0.0 2.1 %pack.1 = (f32[4,160,128]{2,1,0:T(8,128)S(1)}, f32[4,160,128]{2,1,0:T(8,128)S(1)}, f32[2,4,160,128]{3,2,1,0:T(8,128)S(1)}) custom-call(f32[2,8,8,128]{3,2,1,0:T(8,128)} %bitcast.13, f32[2,8,128,128]{3,2,1,0:T(8,128)} %bitcast.12, f32[2,8,8,128]{3,2,1,0:T(8,128)} %bitcast.14, f32[2,8,8,128]{3,2,1,0:T(8,128)} %bitcast.15, f32[128,8]{1,0:T(8,128)} %bitcast.16), custom_call_target="tpu_custom_call" | custom-call | tf_op jit(solution)/shard_map/pack/pallas_call | solution.py:177
  2.1 2.6 %collective-permute-start = (f32[2,4,160,128]{3,2,1,0:T(8,128)S(1)}, f32[2,4,160,128]{3,2,1,0:T(8,128)S(1)}, u32[]{:S(2)}, u32[]{:S(2)}) collective-permute-start(f32[2,4,160,128]{3,2,1,0:T(8,128)S(1)} %get-tuple-element.66), channel_id=1, source_target_pairs={{0,8},{1,9},{2,10},{3,11},{4,12},{5,13},{6,14},{7,15},{8,0},{9,1},... | collective-permute-start | bytes 1966088 | tf_op jit(solution)/shard_map/ppermute | solution.py:212
  4.7 1.7 collective-permute-done
  6.5 0.7 collective-permute-start.2
  7.2 0.7 collective-permute-start.1
  7.9 0.7 collective-permute-start.3
  8.6 0.1 pad_maximum_fusion.refs_0_
  8.7 0.7 collective-permute-start.4
  9.4 0.7 collective-permute-start.5
  10.1 15.9 %collective-permute-start.7 = (f32[2,4,160,128]{3,2,1,0:T(8,128)S(1)}, f32[2,4,160,128]{3,2,1,0:T(8,128)S(1)}, u32[]{:S(2)}, u32[]{:S(2)}) collective-permute-start(f32[2,4,160,128]{3,2,1,0:T(8,128)S(1)} %pad_maximum_fusion.refs_0_), channel_id=1, source_target_pairs={{56,16},{57,17},{58,18},{59,19},{60,20},{61,21},{62,22},{63,23},{8... | collective-permute-start | bytes 1966088 | tf_op jit(solution)/shard_map/ppermute | solution.py:223
  26.1 7.0 %collective-permute-start.6 = (f32[2,4,160,128]{3,2,1,0:T(8,128)S(1)}, f32[2,4,160,128]{3,2,1,0:T(8,128)S(1)}, u32[]{:S(2)}, u32[]{:S(2)}) collective-permute-start(f32[2,4,160,128]{3,2,1,0:T(8,128)S(1)} %pad_maximum_fusion.1), channel_id=1, source_target_pairs={{57,16},{56,17},{59,18},{58,19},{61,20},{60,21},{63,22},{62,23},{9... | collective-permute-start | bytes 1966088 | tf_op jit(solution)/shard_map/ppermute | solution.py:223
  33.1 0.0 collective-permute-done.4.refs_4_
  33.1 8.2 %collective-permute-done.7.refs_7_ = f32[2,4,160,128]{3,2,1,0:T(8,128)S(1)} collective-permute-done((f32[2,4,160,128]{3,2,1,0:T(8,128)S(1)}, f32[2,4,160,128]{3,2,1,0:T(8,128)S(1)}, u32[]{:S(2)}, u32[]{:S(2)}) %collective-permute-start.7) | collective-permute-done | bytes 655392 | tf_op jit(solution)/shard_map/ppermute | solution.py:223
  41.3 0.0 collective-permute-done.6.refs_6_
  41.3 0.7 prepare.1
  42.1 0.7 collective-permute-start.8
  42.7 0.7 collective-permute-start.9
  43.4 0.7 collective-permute-start.10
  44.1 0.0 collective-permute-done.9.refs_3_
  44.2 0.7 collective-permute-start.11
  44.8 0.7 collective-permute-start.12
  45.5 0.7 collective-permute-start.13
  46.2 0.0 collective-permute-done.11.refs_2_
  46.3 0.7 collective-permute-start.14
  46.9 0.7 collective-permute-start.15
  47.6 0.7 collective-permute-start.16
  48.3 0.0 collective-permute-done.16.refs_4_
  48.3 0.7 collective-permute-start.17
  49.0 0.7 collective-permute-start.18
  49.7 0.7 collective-permute-start.19
  50.4 0.0 collective-permute-done.19.refs_4_
  50.4 0.0 collective-permute-done.18.refs_3_
  50.4 0.7 collective-permute-start.20
  51.1 0.7 collective-permute-start.21
  51.8 0.7 collective-permute-start.22
  52.5 0.2 tile_step.19
  52.7 0.7 collective-permute-start.23
  53.4 0.7 collective-permute-start.24
  54.0 0.7 collective-permute-start.25
  54.8 0.7 collective-permute-start.26
  55.5 0.7 collective-permute-start.27
  56.1 0.7 collective-permute-start.28
  56.9 0.7 collective-permute-start.29
  57.6 0.7 collective-permute-start.30
  58.2 0.7 collective-permute-start.31
  59.0 0.7 collective-permute-start.32
  59.6 0.7 collective-permute-start.33
  60.3 0.7 collective-permute-start.34
  61.1 0.7 collective-permute-start.35
  61.7 0.7 collective-permute-start.36
  62.4 0.7 collective-permute-start.37
  63.2 0.7 collective-permute-start.38
  63.8 0.7 collective-permute-start.39
  64.5 0.7 collective-permute-start.40
  65.2 0.7 collective-permute-start.41
  65.9 0.7 collective-permute-start.42
  66.6 0.7 collective-permute-start.43
  67.3 0.3 tile_step.26
  67.6 0.7 collective-permute-start.44
  68.2 0.7 collective-permute-start.45
  68.9 0.7 collective-permute-start.46
  69.6 0.7 tile_step.27
  70.3 108.9 %all_to_all.5.parts = f32[16,4,8,128]{3,2,1,0:T(8,128)S(1)} all-to-all(f32[16,4,8,128]{3,2,1,0:T(8,128)S(1)} %bitcast.9), channel_id=1, replica_groups={{0,1,8,9,16,17,24,25,32,33,40,41,48,49,56,57},{2,3,10,11,18,19,26,27,34..., dimensions={0} | all-to-all | bytes 524288 | tf_op jit(solution)/shard_map/all_to_all | solution.py:280
  179.2 0.8 unpack.1
  (55 shorter events, 0.6 us)
Async XLA Ops:
  2.1 4.3 %collective-permute-start = (f32[2,4,160,128]{3,2,1,0:T(8,128)S(1)}, f32[2,4,160,128]{3,2,1,0:T(8,128)S(1)}, u32[]{:S(2)}, u32[]{:S(2)}) collective-permute-start(f32[2,4,160,128]{3,2,1,0:T(8,128)S(1)} %get-tuple-element.66), channel_id=1, source_target_pairs={{0,8},{1,9},{2,10},{3,11},{4,12},{5,13},{6,14},{7,15},{8,0},{9,1},... | collective-permute-start | bytes 1966088 | tf_op jit(solution)/shard_map/ppermute | solution.py:212
  6.5 3.6 %collective-permute-start.2 = (f32[2,4,160,128]{3,2,1,0:T(8,128)S(1)}, f32[2,4,160,128]{3,2,1,0:T(8,128)S(1)}, u32[]{:S(2)}, u32[]{:S(2)}) collective-permute-start(f32[2,4,160,128]{3,2,1,0:T(8,128)S(1)} %pad_maximum_fusion.1), channel_id=1, source_target_pairs={{1,16},{0,17},{3,18},{2,19},{5,20},{4,21},{7,22},{6,23},{49,32},{4... | collective-permute-start | bytes 1966088 | tf_op jit(solution)/shard_map/ppermute | solution.py:223
  7.2 18.8 %collective-permute-start.1 = (f32[2,4,160,128]{3,2,1,0:T(8,128)S(1)}, f32[2,4,160,128]{3,2,1,0:T(8,128)S(1)}, u32[]{:S(2)}, u32[]{:S(2)}) collective-permute-start(f32[2,4,160,128]{3,2,1,0:T(8,128)S(1)} %pad_maximum_fusion.1), channel_id=1, source_target_pairs={{17,16},{16,17},{19,18},{18,19},{21,20},{20,21},{23,22},{22,23},{3... | collective-permute-start | bytes 1966088 | tf_op jit(solution)/shard_map/ppermute | solution.py:223
  7.9 25.1 %collective-permute-start.3 = (f32[2,4,160,128]{3,2,1,0:T(8,128)S(1)}, f32[2,4,160,128]{3,2,1,0:T(8,128)S(1)}, u32[]{:S(2)}, u32[]{:S(2)}) collective-permute-start(f32[2,4,160,128]{3,2,1,0:T(8,128)S(1)} %pad_maximum_fusion.1), channel_id=1, source_target_pairs={{41,16},{40,17},{43,18},{42,19},{45,20},{44,21},{47,22},{46,23},{2... | collective-permute-start | bytes 1966088 | tf_op jit(solution)/shard_map/ppermute | solution.py:223
  8.7 24.4 %collective-permute-start.4 = (f32[2,4,160,128]{3,2,1,0:T(8,128)S(1)}, f32[2,4,160,128]{3,2,1,0:T(8,128)S(1)}, u32[]{:S(2)}, u32[]{:S(2)}) collective-permute-start(f32[2,4,160,128]{3,2,1,0:T(8,128)S(1)} %pad_maximum_fusion.refs_0_), channel_id=1, source_target_pairs={{40,16},{41,17},{42,18},{43,19},{44,20},{45,21},{46,22},{47,23},{2... | collective-permute-start | bytes 1966088 | tf_op jit(solution)/shard_map/ppermute | solution.py:223
  9.4 23.7 %collective-permute-start.5 = (f32[2,4,160,128]{3,2,1,0:T(8,128)S(1)}, f32[2,4,160,128]{3,2,1,0:T(8,128)S(1)}, u32[]{:S(2)}, u32[]{:S(2)}) collective-permute-start(f32[2,4,160,128]{3,2,1,0:T(8,128)S(1)} %pad_maximum_fusion.refs_0_), channel_id=1, source_target_pairs={{0,16},{1,17},{2,18},{3,19},{4,20},{5,21},{6,22},{7,23},{48,32},{4... | collective-permute-start | bytes 1966088 | tf_op jit(solution)/shard_map/ppermute | solution.py:223
  10.1 31.1 %collective-permute-start.7 = (f32[2,4,160,128]{3,2,1,0:T(8,128)S(1)}, f32[2,4,160,128]{3,2,1,0:T(8,128)S(1)}, u32[]{:S(2)}, u32[]{:S(2)}) collective-permute-start(f32[2,4,160,128]{3,2,1,0:T(8,128)S(1)} %pad_maximum_fusion.refs_0_), channel_id=1, source_target_pairs={{56,16},{57,17},{58,18},{59,19},{60,20},{61,21},{62,22},{63,23},{8... | collective-permute-start | bytes 1966088 | tf_op jit(solution)/shard_map/ppermute | solution.py:223
  26.1 15.2 %collective-permute-start.6 = (f32[2,4,160,128]{3,2,1,0:T(8,128)S(1)}, f32[2,4,160,128]{3,2,1,0:T(8,128)S(1)}, u32[]{:S(2)}, u32[]{:S(2)}) collective-permute-start(f32[2,4,160,128]{3,2,1,0:T(8,128)S(1)} %pad_maximum_fusion.1), channel_id=1, source_target_pairs={{57,16},{56,17},{59,18},{58,19},{61,20},{60,21},{63,22},{62,23},{9... | collective-permute-start | bytes 1966088 | tf_op jit(solution)/shard_map/ppermute | solution.py:223
  42.1 2.0 %collective-permute-start.8 = (f32[17,8,128]{2,1,0:T(8,128)S(1)}, f32[17,8,128]{2,1,0:T(8,128)S(1)}, u32[]{:S(2)}, u32[]{:S(2)}) collective-permute-start(f32[17,8,128]{2,1,0:T(8,128)S(1)} %get-tuple-element.72), channel_id=1, source_target_pairs={{16,96},{167,215},{213,293},{231,279},{277,357},{291,339},{294,342... | collective-permute-start | bytes 208904 | tf_op jit(solution)/shard_map/ppermute | solution.py:271
  42.7 1.4 collective-permute-start.9
  43.4 0.7 collective-permute-start.10
  44.2 2.0 %collective-permute-start.11 = (f32[17,8,128]{2,1,0:T(8,128)S(1)}, f32[17,8,128]{2,1,0:T(8,128)S(1)}, u32[]{:S(2)}, u32[]{:S(2)}) collective-permute-start(f32[17,8,128]{2,1,0:T(8,128)S(1)} %get-tuple-element.76), channel_id=1, source_target_pairs={{18,98},{32,80},{96,144},{215,295},{279,359},{293,341},{339,419},{... | collective-permute-start | bytes 208904 | tf_op jit(solution)/shard_map/ppermute | solution.py:271
  44.8 1.4 collective-permute-start.12
  45.5 0.7 collective-permute-start.13
  46.3 2.0 %collective-permute-start.14 = (f32[17,8,128]{2,1,0:T(8,128)S(1)}, f32[17,8,128]{2,1,0:T(8,128)S(1)}, u32[]{:S(2)}, u32[]{:S(2)}) collective-permute-start(f32[17,8,128]{2,1,0:T(8,128)S(1)} %get-tuple-element.80), channel_id=1, source_target_pairs={{17,97},{20,100},{34,82},{80,160},{98,146},{144,224},{295,343},{34... | collective-permute-start | bytes 208904 | tf_op jit(solution)/shard_map/ppermute | solution.py:271
  46.9 1.4 collective-permute-start.15
  47.6 0.7 collective-permute-start.16
  48.3 2.0 %collective-permute-start.17 = (f32[17,8,128]{2,1,0:T(8,128)S(1)}, f32[17,8,128]{2,1,0:T(8,128)S(1)}, u32[]{:S(2)}, u32[]{:S(2)}) collective-permute-start(f32[17,8,128]{2,1,0:T(8,128)S(1)} %get-tuple-element.84), channel_id=1, source_target_pairs={{19,99},{22,102},{33,81},{36,84},{82,162},{97,145},{100,148},{146,... | collective-permute-start | bytes 208904 | tf_op jit(solution)/shard_map/ppermute | solution.py:271
  49.0 1.4 collective-permute-start.18
  49.7 0.7 collective-permute-start.19
  50.4 2.0 %collective-permute-start.20 = (f32[17,8,128]{2,1,0:T(8,128)S(1)}, f32[17,8,128]{2,1,0:T(8,128)S(1)}, u32[]{:S(2)}, u32[]{:S(2)}) collective-permute-start(f32[17,8,128]{2,1,0:T(8,128)S(1)} %get-tuple-element.88), channel_id=1, source_target_pairs={{21,101},{35,83},{38,86},{81,161},{84,164},{99,147},{102,150},{145... | collective-permute-start | bytes 208904 | tf_op jit(solution)/shard_map/ppermute | solution.py:271
  51.1 1.4 collective-permute-start.21
  51.8 0.7 collective-permute-start.22
  52.7 2.0 %collective-permute-start.23 = (f32[17,8,128]{2,1,0:T(8,128)S(1)}, f32[17,8,128]{2,1,0:T(8,128)S(1)}, u32[]{:S(2)}, u32[]{:S(2)}) collective-permute-start(f32[17,8,128]{2,1,0:T(8,128)S(1)} %get-tuple-element.92), channel_id=1, source_target_pairs={{23,103},{37,85},{83,163},{86,166},{101,149},{147,227},{150,230},{... | collective-permute-start | bytes 208904 | tf_op jit(solution)/shard_map/ppermute | solution.py:271
  53.4 1.4 collective-permute-start.24
  54.0 0.7 collective-permute-start.25
  54.8 2.0 %collective-permute-start.26 = (f32[17,8,128]{2,1,0:T(8,128)S(1)}, f32[17,8,128]{2,1,0:T(8,128)S(1)}, u32[]{:S(2)}, u32[]{:S(2)}) collective-permute-start(f32[17,8,128]{2,1,0:T(8,128)S(1)} %get-tuple-element.96), channel_id=1, source_target_pairs={{39,87},{85,165},{103,151},{149,229},{163,211},{166,214},{209,289}... | collective-permute-start | bytes 208904 | tf_op jit(solution)/shard_map/ppermute | solution.py:271
  55.5 1.4 collective-permute-start.27
  56.1 0.7 collective-permute-start.28
  56.9 2.0 %collective-permute-start.29 = (f32[17,8,128]{2,1,0:T(8,128)S(1)}, f32[17,8,128]{2,1,0:T(8,128)S(1)}, u32[]{:S(2)}, u32[]{:S(2)}) collective-permute-start(f32[17,8,128]{2,1,0:T(8,128)S(1)} %get-tuple-element.100), channel_id=1, source_target_pairs={{87,167},{151,231},{165,213},{211,291},{214,294},{229,277},{275,35... | collective-permute-start | bytes 208904 | tf_op jit(solution)/shard_map/ppermute | solution.py:271
  57.6 1.4 collective-permute-start.30
  58.2 0.7 collective-permute-start.31
  59.0 2.0 %collective-permute-start.32 = (f32[17,8,128]{2,1,0:T(8,128)S(1)}, f32[17,8,128]{2,1,0:T(8,128)S(1)}, u32[]{:S(2)}, u32[]{:S(2)}) collective-permute-start(f32[17,8,128]{2,1,0:T(8,128)S(1)} %get-tuple-element.104), channel_id=1, source_target_pairs={{16,96},{167,215},{213,293},{231,279},{277,357},{291,339},{294,342... | collective-permute-start | bytes 208904 | tf_op jit(solution)/shard_map/ppermute | solution.py:271
  59.6 1.4 collective-permute-start.33
  60.3 0.7 collective-permute-start.34
  61.1 2.0 %collective-permute-start.35 = (f32[17,8,128]{2,1,0:T(8,128)S(1)}, f32[17,8,128]{2,1,0:T(8,128)S(1)}, u32[]{:S(2)}, u32[]{:S(2)}) collective-permute-start(f32[17,8,128]{2,1,0:T(8,128)S(1)} %get-tuple-element.108), channel_id=1, source_target_pairs={{18,98},{32,80},{96,144},{215,295},{279,359},{293,341},{339,419},{... | collective-permute-start | bytes 208904 | tf_op jit(solution)/shard_map/ppermute | solution.py:271
  61.7 1.4 collective-permute-start.36
  62.4 0.7 collective-permute-start.37
  63.2 2.0 %collective-permute-start.38 = (f32[17,8,128]{2,1,0:T(8,128)S(1)}, f32[17,8,128]{2,1,0:T(8,128)S(1)}, u32[]{:S(2)}, u32[]{:S(2)}) collective-permute-start(f32[17,8,128]{2,1,0:T(8,128)S(1)} %get-tuple-element.112), channel_id=1, source_target_pairs={{17,97},{20,100},{34,82},{80,160},{98,146},{144,224},{295,343},{34... | collective-permute-start | bytes 208904 | tf_op jit(solution)/shard_map/ppermute | solution.py:271
  63.8 1.4 collective-permute-start.39
  64.5 0.7 collective-permute-start.40
  65.2 2.0 %collective-permute-start.41 = (f32[17,8,128]{2,1,0:T(8,128)S(1)}, f32[17,8,128]{2,1,0:T(8,128)S(1)}, u32[]{:S(2)}, u32[]{:S(2)}) collective-permute-start(f32[17,8,128]{2,1,0:T(8,128)S(1)} %get-tuple-element.116), channel_id=1, source_target_pairs={{19,99},{22,102},{33,81},{36,84},{82,162},{97,145},{100,148},{146,... | collective-permute-start | bytes 208904 | tf_op jit(solution)/shard_map/ppermute | solution.py:271
  65.9 1.4 collective-permute-start.42
  66.6 0.7 collective-permute-start.43
  67.6 2.0 %collective-permute-start.44 = (f32[17,8,128]{2,1,0:T(8,128)S(1)}, f32[17,8,128]{2,1,0:T(8,128)S(1)}, u32[]{:S(2)}, u32[]{:S(2)}) collective-permute-start(f32[17,8,128]{2,1,0:T(8,128)S(1)} %get-tuple-element.120), channel_id=1, source_target_pairs={{21,101},{35,83},{38,86},{81,161},{84,164},{99,147},{102,150},{145... | collective-permute-start | bytes 208904 | tf_op jit(solution)/shard_map/ppermute | solution.py:271
  68.2 1.4 collective-permute-start.45
  68.9 0.7 collective-permute-start.46
